TPU v7x, 1024 devices: a whole 4x4x32 slice. The times are simulated.
1024 devices in a mesh: sec: 128 (over y, z_hi, x, core), row: 8 (over z_lo).
Axes of the slice: x: 4, y: 4, z: 32 (z_hi: 4, z_lo: 8; z = z_hi * 8 + z_lo), core: 2. Of those that a mesh axis runs over, the one named last changes fastest.
Arguments:
- first_pts: float32 [4, 256, 16, 32, 2, 128], P(None, 'sec', 'row'), may hold values from -1 to 1
- second_pts: float32 [4, 256, 16, 32, 2, 128], P(None, 'sec', 'row'), may hold values from -1 to 1
- counts: int32 [4, 256, 16, 32], P(None, 'sec', 'row'), may hold values from 32 to 128, as said below
Outputs:
- affines: float32 [6, 256, 16, 32], P(None, 'sec', 'row')
- residual: float32 [4, 256, 16, 32, 2, 128], P(None, 'sec', 'row')
Inputs may be any that keep to these rules, and one draw needn't show every extreme that they name: `counts`: points 0 to the count minus one of a pair are live, the rest are padding.
All inputs are finite; a program needn't handle non-finite values.
Results may differ from a plain program's by a relative error of at most 0.035.
Values sent between devices are 32-bit elements; how exact they have to be, the bound alone decides.
No kernel may reach another device: no remote copies, remote signals or barrier semaphores. Data moves between devices by JAX's collectives and lax.ppermute only.
A program may use at most 64 MiB of HBM per device.

v0:
```python
import jax
import jax.numpy as jnp
from jax import lax
from jax.sharding import PartitionSpec as P

ITERS = 4


reg_root = (0.7, 0.7, 0.3, 0.7, 0.7, 0.3)


def passed_along(value, axis, steps):
    count = lax.axis_size(axis)
    leading, last = (max(0, -steps), min(count, count - steps))
    return lax.ppermute(value, axis, [(source, source + steps) for source in range(leading, last)])


def transform(affine, points):
    coord_x = points[..., 0, :]
    coord_y = points[..., 1, :]
    factor = [affine[number][..., None] for number in range(6)]
    return jnp.stack(
        [
            factor[0] * coord_x + factor[1] * coord_y + factor[2],
            factor[3] * coord_x + factor[4] * coord_y + factor[5],
        ],
        axis=-2,
    )


def moments(errors, points):
    err_x = errors[..., 0, :]
    err_y = errors[..., 1, :]
    pos_x = points[..., 0, :]
    pos_y = points[..., 1, :]
    return jnp.stack(
        [
            jnp.sum(err_x * pos_x, -1),
            jnp.sum(err_x * pos_y, -1),
            jnp.sum(err_x, -1),
            jnp.sum(err_y * pos_x, -1),
            jnp.sum(err_y * pos_y, -1),
            jnp.sum(err_y, -1),
        ],
        0,
    )


def piece_of(values, start, limit, axis_no):
    return lax.slice_in_dim(values, start, limit, axis=axis_no)


def pull_pairs(pieces, leading):
    row_dim = leading + 1
    col_dim = leading + 2
    n_sec = pieces[0].shape[leading]
    n_row = pieces[0].shape[row_dim]
    n_col = pieces[0].shape[col_dim]
    along_cols = jnp.concatenate(
        [
            piece_of(pieces[0], 1, n_col, col_dim),
            jnp.zeros_like(piece_of(pieces[0], 0, 1, col_dim)),
        ],
        axis=col_dim,
    )
    top_rows = passed_along(piece_of(pieces[1], 0, 1, row_dim), "row", -1)
    along_rows = jnp.concatenate([piece_of(pieces[1], 1, n_row, row_dim), top_rows], axis=row_dim)
    lowest = jnp.concatenate(
        [piece_of(pieces[2], 0, 1, leading), piece_of(pieces[3], 0, 2, leading)], axis=leading
    )
    above = passed_along(lowest, "sec", -1)
    next_one = jnp.concatenate(
        [piece_of(pieces[2], 1, n_sec, leading), piece_of(above, 0, 1, leading)], axis=leading
    )
    next_two = jnp.concatenate(
        [piece_of(pieces[3], 2, n_sec, leading), piece_of(above, 1, 3, leading)], axis=leading
    )
    return [along_cols, along_rows, next_one, next_two]


def push_pairs(pieces, leading):
    row_dim = leading + 1
    col_dim = leading + 2
    n_sec = pieces[0].shape[leading]
    n_row = pieces[0].shape[row_dim]
    n_col = pieces[0].shape[col_dim]
    along_cols = jnp.concatenate(
        [
            jnp.zeros_like(piece_of(pieces[0], 0, 1, col_dim)),
            piece_of(pieces[0], 0, n_col - 1, col_dim),
        ],
        axis=col_dim,
    )
    low_rows = passed_along(piece_of(pieces[1], n_row - 1, n_row, row_dim), "row", 1)
    along_rows = jnp.concatenate(
        [low_rows, piece_of(pieces[1], 0, n_row - 1, row_dim)], axis=row_dim
    )
    highest = jnp.concatenate(
        [
            piece_of(pieces[2], n_sec - 1, n_sec, leading),
            piece_of(pieces[3], n_sec - 2, n_sec, leading),
        ],
        axis=leading,
    )
    below = passed_along(highest, "sec", 1)
    prev_one = jnp.concatenate(
        [piece_of(below, 0, 1, leading), piece_of(pieces[2], 0, n_sec - 1, leading)], axis=leading
    )
    prev_two = jnp.concatenate(
        [piece_of(below, 1, 3, leading), piece_of(pieces[3], 0, n_sec - 2, leading)], axis=leading
    )
    return [along_cols, along_rows, prev_one, prev_two]


def local_inner(list_a, reg_a, list_b, reg_b):
    summed = jnp.sum(reg_a * reg_b)
    for kind_no in range(4):
        summed = summed + jnp.sum(list_a[kind_no] * list_b[kind_no])
    return summed


def totals(search, image, image_reg, along, along_reg):
    gamma_part = jnp.sum(search * search)
    omega_part = local_inner(image, image_reg, image, image_reg)
    cross_part = local_inner(image, image_reg, along, along_reg)
    return lax.psum((gamma_part, omega_part, cross_part), ("sec", "row"))


def per_device(first_pts, second_pts, counts):
    n_sec = counts.shape[1]
    n_row = counts.shape[2]
    n_col = counts.shape[3]
    width = first_pts.shape[-1]
    total_sec = n_sec * lax.axis_size("sec")
    total_row = n_row * lax.axis_size("row")
    sec_ids = lax.axis_index("sec") * n_sec + jnp.arange(n_sec, dtype=jnp.int32)
    row_ids = lax.axis_index("row") * n_row + jnp.arange(n_row, dtype=jnp.int32)
    col_ids = jnp.arange(n_col, dtype=jnp.int32)
    valid = [
        (col_ids < n_col - 1)[None, None, :],
        (row_ids < total_row - 1)[None, :, None],
        (sec_ids < total_sec - 1)[:, None, None],
        (sec_ids < total_sec - 2)[:, None, None],
    ]
    live = jnp.arange(width)[None, None, None, None, :] < counts[..., None]
    masks = [
        jnp.where(live[kind_no] & valid[kind_no][..., None], 1.0, 0.0).astype(jnp.float32)[
            ..., None, :
        ]
        for kind_no in range(4)
    ]
    root = jnp.array(reg_root, jnp.float32)[:, None, None, None]

    def forward(affine):
        images = pull_pairs([transform(affine, second_pts[kind_no]) for kind_no in range(4)], 0)
        return [
            masks[kind_no] * (transform(affine, first_pts[kind_no]) - images[kind_no])
            for kind_no in range(4)
        ]

    def backward(errors, reg_part):
        moved = push_pairs(errors, 0)
        summed = root * reg_part
        for kind_no in range(4):
            summed = (
                summed
                + moments(errors[kind_no], first_pts[kind_no])
                - moments(moved[kind_no], second_pts[kind_no])
            )
        return summed

    ones = jnp.ones((1, n_sec, n_row, n_col), jnp.float32)
    identity = jnp.array([1.0, 0.0, 0.0, 0.0, 1.0, 0.0], jnp.float32)[:, None, None, None] * ones
    resid = forward(-identity)
    resid_reg = jnp.zeros((6, n_sec, n_row, n_col), jnp.float32)
    search = backward(resid, resid_reg)
    image = forward(search)
    image_reg = root * search
    gamma, curv, unused = totals(search, image, image_reg, image, image_reg)
    direction = search
    along = image
    along_reg = image_reg
    solution = jnp.zeros((6, n_sec, n_row, n_col), jnp.float32)
    for sweep in range(ITERS):
        alpha = gamma / curv
        solution = solution + alpha * direction
        resid = [resid[kind_no] - alpha * along[kind_no] for kind_no in range(4)]
        resid_reg = resid_reg - alpha * along_reg
        if sweep < ITERS - 1:
            search = backward(resid, resid_reg)
            image = forward(search)
            image_reg = root * search
            gamma_new, omega, cross = totals(search, image, image_reg, along, along_reg)
            beta = gamma_new / gamma
            direction = search + beta * direction
            along = [image[kind_no] + beta * along[kind_no] for kind_no in range(4)]
            along_reg = image_reg + beta * along_reg
            curv = omega + 2.0 * beta * cross + beta * beta * curv
            gamma = gamma_new
    return (solution, jnp.stack(resid, 0))


def solution(mesh):
    in_specs = (
        P(None, "sec", "row", None, None, None),
        P(None, "sec", "row", None, None, None),
        P(None, "sec", "row", None),
    )
    out_specs = (P(None, "sec", "row", None), P(None, "sec", "row", None, None, None))
    return jax.shard_map(
        per_device, mesh=mesh, in_specs=in_specs, out_specs=out_specs, check_vma=False
    )
```

profile of v0, /device:TPU:24, one launch (start us, length us, event | category | flops | bytes accessed | tf_op | source)
XLA Modules:
  0.0 944.5 jit_solution(2503872569603368528)
XLA Ops:
  3.9 24.9 %collective-permute-start.2 = (f32[3,2,32,2,128]{4,2,0,1,3:T(8,128)S(1)}, f32[3,2,32,2,128]{4,2,0,1,3:T(8,128)S(1)}, u32[]{:S(2)}, u32[]{:S(2)}) collective-permute-start(f32[3,2,32,2,128]{4,2,0,1,3:T(8,128)S(1)} %fusion.4), channel_id=1, source_target_pairs={{8,0},{16,8},{24,16},{32,24},{40,32},{48,40},{56,48},{64,56},{72,6... | collective-permute-start | bytes 589832 | tf_op jit(solution)/shard_map/ppermute | solution.py:15
  31.6 4.3 collective-permute-start.1
  38.0 9.0 collective-permute-done.2
  47.6 1.9 collective-permute-start.3
  50.2 19.4 %collective-permute-done.3 = f32[3,2,32,2,128]{4,2,1,0,3:T(8,128)S(1)} collective-permute-done((f32[3,2,32,2,128]{4,2,1,0,3:T(8,128)S(1)}, f32[3,2,32,2,128]{4,2,1,0,3:T(8,128)S(1)}, u32[]{:S(2)}, u32[]{:S(2)}) %collective-permute-start.3) | collective-permute-done | bytes 196640 | tf_op jit(solution)/shard_map/ppermute | solution.py:15
  76.3 1.9 collective-permute-start.5
  80.3 8.0 collective-permute-done.4
  89.6 6.9 collective-permute-done.5
  100.8 155.8 %all-reduce.12 = (f32[]{:T(128)}, f32[]{:T(128)}) all-reduce(f32[]{:T(128)} %get-tuple-element.332, f32[]{:T(128)S(6)} %add.1320), channel_id=1, replica_groups=mesh['sec'=128,'row'=8] {'sec','row'}, use_global_device_ids=true, to_apply=%region_49.50 | all-reduce | flops 2 | bytes 16 | tf_op jit(solution)/shard_map/psum | solution.py:126
  260.6 2.8 collective-permute-start.6
  263.4 1.9 collective-permute-start.7
  267.1 23.7 %collective-permute-done.7 = f32[3,2,32,2,128]{4,2,1,0,3:T(8,128)S(1)} collective-permute-done((f32[3,2,32,2,128]{4,2,1,0,3:T(8,128)S(1)}, f32[3,2,32,2,128]{4,2,1,0,3:T(8,128)S(1)}, u32[]{:S(2)}, u32[]{:S(2)}) %collective-permute-start.7) | collective-permute-done | bytes 196640 | tf_op jit(solution)/shard_map/ppermute | solution.py:15
  302.6 12.0 %collective-permute-done.8 = f32[2,1,32,2,128]{4,2,3,0,1:T(8,128)S(1)} collective-permute-done((f32[2,1,32,2,128]{4,2,3,0,1:T(8,128)S(1)}, f32[2,1,32,2,128]{4,2,3,0,1:T(8,128)S(1)}, u32[]{:S(2)}, u32[]{:S(2)}) %collective-permute-start.8) | collective-permute-done | bytes 65568 | tf_op jit(solution)/shard_map/ppermute | solution.py:15
  323.6 154.4 %all-reduce.11 = (f32[]{:T(128)}, f32[]{:T(128)}, f32[]{:T(128)}) all-reduce(f32[]{:T(128)} %get-tuple-element.330, f32[]{:T(128)S(6)} %add.1364, f32[]{:T(128)S(6)} %add.1368), channel_id=1, replica_groups=mesh['sec'=128,'row'=8] {'sec','row'}, use_global_device_ids=true, to_apply=%region_105.106 | all-reduce | flops 3 | bytes 24 | tf_op jit(solution)/shard_map/psum | solution.py:126
  483.7 4.0 collective-permute-start.10
  487.8 1.9 collective-permute-start.11
  490.3 23.8 %collective-permute-done.11 = f32[3,2,32,2,128]{4,2,3,1,0:T(8,128)S(1)} collective-permute-done((f32[3,2,32,2,128]{4,2,3,1,0:T(8,128)S(1)}, f32[3,2,32,2,128]{4,2,3,1,0:T(8,128)S(1)}, u32[]{:S(2)}, u32[]{:S(2)}) %collective-permute-start.11) | collective-permute-done | bytes 196640 | tf_op jit(solution)/shard_map/ppermute | solution.py:15
  542.0 169.1 %all-reduce.10 = (f32[]{:T(128)}, f32[]{:T(128)}, f32[]{:T(128)}) all-reduce(f32[]{:T(128)} %get-tuple-element.329, f32[]{:T(128)S(6)} %add.1421, f32[]{:T(128)S(6)} %add.1425), channel_id=1, replica_groups=mesh['sec'=128,'row'=8] {'sec','row'}, use_global_device_ids=true, to_apply=%region_167.168 | all-reduce | flops 3 | bytes 24 | tf_op jit(solution)/shard_map/psum | solution.py:126
  717.3 3.9 collective-permute-start.14
  721.3 2.1 collective-permute-start.15
  724.6 19.0 %collective-permute-done.15 = f32[3,2,32,2,128]{4,2,1,0,3:T(8,128)S(1)} collective-permute-done((f32[3,2,32,2,128]{4,2,1,0,3:T(8,128)S(1)}, f32[3,2,32,2,128]{4,2,1,0,3:T(8,128)S(1)}, u32[]{:S(2)}, u32[]{:S(2)}) %collective-permute-start.15) | collective-permute-done | bytes 196640 | tf_op jit(solution)/shard_map/ppermute | solution.py:15
  750.6 1.9 collective-permute-start.17
  756.0 2.7 collective-permute-done.16
  764.7 172.3 %all-reduce.9 = (f32[]{:T(128)}, f32[]{:T(128)}, f32[]{:T(128)}) all-reduce(f32[]{:T(128)} %get-tuple-element.328, f32[]{:T(128)S(6)} %add.1478, f32[]{:T(128)S(6)} %add.1482), channel_id=1, replica_groups=mesh['sec'=128,'row'=8] {'sec','row'}, use_global_device_ids=true, to_apply=%region_229.230 | all-reduce | flops 3 | bytes 24 | tf_op jit(solution)/shard_map/psum | solution.py:126
  (517 shorter events, 80.0 us)
Async XLA Ops:
  2.5 28.8 %collective-permute-start = (f32[2,1,32,2,128]{4,2,1,0,3:T(8,128)S(1)}, f32[2,1,32,2,128]{4,2,1,0,3:T(8,128)S(1)}, u32[]{:S(2)}, u32[]{:S(2)}) collective-permute-start(f32[2,1,32,2,128]{4,2,1,0,3:T(8,128)S(1)} %get-tuple-element.401), channel_id=1, source_target_pairs={{1,0},{2,1},{3,2},{4,3},{5,4},{6,5},{7,6},{9,8},{10,9},{11,10},{12... | collective-permute-start | bytes 196616 | tf_op jit(solution)/shard_map/ppermute | solution.py:15
  3.8 25.9 %copy-start.18 = (f32[4,2,2,32,2,128]{5,4,3,2,1,0:T(2,128)S(1)}, f32[4,2,2,32,2,128]{5,4,3,2,1,0:T(2,128)}, u32[]{:S(2)}) copy-start(f32[4,2,2,32,2,128]{5,4,3,2,1,0:T(2,128)} %param.5) | copy-start | bytes 1572868
  3.9 43.1 %collective-permute-start.2 = (f32[3,2,32,2,128]{4,2,0,1,3:T(8,128)S(1)}, f32[3,2,32,2,128]{4,2,0,1,3:T(8,128)S(1)}, u32[]{:S(2)}, u32[]{:S(2)}) collective-permute-start(f32[3,2,32,2,128]{4,2,0,1,3:T(8,128)S(1)} %fusion.4), channel_id=1, source_target_pairs={{8,0},{16,8},{24,16},{32,24},{40,32},{48,40},{56,48},{64,56},{72,6... | collective-permute-start | bytes 589832 | tf_op jit(solution)/shard_map/ppermute | solution.py:15
  31.3 226.6 %copy-start.15 = (f32[2,1,32,2,128]{4,2,1,0,3:T(8,128)}, f32[2,1,32,2,128]{4,2,1,0,3:T(8,128)S(1)}, u32[]{:S(2)}) copy-start(f32[2,1,32,2,128]{4,2,1,0,3:T(8,128)S(1)} %collective-permute-done) | copy-start | bytes 196612
  31.6 6.2 collective-permute-start.1
  47.6 22.1 %collective-permute-start.3 = (f32[3,2,32,2,128]{4,2,1,0,3:T(8,128)S(1)}, f32[3,2,32,2,128]{4,2,1,0,3:T(8,128)S(1)}, u32[]{:S(2)}, u32[]{:S(2)}) collective-permute-start(f32[3,2,32,2,128]{4,2,1,0,3:T(8,128)S(1)} %pad_maximum_fusion.1), channel_id=1, source_target_pairs={{0,8},{8,16},{16,24},{24,32},{32,40},{40,48},{48,56},{56,64},{64,7... | collective-permute-start | bytes 589832 | tf_op jit(solution)/shard_map/ppermute | solution.py:15
  74.3 13.9 %collective-permute-start.4 = (f32[2,1,32,2,128]{4,2,1,0,3:T(8,128)S(1)}, f32[2,1,32,2,128]{4,2,1,0,3:T(8,128)S(1)}, u32[]{:S(2)}, u32[]{:S(2)}) collective-permute-start(f32[2,1,32,2,128]{4,2,1,0,3:T(8,128)S(1)} %get-tuple-element.398), channel_id=1, source_target_pairs={{1,0},{2,1},{3,2},{4,3},{5,4},{6,5},{7,6},{9,8},{10,9},{11,10},{12... | collective-permute-start | bytes 196616 | tf_op jit(solution)/shard_map/ppermute | solution.py:15
  76.3 20.2 %collective-permute-start.5 = (f32[3,2,32,2,128]{4,2,1,0,3:T(8,128)}, f32[3,2,32,2,128]{4,2,1,0,3:T(8,128)}, u32[]{:S(2)}, u32[]{:S(2)}) collective-permute-start(f32[3,2,32,2,128]{4,2,1,0,3:T(8,128)} %fusion.3), channel_id=1, source_target_pairs={{8,0},{16,8},{24,16},{32,24},{40,32},{48,40},{56,48},{64,56},{72,6... | collective-permute-start | bytes 589832 | tf_op jit(solution)/shard_map/ppermute | solution.py:15
  260.6 6.3 collective-permute-start.6
  263.4 27.5 %collective-permute-start.7 = (f32[3,2,32,2,128]{4,2,1,0,3:T(8,128)S(1)}, f32[3,2,32,2,128]{4,2,1,0,3:T(8,128)S(1)}, u32[]{:S(2)}, u32[]{:S(2)}) collective-permute-start(f32[3,2,32,2,128]{4,2,1,0,3:T(8,128)S(1)} %pad_maximum_fusion.2), channel_id=1, source_target_pairs={{0,8},{8,16},{16,24},{24,32},{32,40},{40,48},{48,56},{56,64},{64,7... | collective-permute-start | bytes 589832 | tf_op jit(solution)/shard_map/ppermute | solution.py:15
  293.0 25.6 %copy-start.8 = (f32[2,2,32,1,128]{4,2,1,0,3:T(8,128)}, f32[2,2,32,1,128]{4,2,1,0,3:T(8,128)S(1)}, u32[]{:S(2)}) copy-start(f32[2,2,32,1,128]{4,2,1,0,3:T(8,128)S(1)} %get-tuple-element.565) | copy-start | bytes 196612
  294.8 22.4 %collective-permute-start.9 = (f32[3,2,32,2,128]{4,2,0,1,3:T(8,128)}, f32[3,2,32,2,128]{4,2,0,1,3:T(8,128)}, u32[]{:S(2)}, u32[]{:S(2)}) collective-permute-start(f32[3,2,32,2,128]{4,2,0,1,3:T(8,128)} %copy.1042), channel_id=1, source_target_pairs={{8,0},{16,8},{24,16},{32,24},{40,32},{48,40},{56,48},{64,56},{72,6... | collective-permute-start | bytes 589832 | tf_op jit(solution)/shard_map/ppermute | solution.py:15
  296.7 17.8 %collective-permute-start.8 = (f32[2,1,32,2,128]{4,2,3,0,1:T(8,128)S(1)}, f32[2,1,32,2,128]{4,2,3,0,1:T(8,128)S(1)}, u32[]{:S(2)}, u32[]{:S(2)}) collective-permute-start(f32[2,1,32,2,128]{4,2,3,0,1:T(8,128)S(1)} %copy.1027), channel_id=1, source_target_pairs={{1,0},{2,1},{3,2},{4,3},{5,4},{6,5},{7,6},{9,8},{10,9},{11,10},{12... | collective-permute-start | bytes 196616 | tf_op jit(solution)/shard_map/ppermute | solution.py:15
  483.7 6.4 collective-permute-start.10
  487.8 26.3 %collective-permute-start.11 = (f32[3,2,32,2,128]{4,2,3,1,0:T(8,128)S(1)}, f32[3,2,32,2,128]{4,2,3,1,0:T(8,128)S(1)}, u32[]{:S(2)}, u32[]{:S(2)}) collective-permute-start(f32[3,2,32,2,128]{4,2,3,1,0:T(8,128)S(1)} %pad_maximum_fusion.3), channel_id=1, source_target_pairs={{0,8},{8,16},{16,24},{24,32},{32,40},{40,48},{48,56},{56,64},{64,7... | collective-permute-start | bytes 589832 | tf_op jit(solution)/shard_map/ppermute | solution.py:15
  521.8 9.1 collective-permute-start.12
  523.7 11.7 %collective-permute-start.13 = (f32[3,2,32,2,128]{4,2,1,0,3:T(8,128)}, f32[3,2,32,2,128]{4,2,1,0,3:T(8,128)}, u32[]{:S(2)}, u32[]{:S(2)}) collective-permute-start(f32[3,2,32,2,128]{4,2,1,0,3:T(8,128)} %fusion.1), channel_id=1, source_target_pairs={{8,0},{16,8},{24,16},{32,24},{40,32},{48,40},{56,48},{64,56},{72,6... | collective-permute-start | bytes 589832 | tf_op jit(solution)/shard_map/ppermute | solution.py:15
  717.3 7.0 collective-permute-start.14
  721.3 22.3 %collective-permute-start.15 = (f32[3,2,32,2,128]{4,2,1,0,3:T(8,128)S(1)}, f32[3,2,32,2,128]{4,2,1,0,3:T(8,128)S(1)}, u32[]{:S(2)}, u32[]{:S(2)}) collective-permute-start(f32[3,2,32,2,128]{4,2,1,0,3:T(8,128)S(1)} %pad_maximum_fusion.4), channel_id=1, source_target_pairs={{0,8},{8,16},{16,24},{24,32},{32,40},{40,48},{48,56},{56,64},{64,7... | collective-permute-start | bytes 589832 | tf_op jit(solution)/shard_map/ppermute | solution.py:15
  749.3 9.4 collective-permute-start.16
  750.6 10.0 %collective-permute-start.17 = (f32[3,2,32,2,128]{4,2,3,1,0:T(8,128)S(1)}, f32[3,2,32,2,128]{4,2,3,1,0:T(8,128)S(1)}, u32[]{:S(2)}, u32[]{:S(2)}) collective-permute-start(f32[3,2,32,2,128]{4,2,3,1,0:T(8,128)S(1)} %fusion), channel_id=1, source_target_pairs={{8,0},{16,8},{24,16},{32,24},{40,32},{48,40},{56,48},{64,56},{72,6... | collective-permute-start | bytes 589832 | tf_op jit(solution)/shard_map/ppermute | solution.py:15
  762.0 178.2 %copy-start.50 = (f32[6,2,2,32]{3,2,1,0:T(2,128)S(1)}, f32[6,2,2,32]{3,2,1,0:T(2,128)}, u32[]{:S(2)}) copy-start(f32[6,2,2,32]{3,2,1,0:T(2,128)} %copy-done.49) | copy-start | bytes 9220
  764.7 175.6 %copy-start.45 = (f32[6,2,2,32]{3,2,1,0:T(2,128)S(1)}, f32[6,2,2,32]{3,2,1,0:T(2,128)}, u32[]{:S(2)}) copy-start(f32[6,2,2,32]{3,2,1,0:T(2,128)} %copy-done.43) | copy-start | bytes 9220
  764.7 175.6 %copy-start.48 = (f32[6,2,2,32]{3,2,1,0:T(2,128)S(1)}, f32[6,2,2,32]{3,2,1,0:T(2,128)}, u32[]{:S(2)}) copy-start(f32[6,2,2,32]{3,2,1,0:T(2,128)} %copy-done.46) | copy-start | bytes 9220
  (50 other events, 152.6 us)
where the time goes:
time: 950 us; the launch traced here: 944 us
  blocking collectives  652 us (69%)
  waiting for transfers between devices  127 us (13%)
  starting transfers between devices  61.8 us (7%)
  other arithmetic  45 us (5%)
  between operations  36.9 us (4%)
  local copies, waits for them, and re-layouts  22.7 us (2%)
    psum x4, blocking collectives, totals(): return lax.psum((gamma_part, omega_part, cross_part), ('sec', 'row'))  652 us
    ppermute x18, waiting for transfers between devices, passed_along(): lax.ppermute(value, axis, [(source, source + steps) for source in range(l...  127 us
    ppermute x18, starting transfers between devices, passed_along(): lax.ppermute(value, axis, [(source, source + steps) for source in range(l...  61.8 us
  transfers between devices with their start and end apart: 18, of which 11 were waited for; matrix products, arithmetic and copies ran while one was open for 2% of the time, Pallas kernels for 0%

commit v1 on v0

v1 whole, which is shorter than its diff:
```python
import functools

import jax
import jax.numpy as jnp
from jax import lax
from jax.experimental import pallas as pl
from jax.experimental.pallas import tpu as pltpu
from jax.sharding import Mesh
from jax.sharding import PartitionSpec as P

ITERS = 4
SPAN = 1024.0
SHIFT = 512.0
HALF = SHIFT / SPAN
SQUARES = (0.49, 0.49, 0.09)
SYM = ((0, 0), (0, 1), (0, 2), (1, 1), (1, 2), (2, 2))
SEC_AXES = ("y", "zhi", "x", "core")
GROUP = ("x", "core")
OTHERS = ("y", "zhi", "row")

ROWS = 80
AT_C = 12
AT_LOW = 48
AT_SEND = 57


def sym_at(a, b):
    return SYM.index((min(a, b), max(a, b)))


def roll(value, shift, axis):
    size = value.shape[axis]
    return pltpu.roll(value, shift % size, axis)


def lane_bits(shape):
    lane = lax.broadcasted_iota(jnp.int32, shape, len(shape) - 1)
    return (lane // 32) % 2 == 0, lane < 64


def block_sums(first, second, live):
    u, v = first
    p, q = second
    dx = p - u
    dy = q - v

    def red(z):
        return jnp.sum(z, axis=0, keepdims=True)

    su, sv, sp, sq, n = red(u), red(v), red(p), red(q), red(live)
    F = [red(u * u), red(u * v), su, red(v * v), sv, n]
    G = [red(p * p), red(p * q), sp, red(q * q), sq, n]
    C = [red(u * p), red(u * q), su, red(v * p), red(v * q), sv, sp, sq, n]
    tx, ty = red(dx), red(dy)
    s1 = [red(dx * u), red(dx * v), tx, red(dy * u), red(dy * v), ty]
    s2 = [red(dx * p), red(dx * q), tx, red(dy * p), red(dy * q), ty]
    return F, G, C, s1, s2


def gram_kernel(flags, f_ref, g_ref, counts_ref, up_ref, next_ref, low_ref, packet, kept):
    row_zero, sec_zero = lane_bits((1, 128))
    lane = lax.broadcasted_iota(jnp.int32, (1, 128), 1)
    last_row = flags[0] == 1
    last_sec = flags[1] == 1

    def pair_rows(ref, start, count, comp):
        return ref[pl.ds(2 * start + comp, count, stride=2), :]

    def own(ref, kind):
        return [pair_rows(ref, kind * 128, 128, comp).T for comp in range(2)]

    counts = counts_ref[...].astype(jnp.float32)
    zero = jnp.zeros((1, 128), jnp.float32)
    alive = [
        jnp.where(lane % 32 == 31, zero, counts[0:1]),
        jnp.where(jnp.logical_and(jnp.logical_not(row_zero), last_row), zero, counts[1:2]),
        jnp.where(jnp.logical_and(jnp.logical_not(sec_zero), last_sec), zero, counts[2:3]),
        jnp.where(last_sec, zero, counts[3:4]),
    ]
    point = lax.broadcasted_iota(jnp.int32, (128, 128), 0).astype(jnp.float32)

    def masked(points, count):
        live = jnp.where(point < count, 1.0, 0.0)
        return [z * live for z in points], live

    def second_of(kind):
        if kind == 0:
            return [roll(z, -1, 1) for z in own(g_ref, 0)]
        out = []
        for comp in range(2):
            if kind == 1:
                parts = [
                    pair_rows(g_ref, 128 + 32, 32, comp),
                    pair_rows(next_ref, 0, 32, comp),
                    pair_rows(g_ref, 128 + 96, 32, comp),
                    pair_rows(next_ref, 32, 32, comp),
                ]
            elif kind == 2:
                parts = [pair_rows(g_ref, 256 + 64, 64, comp), pair_rows(up_ref, 0, 64, comp)]
            else:
                parts = [pair_rows(up_ref, 64, 128, comp)]
            out.append(jnp.concatenate(parts, axis=0).T)
        return out

    D = [zero] * 6
    S = [zero] * 6
    unit = 1.0 / SPAN

    def put(row, value):
        packet[row : row + 1, :] = value

    for kind in range(4):
        first, live = masked(own(f_ref, kind), alive[kind])
        second, _ = masked(second_of(kind), alive[kind])
        kept[5 * kind] = first[0]
        kept[5 * kind + 1] = first[1]
        kept[5 * kind + 2] = second[0]
        kept[5 * kind + 3] = second[1]
        kept[5 * kind + 4] = live
        F, G, C, s1, s2 = block_sums(first, second, live)
        D = [a + b for a, b in zip(D, F)]
        S = [a + b for a, b in zip(S, s1)]
        for i in range(9):
            put(AT_C + 9 * kind + i, C[i] * unit)
        if kind == 0:
            D = [a + roll(b, 1, 1) for a, b in zip(D, G)]
            S = [a - roll(b, 1, 1) for a, b in zip(S, s2)]
        elif kind == 1:
            D = [a + jnp.where(row_zero, zero, roll(b, 32, 1)) for a, b in zip(D, G)]
            S = [a - jnp.where(row_zero, zero, roll(b, 32, 1)) for a, b in zip(S, s2)]
        elif kind == 2:
            D = [a + jnp.where(sec_zero, zero, roll(b, 64, 1)) for a, b in zip(D, G)]
            S = [a - jnp.where(sec_zero, zero, roll(b, 64, 1)) for a, b in zip(S, s2)]
        if kind >= 2:
            base = AT_SEND + 9 * (kind - 2)
            put(base, G[0] * unit)
            put(base + 1, G[1] * unit)
            put(base + 2, G[3] * unit)
            for i in range(6):
                put(base + 3 + i, s2[i])

    low_count = jnp.where(row_zero, zero, low_ref[128:129, :])
    first = []
    second = []
    for comp in range(2):
        low = [pair_rows(low_ref, 32 * sec, 32, comp) for sec in range(2)]
        first.append(jnp.concatenate([low[0], low[0], low[1], low[1]], axis=0).T)
        mine = [pair_rows(g_ref, 128 + 64 * sec, 32, comp) for sec in range(2)]
        second.append(jnp.concatenate([mine[0], mine[0], mine[1], mine[1]], axis=0).T)
    first, live = masked(first, low_count)
    second, _ = masked(second, low_count)
    F, G, C, s1, s2 = block_sums(first, second, live)
    for i in range(9):
        put(AT_LOW + i, C[i] * unit)
    D = [a + jnp.where(row_zero, roll(b, -32, 1), zero) for a, b in zip(D, G)]
    S = [a - jnp.where(row_zero, roll(b, -32, 1), zero) for a, b in zip(S, s2)]

    for i in range(6):
        a, b = SYM[i]
        put(i, D[i] * unit + ((SQUARES[a] - SHIFT) * unit if a == b else 0.0))
        put(6 + i, S[i])
    for row in range(AT_SEND + 18, ROWS):
        put(row, zero)


def from_above(value):
    return roll(value, -1, 0)


def from_below(value):
    return roll(value, 1, 0)


def seconds_of(value, value_next, bits):
    row_zero, sec_zero = bits
    half = roll(value, 64, 1)
    return [
        roll(value, -1, 1),
        jnp.where(row_zero, roll(value, -32, 1), roll(value_next, 32, 1)),
        jnp.where(sec_zero, half, from_above(half)),
        from_above(value),
    ]


def window_kernel(got, blocks, start):
    n_dev = got.shape[0] // (2 * ROWS)

    def row(i):
        parts = []
        for slot, dev in [(1, d) for d in range(n_dev // 2, n_dev)] + [(0, d) for d in range(n_dev)] + [
            (1, d) for d in range(n_dev // 2)
        ]:
            at = (dev * 2 + slot) * ROWS + i
            parts.append(got[at : at + 1, :])
        return jnp.concatenate(parts, axis=0)

    row_zero, sec_zero = lane_bits((2 * n_dev, 128))
    zero = jnp.zeros((2 * n_dev, 128), jnp.float32)
    C = {(k, i): row(AT_C + 9 * k + i) for k in range(4) for i in range(9)}
    for (k, i), value in C.items():
        blocks[6 + 9 * k + i] = value
    for i in range(9):
        blocks[42 + i] = row(AT_LOW + i)

    def pushed(kind, value):
        if kind == 2:
            return from_below(jnp.where(sec_zero, roll(value, 64, 1), zero))
        return from_below(value)

    D = [row(i) for i in range(6)]
    S = [row(6 + i) for i in range(6)]
    for kind in (2, 3):
        base = AT_SEND + 9 * (kind - 2)
        G = [row(base), row(base + 1), C[kind, 6], row(base + 2), C[kind, 7], C[kind, 8]]
        D = [a + pushed(kind, b) for a, b in zip(D, G)]
        S = [a - pushed(kind, row(base + 3 + i)) for i, a in enumerate(S)]
    for i in range(6):
        blocks[i] = D[i]
        start[i] = S[i]


def apply_kernel(blocks, v_ref, next_ref, low_ref, out):
    shape = v_ref.shape[1:]
    bits = lane_bits(shape)
    row_zero, sec_zero = bits
    v = [v_ref[i] for i in range(6)]
    after = [seconds_of(v[i], next_ref[i], bits) for i in range(6)]
    total = [None] * 6
    for half in range(2):
        a = v[3 * half : 3 * half + 3]
        for i in range(3):
            total[3 * half + i] = sum(blocks[sym_at(i, j)] * a[j] for j in range(3))
    for kind in range(4):
        C = [[blocks[6 + 9 * kind + 3 * i + j] for j in range(3)] for i in range(3)]
        for half in range(2):
            a = v[3 * half : 3 * half + 3]
            b = [after[3 * half + j][kind] for j in range(3)]
            for i in range(3):
                total[3 * half + i] -= C[i][0] * b[0] + C[i][1] * b[1] + C[i][2] * b[2]
            for j in range(3):
                t = C[0][j] * a[0] + C[1][j] * a[1] + C[2][j] * a[2]
                if kind == 0:
                    t = roll(t, 1, 1)
                elif kind == 1:
                    low = [low_ref[3 * half + i] for i in range(3)]
                    t_low = sum(blocks[42 + 3 * i + j] * low[i] for i in range(3))
                    t = jnp.where(row_zero, roll(t_low, -32, 1), roll(t, 32, 1))
                elif kind == 2:
                    t = roll(t, 64, 1)
                    t = jnp.where(sec_zero, from_below(t), t)
                else:
                    t = from_below(t)
                total[3 * half + j] -= t
    for i in range(6):
        out[i] = total[i]


def moments_kernel(blocks, v0, v1, v2, v3, next_ref, out):
    shape = v3.shape[1:]
    bits = lane_bits(shape)
    quarter = shape[0] // 4
    dev = lax.broadcasted_iota(jnp.int32, shape, 0)
    inside = jnp.logical_and(dev >= quarter, dev < 3 * quarter)
    vs = [[ref[i] for i in range(6)] for ref in (v0, v1, v2, v3)]

    def dot(left, right):
        return sum(a * b for a, b in zip(left, right))

    products = [dot(vs[n // 2], vs[n - n // 2]) for n in range(7)]
    energy = 0.0
    after = [seconds_of(vs[3][i], next_ref[i], bits) for i in range(6)]
    for half in range(2):
        a = vs[3][3 * half : 3 * half + 3]
        for i in range(3):
            inner = sum(blocks[sym_at(i, j)] * a[j] for j in range(3))
            for kind in range(4):
                cross = sum(blocks[6 + 9 * kind + 3 * i + j] * after[3 * half + j][kind] for j in range(3))
                inner = inner - 2.0 * cross
            energy = energy + a[i] * inner
    products.append(energy)
    lane = lax.broadcasted_iota(jnp.int32, (1, 128), 1)
    packed = jnp.zeros((1, 128), jnp.float32)
    for n, value in enumerate(products):
        value = jnp.where(inside, value, 0.0)
        value = jnp.sum(jnp.sum(value, axis=0, keepdims=True), axis=1, keepdims=True)
        packed = jnp.where(lane == n, value, packed)
    out[...] = packed


def coefficients(moments):
    zero = jnp.zeros_like(moments[0])

    def inner(s, p, offset):
        total = zero
        for i, a in enumerate(s):
            for j, b in enumerate(p):
                total = total + a * b * moments[i + j + offset]
        return total

    def energy(p):
        return inner(p, p, 1) + HALF * inner(p, p, 0)

    s = [zero + 1.0]
    p = [zero + 1.0]
    x = [zero] * ITERS
    gamma = inner(s, s, 0)
    for sweep in range(ITERS):
        alpha = gamma / energy(p)
        x = [x[i] + (alpha * p[i] if i < len(p) else 0.0) for i in range(ITERS)]
        if sweep < ITERS - 1:
            image = [(p[i - 1] if i else 0.0) + (HALF * p[i] if i < len(p) else 0.0) for i in range(len(p) + 1)]
            s = [(s[i] if i < len(s) else 0.0) - alpha * image[i] for i in range(len(image))]
            gamma_new = inner(s, s, 0)
            beta = gamma_new / gamma
            p = [s[i] + (beta * p[i] if i < len(p) else 0.0) for i in range(len(s))]
            gamma = gamma_new
    return [value * (1.0 / SPAN) for value in x]


def finish_kernel(place, sums, v0, v1, v2, v3, n0, n1, n2, n3, kept, affines, residual):
    total = jnp.sum(sums[...], axis=0, keepdims=True)
    lane = lax.broadcasted_iota(jnp.int32, (1, 128), 1)
    moments = [jnp.sum(jnp.where(lane == n, total, 0.0), axis=1, keepdims=True) for n in range(8)]
    weights = coefficients(moments)
    at = place[0]
    row_zero, sec_zero = lane_bits((1, 128))

    def mix(refs, i, dev):
        return sum(w * ref[i, pl.ds(dev, 1), :] for w, ref in zip(weights, refs))

    vs = (v0, v1, v2, v3)
    x = [mix(vs, i, at) for i in range(6)]
    above = [mix(vs, i, at + 1) for i in range(6)]
    beside = [mix((n0, n1, n2, n3), i, at) for i in range(6)]
    for i in range(6):
        affines[i : i + 1, :] = x[i]
    for kind in range(4):
        if kind == 0:
            b = [roll(z, -1, 1) for z in x]
        elif kind == 1:
            b = [jnp.where(row_zero, roll(z, -32, 1), roll(w, 32, 1)) for z, w in zip(x, beside)]
        elif kind == 2:
            b = [jnp.where(sec_zero, roll(z, 64, 1), roll(w, 64, 1)) for z, w in zip(x, above)]
        else:
            b = above
        u, v, p, q, live = (kept[5 * kind + i] for i in range(5))
        for comp in range(2):
            o = 3 * comp
            r = (p - u) if comp == 0 else (q - v)
            r = r - (x[o] * u + x[o + 1] * v) + (b[o] * p + b[o + 1] * q) - live * (x[o + 2] - b[o + 2])
            residual[pl.ds(kind * 256 + comp, 128, stride=2), :] = r.T


def shape_of(*shape):
    return jax.ShapeDtypeStruct(shape, jnp.float32)


def call(kernel, outs, *args, scalars=0, interpret=False):
    spaces = [pl.BlockSpec(memory_space=pltpu.SMEM)] * scalars
    spaces += [pl.BlockSpec(memory_space=pltpu.VMEM)] * (len(args) - scalars)
    many = isinstance(outs, (list, tuple))
    out_specs = [pl.BlockSpec(memory_space=pltpu.VMEM) for _ in outs] if many else pl.BlockSpec(memory_space=pltpu.VMEM)
    return pl.pallas_call(kernel, out_shape=outs, in_specs=spaces, out_specs=out_specs, interpret=interpret)(*args)


def shifted(value, axes, steps):
    count = lax.axis_size(axes)
    pairs = [(i, i + steps) for i in range(count) if 0 <= i + steps < count]
    return lax.ppermute(value, axes, pairs)


def per_device(interpret, first_pts, second_pts, counts):
    run = functools.partial(call, interpret=interpret)
    n_sec = lax.axis_size(SEC_AXES)
    n_dev = lax.axis_size(GROUP)
    n_group = n_sec // n_dev
    sec = lax.axis_index(SEC_AXES)
    member = lax.axis_index(GROUP)
    f = first_pts.reshape(1024, 128)
    g = second_pts.reshape(1024, 128)
    lives = counts.reshape(4, 128)

    up = shifted(jnp.concatenate([g[512:640], g[768:1024]], axis=0), SEC_AXES, -1)
    beside = shifted(jnp.concatenate([g[256:320], g[384:448]], axis=0), "row", -1)
    odd = jnp.concatenate(
        [f[320:384], f[448:512], jnp.broadcast_to(lives[1:2].astype(jnp.float32), (8, 128))], axis=0
    )
    low = shifted(odd, "row", 1)
    flags = jnp.stack(
        [
            (lax.axis_index("row") == lax.axis_size("row") - 1).astype(jnp.int32),
            (sec == n_sec - 1).astype(jnp.int32),
        ]
    )
    packet, kept = run(gram_kernel, [shape_of(ROWS, 128), shape_of(20, 128, 128)], flags, f, g, lives, up, beside, low, scalars=1)

    half = n_dev // 2
    pairs = []
    for group in range(n_group):
        for dev in range(n_dev):
            source = group + (1 if dev < half else -1)
            if 0 <= source < n_group:
                pairs.append((source * n_dev + dev, group * n_dev + dev))
    other = lax.ppermute(packet, SEC_AXES, pairs)
    mine = jnp.concatenate([packet, other], axis=0)
    got = lax.all_to_all(jnp.broadcast_to(mine[None], (n_dev, 2 * ROWS, 128)), GROUP, 0, 0, tiled=False)
    blocks, v0 = run(
        window_kernel, [shape_of(51, 2 * n_dev, 128), shape_of(6, 2 * n_dev, 128)], got.reshape(n_dev * 2 * ROWS, 128)
    )
    vs = [v0]
    nexts = []
    for step in range(ITERS - 1):
        v = vs[-1]
        nexts.append(shifted(v, "row", -1))
        lows = shifted(v, "row", 1)
        vs.append(run(apply_kernel, shape_of(*v.shape), blocks, v, nexts[-1], lows))
    nexts.append(shifted(vs[-1], "row", -1))
    part = run(moments_kernel, shape_of(1, 128), blocks, *vs, nexts[-1])
    n_other = lax.axis_size(OTHERS)
    sums = lax.all_to_all(jnp.broadcast_to(part[None], (n_other, 1, 128)), OTHERS, 0, 0, tiled=False)
    place = (member + n_dev // 2).astype(jnp.int32).reshape(1)
    affines, residual = run(
        finish_kernel,
        [shape_of(6, 128), shape_of(1024, 128)],
        place,
        sums.reshape(n_other, 128),
        *vs,
        *nexts,
        kept,
        scalars=1,
    )
    return affines.reshape((6,) + counts.shape[1:]), residual.reshape(first_pts.shape)


def split_mesh(mesh):
    n_row = mesh.shape["row"]
    return Mesh(mesh.devices.reshape(4, 4, 4, 2, n_row), SEC_AXES + ("row",))


def solution(mesh, inner=None, interpret=False):
    inner = inner or split_mesh(mesh)
    in_specs = (
        P(None, SEC_AXES, "row", None, None, None),
        P(None, SEC_AXES, "row", None, None, None),
        P(None, SEC_AXES, "row", None),
    )
    out_specs = (P(None, SEC_AXES, "row", None), P(None, SEC_AXES, "row", None, None, None))
    return jax.shard_map(
        functools.partial(per_device, interpret), mesh=inner, in_specs=in_specs, out_specs=out_specs, check_vma=False
    )
```

time: 950 us -> 189 us (0.20)
  blocking collectives: 652 us -> 15.6 us
  waiting for transfers between devices: 127 us -> 49.9 us
  other arithmetic: 45 us -> 2.12 us
  between operations: 36.9 us -> 0.79 us
  starting transfers between devices: 61.8 us -> 91.4 us
  Pallas kernels: 0 us -> 15.2 us
  local copies, waits for them, and re-layouts: 22.7 us -> 11.2 us
    psum x4 -> x0, blocking collectives: 652 us -> none  [totals(): return lax.psum((gamma_part, omega_part, cross_part), ('sec', 'row'))]
    ppermute x18 -> x11, waiting for transfers between devices: 127 us -> 26.6 us  [the longest x10 20.2 us: shifted(): return lax.ppermute(value, axes, pairs)]
    all_to_all x0 -> x1, starting transfers between devices: none -> 28.4 us  [per_device(): lax.all_to_all(jnp.broadcast_to(part[None], (n_other, 1, 128)), OTHERS, 0...]
    reduce_sum x56 -> x0, other arithmetic: 26.1 us -> none  [the longest x17 16 us: local_inner(): summed = summed + jnp.sum(list_a[kind_no] * list_b[kind_no])]
    all_to_all x0 -> x1, waiting for transfers between devices: none -> 23.3 us  [per_device(): lax.all_to_all(jnp.broadcast_to(part[None], (n_other, 1, 128)), OTHERS, 0...]
    all_to_all x0 -> x1, blocking collectives: none -> 15.6 us  [per_device(): lax.all_to_all(jnp.broadcast_to(mine[None], (n_dev, 2 * ROWS, 128)), GROU...]
    pallas_call x0 -> x7, Pallas kernels: none -> 15.2 us  [call(): pl.pallas_call(kernel, out_shape=outs, in_specs=spaces, out_specs=out_spe...]
    unnamed x291 -> x24, local copies, waits for them, and re-layouts: 15.7 us -> 4.39 us
  transfers between devices with their start and end apart: 18 -> 12, of which waited for: 11 -> 10; matrix products, arithmetic and copies ran while one was open for 2% -> 2% of each run, Pallas kernels for 0% -> 0%
where the time goes in v1:
time: 189 us; the launch traced here: 186 us
  starting transfers between devices  91.4 us (48%)
  waiting for transfers between devices  49.9 us (26%)
  blocking collectives  15.6 us (8%)
  Pallas kernels  15.2 us (8%)
  local copies, waits for them, and re-layouts  11.2 us (6%)
  other arithmetic  2.12 us (1%)
    ppermute x10, starting transfers between devices, shifted(): return lax.ppermute(value, axes, pairs)  54.6 us
    all_to_all x1, starting transfers between devices, per_device(): lax.all_to_all(jnp.broadcast_to(part[None], (n_other, 1, 128)), OTHERS, 0...  28.4 us
    all_to_all x1, waiting for transfers between devices, per_device(): lax.all_to_all(jnp.broadcast_to(part[None], (n_other, 1, 128)), OTHERS, 0...  23.3 us
    ppermute x10, waiting for transfers between devices, shifted(): return lax.ppermute(value, axes, pairs)  20.2 us
    all_to_all x1, blocking collectives, per_device(): lax.all_to_all(jnp.broadcast_to(mine[None], (n_dev, 2 * ROWS, 128)), GROU...  15.6 us
    pallas_call x7, Pallas kernels, call(): pl.pallas_call(kernel, out_shape=outs, in_specs=spaces, out_specs=out_spe...  15.2 us
    ppermute x1, starting transfers between devices, per_device(): other = lax.ppermute(packet, SEC_AXES, pairs)  8.43 us
    ppermute x1, waiting for transfers between devices, per_device(): other = lax.ppermute(packet, SEC_AXES, pairs)  6.37 us
  transfers between devices with their start and end apart: 12, of which 10 were waited for; matrix products, arithmetic and copies ran while one was open for 2% of the time, Pallas kernels for 0%

profile of v1, /device:TPU:24, one launch (start us, length us, event | category | flops | bytes accessed | tf_op | source)
XLA Modules:
  0.0 186.2 jit_solution(6030834542482754501)
XLA Ops:
  1.4 1.3 collective-permute-start.1
  4.5 24.8 %collective-permute-start = (f32[384,128]{1,0:T(8,128)S(1)}, f32[384,128]{1,0:T(8,128)S(1)}, u32[]{:S(2)}, u32[]{:S(2)}) collective-permute-start(f32[384,128]{1,0:T(8,128)S(1)} %pad_maximum_fusion), channel_id=1, source_target_pairs={{8,0},{16,8},{24,16},{32,24},{40,32},{48,40},{56,48},{64,56},{72,6... | collective-permute-start | bytes 589832 | tf_op jit(solution)/shard_map/ppermute | solution.py:369
  30.9 4.3 %collective-permute-start.2 = (f32[136,128]{1,0:T(8,128)S(1)}, f32[136,128]{1,0:T(8,128)S(1)}, u32[]{:S(2)}, u32[]{:S(2)}) collective-permute-start(f32[136,128]{1,0:T(8,128)S(1)} %pad_maximum_fusion.2), channel_id=1, source_target_pairs={{0,1},{1,2},{2,3},{3,4},{4,5},{5,6},{6,7},{8,9},{9,10},{10,11},{11... | collective-permute-start | bytes 208904 | tf_op jit(solution)/shard_map/ppermute | solution.py:369
  38.4 2.9 %shard_map.50 = (f32[80,128]{1,0:T(8,128)}, f32[20,128,128]{2,1,0:T(8,128)}) custom-call(s32[2]{0:T(128)} %add_convert_fusion.flags, f32[1024,128]{1,0:T(8,128)} %bitcast.15, f32[1024,128]{1,0:T(8,128)} %bitcast.13, s32[4,128]{1,0:T(4,128)} %reshape.45.counts_ref, f32[384,128]{1,0:T(8,128)} %copy-done.1, f32[128,128]{1,0:T(8,128)} %copy-done.7, ...), custom_call_target="tpu_custom_call" | custom-call | tf_op jit(solution)/shard_map/pallas_call | solution.py:363
  41.3 8.4 %collective-permute-start.3 = (f32[80,128]{1,0:T(8,128)}, f32[80,128]{1,0:T(8,128)S(1)}, u32[]{:S(2)}, u32[]{:S(2)}) collective-permute-start(f32[80,128]{1,0:T(8,128)} %get-tuple-element.8), channel_id=1, source_target_pairs={{64,0},{72,8},{80,16},{88,24},{128,64},{136,72},{144,80},{152,88},... | collective-permute-start | bytes 122888 | tf_op jit(solution)/shard_map/ppermute | solution.py:404
  49.7 6.4 %collective-permute-done.3 = f32[80,128]{1,0:T(8,128)S(1)} collective-permute-done((f32[80,128]{1,0:T(8,128)}, f32[80,128]{1,0:T(8,128)S(1)}, u32[]{:S(2)}, u32[]{:S(2)}) %collective-permute-start.3) | collective-permute-done | bytes 40992 | tf_op jit(solution)/shard_map/ppermute | solution.py:404
  56.9 15.6 %all_to_all.10 = f32[8,160,128]{2,1,0:T(8,128)} all-to-all(f32[8,160,128]{2,1,0:T(8,128)S(1)} %broadcast_in_dim.9), channel_id=1, replica_groups=mesh['y'=4,'zhi'=4,'x'=4,'core'=2,'row'=8] {'x','core'}, dimensions={0} | all-to-all | bytes 1310720 | tf_op jit(solution)/shard_map/all_to_all | solution.py:406
  72.5 2.2 %shard_map.51 = (f32[51,16,128]{2,1,0:T(8,128)}, f32[6,16,128]{2,1,0:T(8,128)}) custom-call(f32[1280,128]{1,0:T(8,128)} %bitcast.10), custom_call_target="tpu_custom_call" | custom-call | tf_op jit(solution)/shard_map/pallas_call | solution.py:363
  74.7 15.2 %collective-permute-start.5 = (f32[6,16,128]{2,1,0:T(8,128)}, f32[6,16,128]{2,1,0:T(8,128)S(1)}, u32[]{:S(2)}, u32[]{:S(2)}) collective-permute-start(f32[6,16,128]{2,1,0:T(8,128)} %get-tuple-element.10.v_ref.v0), channel_id=1, source_target_pairs={{0,1},{1,2},{2,3},{3,4},{4,5},{5,6},{6,7},{8,9},{9,10},{10,11},{11... | collective-permute-start | bytes 147464 | tf_op jit(solution)/shard_map/ppermute | solution.py:369
  92.0 4.1 %collective-permute-done.4.next_ref.n0 = f32[6,16,128]{2,1,0:T(8,128)S(1)} collective-permute-done((f32[6,16,128]{2,1,0:T(8,128)}, f32[6,16,128]{2,1,0:T(8,128)S(1)}, u32[]{:S(2)}, u32[]{:S(2)}) %collective-permute-start.4) | collective-permute-done | bytes 49184 | tf_op jit(solution)/shard_map/ppermute | solution.py:369
  96.7 1.8 shard_map.52.v_ref.v1
  98.5 1.9 %collective-permute-start.7 = (f32[6,16,128]{2,1,0:T(8,128)}, f32[6,16,128]{2,1,0:T(8,128)S(1)}, u32[]{:S(2)}, u32[]{:S(2)}) collective-permute-start(f32[6,16,128]{2,1,0:T(8,128)} %shard_map.52.v_ref.v1), channel_id=1, source_target_pairs={{0,1},{1,2},{2,3},{3,4},{4,5},{5,6},{6,7},{8,9},{9,10},{10,11},{11... | collective-permute-start | bytes 147464 | tf_op jit(solution)/shard_map/ppermute | solution.py:369
  102.5 4.1 %collective-permute-done.6.next_ref.n1 = f32[6,16,128]{2,1,0:T(8,128)S(1)} collective-permute-done((f32[6,16,128]{2,1,0:T(8,128)}, f32[6,16,128]{2,1,0:T(8,128)S(1)}, u32[]{:S(2)}, u32[]{:S(2)}) %collective-permute-start.6) | collective-permute-done | bytes 49184 | tf_op jit(solution)/shard_map/ppermute | solution.py:369
  107.3 1.8 shard_map.53.v_ref.v2
  109.1 1.9 %collective-permute-start.9 = (f32[6,16,128]{2,1,0:T(8,128)}, f32[6,16,128]{2,1,0:T(8,128)S(1)}, u32[]{:S(2)}, u32[]{:S(2)}) collective-permute-start(f32[6,16,128]{2,1,0:T(8,128)} %shard_map.53.v_ref.v2), channel_id=1, source_target_pairs={{0,1},{1,2},{2,3},{3,4},{4,5},{5,6},{6,7},{8,9},{9,10},{10,11},{11... | collective-permute-start | bytes 147464 | tf_op jit(solution)/shard_map/ppermute | solution.py:369
  113.1 4.1 %collective-permute-done.8.next_ref.n2 = f32[6,16,128]{2,1,0:T(8,128)S(1)} collective-permute-done((f32[6,16,128]{2,1,0:T(8,128)}, f32[6,16,128]{2,1,0:T(8,128)S(1)}, u32[]{:S(2)}, u32[]{:S(2)}) %collective-permute-start.8) | collective-permute-done | bytes 49184 | tf_op jit(solution)/shard_map/ppermute | solution.py:369
  117.8 1.8 shard_map.54.v3
  120.9 4.9 %collective-permute-done.10.next_ref.n3 = f32[6,16,128]{2,1,0:T(8,128)S(1)} collective-permute-done((f32[6,16,128]{2,1,0:T(8,128)}, f32[6,16,128]{2,1,0:T(8,128)S(1)}, u32[]{:S(2)}, u32[]{:S(2)}) %collective-permute-start.10) | collective-permute-done | bytes 49184 | tf_op jit(solution)/shard_map/ppermute | solution.py:369
  126.5 1.8 shard_map.55
  128.2 1.3 broadcast_in_dim.22
  129.6 28.4 %all-to-all-start.1 = ((f32[128,1,128]{2,1,0:T(1,128)}), f32[128,1,128]{2,1,0:T(1,128)S(1)}, u32[]{:S(2)}, u32[]{:S(2)}) async-start(f32[128,1,128]{2,1,0:T(1,128)} %broadcast_in_dim.22), calls=%async_computation.1 | async-start | bytes 131072 | tf_op jit(solution)/shard_map/all_to_all | solution.py:420
  158.0 23.3 %all-to-all-done.1 = f32[128,1,128]{2,1,0:T(1,128)S(1)} async-done(((f32[128,1,128]{2,1,0:T(1,128)}), f32[128,1,128]{2,1,0:T(1,128)S(1)}, u32[]{:S(2)}, u32[]{:S(2)}) %all-to-all-start.1) | async-done | bytes 65568 | tf_op jit(solution)/shard_map/all_to_all | solution.py:420
  181.9 2.9 %shard_map.56 = (f32[6,128]{1,0:T(8,128)}, f32[1024,128]{1,0:T(8,128)}) custom-call(s32[1]{0:T(128)} %bitcast.place, f32[128,128]{1,0:T(8,128)} %bitcast.17, f32[6,16,128]{2,1,0:T(8,128)} %get-tuple-element.10.v_ref.v0, f32[6,16,128]{2,1,0:T(8,128)} %shard_map.52.v_ref.v1, f32[6,16,128]{2,1,0:T(8,128)} %shard_map.53.v_ref.v2, f32[6,16,128]{2,1,0:T(8,128)} %shard_map.54.v3, ...), custom_call_target="tpu_custom_call" | custom-call | tf_op jit(solution)/shard_map/pallas_call | solution.py:363
  184.8 1.3 reshape.48
  (48 shorter events, 18.7 us)
Async XLA Ops:
  0.6 34.6 %copy-start.11 = (s32[4,2,2,32]{3,2,1,0:T(2,128)S(1)}, s32[4,2,2,32]{3,2,1,0:T(2,128)}, u32[]{:S(2)}) copy-start(s32[4,2,2,32]{3,2,1,0:T(2,128)} %param.5) | copy-start | bytes 6148
  1.4 35.0 %collective-permute-start.1 = (f32[128,128]{1,0:T(8,128)S(1)}, f32[128,128]{1,0:T(8,128)S(1)}, u32[]{:S(2)}, u32[]{:S(2)}) collective-permute-start(f32[128,128]{1,0:T(8,128)S(1)} %pad_maximum_fusion.3), channel_id=1, source_target_pairs={{1,0},{2,1},{3,2},{4,3},{5,4},{6,5},{7,6},{9,8},{10,9},{11,10},{12... | collective-permute-start | bytes 196616 | tf_op jit(solution)/shard_map/ppermute | solution.py:369
  4.5 32.6 %collective-permute-start = (f32[384,128]{1,0:T(8,128)S(1)}, f32[384,128]{1,0:T(8,128)S(1)}, u32[]{:S(2)}, u32[]{:S(2)}) collective-permute-start(f32[384,128]{1,0:T(8,128)S(1)} %pad_maximum_fusion), channel_id=1, source_target_pairs={{8,0},{16,8},{24,16},{32,24},{40,32},{48,40},{56,48},{64,56},{72,6... | collective-permute-start | bytes 589832 | tf_op jit(solution)/shard_map/ppermute | solution.py:369
  30.9 6.2 %collective-permute-start.2 = (f32[136,128]{1,0:T(8,128)S(1)}, f32[136,128]{1,0:T(8,128)S(1)}, u32[]{:S(2)}, u32[]{:S(2)}) collective-permute-start(f32[136,128]{1,0:T(8,128)S(1)} %pad_maximum_fusion.2), channel_id=1, source_target_pairs={{0,1},{1,2},{2,3},{3,4},{4,5},{5,6},{6,7},{8,9},{9,10},{10,11},{11... | collective-permute-start | bytes 208904 | tf_op jit(solution)/shard_map/ppermute | solution.py:369
  36.5 0.6 copy-start.7
  37.1 0.6 copy-start.6
  37.7 0.7 copy-start.1
  41.3 14.8 %collective-permute-start.3 = (f32[80,128]{1,0:T(8,128)}, f32[80,128]{1,0:T(8,128)S(1)}, u32[]{:S(2)}, u32[]{:S(2)}) collective-permute-start(f32[80,128]{1,0:T(8,128)} %get-tuple-element.8), channel_id=1, source_target_pairs={{64,0},{72,8},{80,16},{88,24},{128,64},{136,72},{144,80},{152,88},... | collective-permute-start | bytes 122888 | tf_op jit(solution)/shard_map/ppermute | solution.py:404
  74.7 17.3 %collective-permute-start.5 = (f32[6,16,128]{2,1,0:T(8,128)}, f32[6,16,128]{2,1,0:T(8,128)S(1)}, u32[]{:S(2)}, u32[]{:S(2)}) collective-permute-start(f32[6,16,128]{2,1,0:T(8,128)} %get-tuple-element.10.v_ref.v0), channel_id=1, source_target_pairs={{0,1},{1,2},{2,3},{3,4},{4,5},{5,6},{6,7},{8,9},{9,10},{10,11},{11... | collective-permute-start | bytes 147464 | tf_op jit(solution)/shard_map/ppermute | solution.py:369
  89.9 6.2 %collective-permute-start.4 = (f32[6,16,128]{2,1,0:T(8,128)}, f32[6,16,128]{2,1,0:T(8,128)S(1)}, u32[]{:S(2)}, u32[]{:S(2)}) collective-permute-start(f32[6,16,128]{2,1,0:T(8,128)} %get-tuple-element.10.v_ref.v0), channel_id=1, source_target_pairs={{1,0},{2,1},{3,2},{4,3},{5,4},{6,5},{7,6},{9,8},{10,9},{11,10},{12... | collective-permute-start | bytes 147464 | tf_op jit(solution)/shard_map/ppermute | solution.py:369
  92.0 4.2 %copy-start.8 = (f32[6,16,128]{2,1,0:T(8,128)}, f32[6,16,128]{2,1,0:T(8,128)S(1)}, u32[]{:S(2)}) copy-start(f32[6,16,128]{2,1,0:T(8,128)S(1)} %collective-permute-done.5.low_ref) | copy-start | bytes 147460
  96.1 0.6 copy-start.2
  98.5 4.0 %collective-permute-start.7 = (f32[6,16,128]{2,1,0:T(8,128)}, f32[6,16,128]{2,1,0:T(8,128)S(1)}, u32[]{:S(2)}, u32[]{:S(2)}) collective-permute-start(f32[6,16,128]{2,1,0:T(8,128)} %shard_map.52.v_ref.v1), channel_id=1, source_target_pairs={{0,1},{1,2},{2,3},{3,4},{4,5},{5,6},{6,7},{8,9},{9,10},{10,11},{11... | collective-permute-start | bytes 147464 | tf_op jit(solution)/shard_map/ppermute | solution.py:369
  100.5 6.2 %collective-permute-start.6 = (f32[6,16,128]{2,1,0:T(8,128)}, f32[6,16,128]{2,1,0:T(8,128)S(1)}, u32[]{:S(2)}, u32[]{:S(2)}) collective-permute-start(f32[6,16,128]{2,1,0:T(8,128)} %shard_map.52.v_ref.v1), channel_id=1, source_target_pairs={{1,0},{2,1},{3,2},{4,3},{5,4},{6,5},{7,6},{9,8},{10,9},{11,10},{12... | collective-permute-start | bytes 147464 | tf_op jit(solution)/shard_map/ppermute | solution.py:369
  102.5 4.1 %copy-start.9 = (f32[6,16,128]{2,1,0:T(8,128)}, f32[6,16,128]{2,1,0:T(8,128)S(1)}, u32[]{:S(2)}) copy-start(f32[6,16,128]{2,1,0:T(8,128)S(1)} %collective-permute-done.7.low_ref) | copy-start | bytes 147460
  106.7 0.6 copy-start.3
  109.1 4.0 %collective-permute-start.9 = (f32[6,16,128]{2,1,0:T(8,128)}, f32[6,16,128]{2,1,0:T(8,128)S(1)}, u32[]{:S(2)}, u32[]{:S(2)}) collective-permute-start(f32[6,16,128]{2,1,0:T(8,128)} %shard_map.53.v_ref.v2), channel_id=1, source_target_pairs={{0,1},{1,2},{2,3},{3,4},{4,5},{5,6},{6,7},{8,9},{9,10},{10,11},{11... | collective-permute-start | bytes 147464 | tf_op jit(solution)/shard_map/ppermute | solution.py:369
  111.0 6.2 %collective-permute-start.8 = (f32[6,16,128]{2,1,0:T(8,128)}, f32[6,16,128]{2,1,0:T(8,128)S(1)}, u32[]{:S(2)}, u32[]{:S(2)}) collective-permute-start(f32[6,16,128]{2,1,0:T(8,128)} %shard_map.53.v_ref.v2), channel_id=1, source_target_pairs={{1,0},{2,1},{3,2},{4,3},{5,4},{6,5},{7,6},{9,8},{10,9},{11,10},{12... | collective-permute-start | bytes 147464 | tf_op jit(solution)/shard_map/ppermute | solution.py:369
  113.1 4.1 %copy-start.10 = (f32[6,16,128]{2,1,0:T(8,128)}, f32[6,16,128]{2,1,0:T(8,128)S(1)}, u32[]{:S(2)}) copy-start(f32[6,16,128]{2,1,0:T(8,128)S(1)} %collective-permute-done.9.low_ref) | copy-start | bytes 147460
  117.2 0.6 copy-start.4
  119.7 6.2 %collective-permute-start.10 = (f32[6,16,128]{2,1,0:T(8,128)}, f32[6,16,128]{2,1,0:T(8,128)S(1)}, u32[]{:S(2)}, u32[]{:S(2)}) collective-permute-start(f32[6,16,128]{2,1,0:T(8,128)} %shard_map.54.v3), channel_id=1, source_target_pairs={{1,0},{2,1},{3,2},{4,3},{5,4},{6,5},{7,6},{9,8},{10,9},{11,10},{12... | collective-permute-start | bytes 147464 | tf_op jit(solution)/shard_map/ppermute | solution.py:369
  125.8 0.6 copy-start.5
  129.6 51.8 %all-to-all-start.1 = ((f32[128,1,128]{2,1,0:T(1,128)}), f32[128,1,128]{2,1,0:T(1,128)S(1)}, u32[]{:S(2)}, u32[]{:S(2)}) async-start(f32[128,1,128]{2,1,0:T(1,128)} %broadcast_in_dim.22), calls=%async_computation.1 | async-start | bytes 131072 | tf_op jit(solution)/shard_map/all_to_all | solution.py:420
  181.3 0.6 copy-start

commit v2 on v1

--- a/solution.py
+++ b/solution.py
@@ -18,10 +18,15 @@
 GROUP = ("x", "core")
 OTHERS = ("y", "zhi", "row")
 
-ROWS = 80
+ROWS = 72
 AT_C = 12
-AT_LOW = 48
-AT_SEND = 57
+AT_SEND = 48
+USED = 66
+AT_E = 66
+AT_E2 = 132
+DOUBLE = 160
+BEYOND = [AT_C + 9 + i for i in range(9)] + [6 + i for i in range(6)]
+BEYOND += [AT_SEND + 3 + i for i in range(6)] + [AT_SEND + 12 + i for i in range(6)]
 
 
 def sym_at(a, b):
@@ -36,6 +41,11 @@
 def lane_bits(shape):
     lane = lax.broadcasted_iota(jnp.int32, shape, len(shape) - 1)
     return (lane // 32) % 2 == 0, lane < 64
+
+
+def counts_row(ref, kind):
+    cells = [ref[kind, sec, row : row + 1, :] for sec in range(2) for row in range(2)]
+    return jnp.concatenate(cells, axis=1).astype(jnp.float32)
 
 
 def block_sums(first, second, live):
@@ -69,13 +79,13 @@
     def own(ref, kind):
         return [pair_rows(ref, kind * 128, 128, comp).T for comp in range(2)]
 
-    counts = counts_ref[...].astype(jnp.float32)
     zero = jnp.zeros((1, 128), jnp.float32)
+    counts = [counts_row(counts_ref, kind) for kind in range(4)]
     alive = [
-        jnp.where(lane % 32 == 31, zero, counts[0:1]),
-        jnp.where(jnp.logical_and(jnp.logical_not(row_zero), last_row), zero, counts[1:2]),
-        jnp.where(jnp.logical_and(jnp.logical_not(sec_zero), last_sec), zero, counts[2:3]),
-        jnp.where(last_sec, zero, counts[3:4]),
+        jnp.where(lane % 32 == 31, zero, counts[0]),
+        jnp.where(jnp.logical_and(jnp.logical_not(row_zero), last_row), zero, counts[1]),
+        jnp.where(jnp.logical_and(jnp.logical_not(sec_zero), last_sec), zero, counts[2]),
+        jnp.where(last_sec, zero, counts[3]),
     ]
     point = lax.broadcasted_iota(jnp.int32, (128, 128), 0).astype(jnp.float32)
 
@@ -150,8 +160,6 @@
     first, live = masked(first, low_count)
     second, _ = masked(second, low_count)
     F, G, C, s1, s2 = block_sums(first, second, live)
-    for i in range(9):
-        put(AT_LOW + i, C[i] * unit)
     D = [a + jnp.where(row_zero, roll(b, -32, 1), zero) for a, b in zip(D, G)]
     S = [a - jnp.where(row_zero, roll(b, -32, 1), zero) for a, b in zip(S, s2)]
 
@@ -171,117 +179,196 @@
     return roll(value, 1, 0)
 
 
-def seconds_of(value, value_next, bits):
-    row_zero, sec_zero = bits
-    half = roll(value, 64, 1)
-    return [
-        roll(value, -1, 1),
-        jnp.where(row_zero, roll(value, -32, 1), roll(value_next, 32, 1)),
-        jnp.where(sec_zero, half, from_above(half)),
-        from_above(value),
+def pack_up_kernel(g_ref, up, sems):
+    copies = [
+        pltpu.make_async_copy(g_ref.at[pl.ds(512, 128)], up.at[pl.ds(0, 128)], sems.at[0]),
+        pltpu.make_async_copy(g_ref.at[pl.ds(768, 256)], up.at[pl.ds(128, 256)], sems.at[1]),
     ]
-
-
-def window_kernel(got, blocks, start):
-    n_dev = got.shape[0] // (2 * ROWS)
-
-    def row(i):
-        parts = []
-        for slot, dev in [(1, d) for d in range(n_dev // 2, n_dev)] + [(0, d) for d in range(n_dev)] + [
-            (1, d) for d in range(n_dev // 2)
-        ]:
-            at = (dev * 2 + slot) * ROWS + i
-            parts.append(got[at : at + 1, :])
-        return jnp.concatenate(parts, axis=0)
-
+    for copy in copies:
+        copy.start()
+    for copy in copies:
+        copy.wait()
+
+
+def pack_rows_kernel(f_ref, g_ref, counts_ref, beside, odd, sems):
+    copies = [
+        pltpu.make_async_copy(g_ref.at[pl.ds(256, 64)], beside.at[pl.ds(0, 64)], sems.at[0]),
+        pltpu.make_async_copy(g_ref.at[pl.ds(384, 64)], beside.at[pl.ds(64, 64)], sems.at[1]),
+        pltpu.make_async_copy(f_ref.at[pl.ds(320, 64)], odd.at[pl.ds(0, 64)], sems.at[2]),
+        pltpu.make_async_copy(f_ref.at[pl.ds(448, 64)], odd.at[pl.ds(64, 64)], sems.at[3]),
+    ]
+    for copy in copies:
+        copy.start()
+    odd[128:136, :] = jnp.broadcast_to(counts_row(counts_ref, 1), (8, 128))
+    for copy in copies:
+        copy.wait()
+
+
+def merge_kernel(both, above, below, out):
+    row_zero, _ = lane_bits((1, 128))
+    for part in range(2):
+        at = part * ROWS
+        to = part * DOUBLE
+        out[to : to + USED, :] = both[at : at + USED, :]
+        a = above[at : at + USED, :]
+        b = below[at : at + USED, :]
+        out[to + AT_E : to + AT_E + USED, :] = jnp.where(row_zero, a, b)
+        for i, source in enumerate(BEYOND):
+            out[to + AT_E2 + i : to + AT_E2 + i + 1, :] = jnp.where(
+                row_zero, b[source : source + 1], a[source : source + 1]
+            )
+        out[to + AT_E2 + len(BEYOND) : to + DOUBLE, :] = jnp.zeros((DOUBLE - AT_E2 - len(BEYOND), 128), jnp.float32)
+
+
+class Window:
+    def __init__(self, load, n_dev):
+        self.load = load
+        self.bits = lane_bits((2 * n_dev, 128))
+
+    def seconds(self, v, row_values):
+        row_zero, sec_zero = self.bits
+        half = roll(v, 64, 1)
+        return [
+            roll(v, -1, 1),
+            row_values,
+            jnp.where(sec_zero, half, from_above(half)),
+            from_above(v),
+        ]
+
+    def row_pairs(self, v, e, e2):
+        row_zero, _ = self.bits
+        forth, back = roll(v, 32, 1), roll(v, -32, 1)
+        own = jnp.where(row_zero, back, roll(e, 32, 1))
+        side = jnp.where(row_zero, roll(e2, -32, 1), forth)
+        return own, side
+
+    def c(self, side, kind, i, j):
+        return self.load(side * 42 + 6 + 9 * kind + 3 * i + j)
+
+    def d(self, side, i, j):
+        return self.load(side * 42 + sym_at(i, j))
+
+    def c_e2(self, i, j):
+        return self.load(84 + 3 * i + j)
+
+    def transposed(self, c, a):
+        return [c(0, j) * a[0] + c(1, j) * a[1] + c(2, j) * a[2] for j in range(3)]
+
+    def apply(self, v, e, e2, sides):
+        row_zero, sec_zero = self.bits
+        outs = ([None] * 6, [None] * 6)
+        for half in range(2):
+            span = slice(3 * half, 3 * half + 3)
+            sets = (v[span], e[span])
+            beyond = e2[span]
+            pairs = [self.row_pairs(*z) for z in zip(v[span], e[span], beyond)]
+            t_row = [self.transposed(functools.partial(self.c, side, 1), sets[side]) for side in range(2)]
+            for side in sides:
+                a = sets[side]
+                after = [self.seconds(a[j], pairs[j][side]) for j in range(3)]
+                total = []
+                for i in range(3):
+                    y = sum(self.d(side, i, j) * a[j] for j in range(3))
+                    for kind in range(4):
+                        y = y - sum(self.c(side, kind, i, j) * after[j][kind] for j in range(3))
+                    total.append(y)
+                col = self.transposed(functools.partial(self.c, side, 0), a)
+                one = self.transposed(functools.partial(self.c, side, 2), a)
+                two = self.transposed(functools.partial(self.c, side, 3), a)
+                if side == 1:
+                    outer = self.transposed(self.c_e2, beyond)
+                for j in range(3):
+                    t = roll(one[j], 64, 1)
+                    y = total[j] - roll(col[j], 1, 1) - jnp.where(sec_zero, from_below(t), t) - from_below(two[j])
+                    if side == 0:
+                        y = y - jnp.where(row_zero, roll(t_row[1][j], -32, 1), roll(t_row[0][j], 32, 1))
+                    else:
+                        y = y - jnp.where(row_zero, roll(t_row[0][j], -32, 1), roll(outer[j], 32, 1))
+                    outs[side][3 * half + j] = y
+        return outs
+
+
+def window_kernel(got, blocks, v0, e0, v1, e1, v2):
+    n_dev = got.shape[0] // (2 * DOUBLE)
     row_zero, sec_zero = lane_bits((2 * n_dev, 128))
     zero = jnp.zeros((2 * n_dev, 128), jnp.float32)
-    C = {(k, i): row(AT_C + 9 * k + i) for k in range(4) for i in range(9)}
-    for (k, i), value in C.items():
-        blocks[6 + 9 * k + i] = value
-    for i in range(9):
-        blocks[42 + i] = row(AT_LOW + i)
+
+    def row(i):
+        return jnp.concatenate(
+            [got[pl.ds(slot * DOUBLE + i, n_dev, stride=2 * DOUBLE), :] for slot in range(2)], axis=0
+        )
 
     def pushed(kind, value):
         if kind == 2:
             return from_below(jnp.where(sec_zero, roll(value, 64, 1), zero))
         return from_below(value)
 
-    D = [row(i) for i in range(6)]
-    S = [row(6 + i) for i in range(6)]
-    for kind in (2, 3):
-        base = AT_SEND + 9 * (kind - 2)
-        G = [row(base), row(base + 1), C[kind, 6], row(base + 2), C[kind, 7], C[kind, 8]]
-        D = [a + pushed(kind, b) for a, b in zip(D, G)]
-        S = [a - pushed(kind, row(base + 3 + i)) for i, a in enumerate(S)]
+    starts = []
+    for side, at in enumerate((0, AT_E)):
+        for i in range(36):
+            blocks[side * 42 + 6 + i] = row(at + AT_C + i)
+        D = [row(at + i) for i in range(6)]
+        S = [row(at + 6 + i) for i in range(6)]
+        for kind in (2, 3):
+            base = at + AT_SEND + 9 * (kind - 2)
+            last = [blocks[side * 42 + 6 + 9 * kind + i] for i in (6, 7, 8)]
+            G = [row(base), row(base + 1), last[0], row(base + 2), last[1], last[2]]
+            D = [a + pushed(kind, b) for a, b in zip(D, G)]
+            S = [a - pushed(kind, row(base + 3 + i)) for i, a in enumerate(S)]
+        for i in range(6):
+            blocks[side * 42 + i] = D[i]
+        starts.append(S)
+    for i in range(9):
+        blocks[84 + i] = row(AT_E2 + i)
+    outer = [
+        row(AT_E2 + 9 + i) - pushed(2, row(AT_E2 + 15 + i)) - pushed(3, row(AT_E2 + 21 + i)) for i in range(6)
+    ]
+    window = Window(lambda i: blocks[i], n_dev)
+    v, e = starts
+    w, f = window.apply(v, e, outer, (0, 1))
+    last, _ = window.apply(w, f, f, (0,))
     for i in range(6):
-        blocks[i] = D[i]
-        start[i] = S[i]
-
-
-def apply_kernel(blocks, v_ref, next_ref, low_ref, out):
-    shape = v_ref.shape[1:]
+        v0[i] = v[i]
+        e0[i] = e[i]
+        v1[i] = w[i]
+        e1[i] = f[i]
+        v2[i] = last[i]
+
+
+def moments_kernel(blocks, v0, v1, v2, above, below, e2, v3, e3, out):
+    shape = v2.shape[1:]
+    n_dev = shape[0] // 2
     bits = lane_bits(shape)
-    row_zero, sec_zero = bits
-    v = [v_ref[i] for i in range(6)]
-    after = [seconds_of(v[i], next_ref[i], bits) for i in range(6)]
-    total = [None] * 6
-    for half in range(2):
-        a = v[3 * half : 3 * half + 3]
-        for i in range(3):
-            total[3 * half + i] = sum(blocks[sym_at(i, j)] * a[j] for j in range(3))
-    for kind in range(4):
-        C = [[blocks[6 + 9 * kind + 3 * i + j] for j in range(3)] for i in range(3)]
-        for half in range(2):
-            a = v[3 * half : 3 * half + 3]
-            b = [after[3 * half + j][kind] for j in range(3)]
-            for i in range(3):
-                total[3 * half + i] -= C[i][0] * b[0] + C[i][1] * b[1] + C[i][2] * b[2]
-            for j in range(3):
-                t = C[0][j] * a[0] + C[1][j] * a[1] + C[2][j] * a[2]
-                if kind == 0:
-                    t = roll(t, 1, 1)
-                elif kind == 1:
-                    low = [low_ref[3 * half + i] for i in range(3)]
-                    t_low = sum(blocks[42 + 3 * i + j] * low[i] for i in range(3))
-                    t = jnp.where(row_zero, roll(t_low, -32, 1), roll(t, 32, 1))
-                elif kind == 2:
-                    t = roll(t, 64, 1)
-                    t = jnp.where(sec_zero, from_below(t), t)
-                else:
-                    t = from_below(t)
-                total[3 * half + j] -= t
+    row_zero, _ = bits
+    window = Window(lambda i: blocks[i], n_dev)
+    v = [v2[i] for i in range(6)]
+    side = [jnp.where(row_zero, above[i], below[i]) for i in range(6)]
+    outer = [jnp.where(row_zero, below[i], above[i]) for i in range(6)]
+    w, f = window.apply(v, side, outer, (0, 1))
     for i in range(6):
-        out[i] = total[i]
-
-
-def moments_kernel(blocks, v0, v1, v2, v3, next_ref, out):
-    shape = v3.shape[1:]
-    bits = lane_bits(shape)
-    quarter = shape[0] // 4
-    dev = lax.broadcasted_iota(jnp.int32, shape, 0)
-    inside = jnp.logical_and(dev >= quarter, dev < 3 * quarter)
-    vs = [[ref[i] for i in range(6)] for ref in (v0, v1, v2, v3)]
+        e2[i] = side[i]
+        v3[i] = w[i]
+        e3[i] = f[i]
+    vs = [[v0[i] for i in range(6)], [v1[i] for i in range(6)], v, w]
 
     def dot(left, right):
-        return sum(a * b for a, b in zip(left, right))
+        return sum(a[:n_dev] * b[:n_dev] for a, b in zip(left, right))
 
     products = [dot(vs[n // 2], vs[n - n // 2]) for n in range(7)]
     energy = 0.0
-    after = [seconds_of(vs[3][i], next_ref[i], bits) for i in range(6)]
     for half in range(2):
-        a = vs[3][3 * half : 3 * half + 3]
+        a = w[3 * half : 3 * half + 3]
+        b = f[3 * half : 3 * half + 3]
+        after = [window.seconds(a[j], jnp.where(row_zero, roll(a[j], -32, 1), roll(b[j], 32, 1))) for j in range(3)]
         for i in range(3):
-            inner = sum(blocks[sym_at(i, j)] * a[j] for j in range(3))
+            inner = sum(window.d(0, i, j) * a[j] for j in range(3))
             for kind in range(4):
-                cross = sum(blocks[6 + 9 * kind + 3 * i + j] * after[3 * half + j][kind] for j in range(3))
-                inner = inner - 2.0 * cross
-            energy = energy + a[i] * inner
+                inner = inner - 2.0 * sum(window.c(0, kind, i, j) * after[j][kind] for j in range(3))
+            energy = energy + a[i][:n_dev] * inner[:n_dev]
     products.append(energy)
     lane = lax.broadcasted_iota(jnp.int32, (1, 128), 1)
     packed = jnp.zeros((1, 128), jnp.float32)
     for n, value in enumerate(products):
-        value = jnp.where(inside, value, 0.0)
         value = jnp.sum(jnp.sum(value, axis=0, keepdims=True), axis=1, keepdims=True)
         packed = jnp.where(lane == n, value, packed)
     out[...] = packed
@@ -322,7 +409,7 @@
     lane = lax.broadcasted_iota(jnp.int32, (1, 128), 1)
     moments = [jnp.sum(jnp.where(lane == n, total, 0.0), axis=1, keepdims=True) for n in range(8)]
     weights = coefficients(moments)
-    at = place[0]
+    at = place[2]
     row_zero, sec_zero = lane_bits((1, 128))
 
     def mix(refs, i, dev):
@@ -333,7 +420,10 @@
     above = [mix(vs, i, at + 1) for i in range(6)]
     beside = [mix((n0, n1, n2, n3), i, at) for i in range(6)]
     for i in range(6):
-        affines[i : i + 1, :] = x[i]
+        for sec in range(2):
+            for row in range(2):
+                start = 64 * sec + 32 * row
+                affines[i, sec, row : row + 1, :] = x[i][:, start : start + 32]
     for kind in range(4):
         if kind == 0:
             b = [roll(z, -1, 1) for z in x]
@@ -355,12 +445,26 @@
     return jax.ShapeDtypeStruct(shape, jnp.float32)
 
 
-def call(kernel, outs, *args, scalars=0, interpret=False):
+def call(interpret, kernel, outs, *args, scalars=0, anywhere=0, copies=0, results="vmem"):
     spaces = [pl.BlockSpec(memory_space=pltpu.SMEM)] * scalars
-    spaces += [pl.BlockSpec(memory_space=pltpu.VMEM)] * (len(args) - scalars)
-    many = isinstance(outs, (list, tuple))
-    out_specs = [pl.BlockSpec(memory_space=pltpu.VMEM) for _ in outs] if many else pl.BlockSpec(memory_space=pltpu.VMEM)
-    return pl.pallas_call(kernel, out_shape=outs, in_specs=spaces, out_specs=out_specs, interpret=interpret)(*args)
+    spaces += [pl.BlockSpec(memory_space=pl.ANY)] * anywhere
+    spaces += [pl.BlockSpec(memory_space=pltpu.VMEM)] * (len(args) - scalars - anywhere)
+    args = list(args)
+    shapes = [shape_of(*out) for out in outs]
+    if not interpret:
+        for n in range(scalars + anywhere, len(args)):
+            if args[n].dtype == jnp.float32:
+                args[n] = pltpu.with_memory_space_constraint(args[n], pltpu.VMEM)
+        if results == "vmem":
+            shapes = [pltpu.VMEM(out, jnp.float32) for out in outs]
+    return pl.pallas_call(
+        kernel,
+        out_shape=shapes,
+        in_specs=spaces,
+        out_specs=[pl.BlockSpec(memory_space=pltpu.VMEM) for _ in outs],
+        scratch_shapes=[pltpu.SemaphoreType.DMA((copies,))] if copies else [],
+        interpret=interpret,
+    )(*args)
 
 
 def shifted(value, axes, steps):
@@ -369,30 +473,35 @@
     return lax.ppermute(value, axes, pairs)
 
 
+def pack_up(run, g):
+    return run(pack_up_kernel, [(384, 128)], g, anywhere=1, copies=2)[0]
+
+
+def pack_rows(run, f, g, counts):
+    return run(pack_rows_kernel, [(128, 128), (136, 128)], f, g, counts, anywhere=2, copies=4)
+
+
 def per_device(interpret, first_pts, second_pts, counts):
-    run = functools.partial(call, interpret=interpret)
+    run = functools.partial(call, interpret)
     n_sec = lax.axis_size(SEC_AXES)
     n_dev = lax.axis_size(GROUP)
     n_group = n_sec // n_dev
     sec = lax.axis_index(SEC_AXES)
-    member = lax.axis_index(GROUP)
     f = first_pts.reshape(1024, 128)
     g = second_pts.reshape(1024, 128)
-    lives = counts.reshape(4, 128)
-
-    up = shifted(jnp.concatenate([g[512:640], g[768:1024]], axis=0), SEC_AXES, -1)
-    beside = shifted(jnp.concatenate([g[256:320], g[384:448]], axis=0), "row", -1)
-    odd = jnp.concatenate(
-        [f[320:384], f[448:512], jnp.broadcast_to(lives[1:2].astype(jnp.float32), (8, 128))], axis=0
-    )
-    low = shifted(odd, "row", 1)
     flags = jnp.stack(
         [
             (lax.axis_index("row") == lax.axis_size("row") - 1).astype(jnp.int32),
             (sec == n_sec - 1).astype(jnp.int32),
+            lax.axis_index(GROUP).astype(jnp.int32),
         ]
     )
-    packet, kept = run(gram_kernel, [shape_of(ROWS, 128), shape_of(20, 128, 128)], flags, f, g, lives, up, beside, low, scalars=1)
+
+    up = shifted(pack_up(run, g), SEC_AXES, -1)
+    beside, odd = pack_rows(run, f, g, counts)
+    beside = shifted(beside, "row", -1)
+    low = shifted(odd, "row", 1)
+    packet, kept = run(gram_kernel, [(ROWS, 128), (20, 128, 128)], flags, f, g, counts, up, beside, low, scalars=1)
 
     half = n_dev // 2
     pairs = []
@@ -402,34 +511,43 @@
             if 0 <= source < n_group:
                 pairs.append((source * n_dev + dev, group * n_dev + dev))
     other = lax.ppermute(packet, SEC_AXES, pairs)
-    mine = jnp.concatenate([packet, other], axis=0)
-    got = lax.all_to_all(jnp.broadcast_to(mine[None], (n_dev, 2 * ROWS, 128)), GROUP, 0, 0, tiled=False)
-    blocks, v0 = run(
-        window_kernel, [shape_of(51, 2 * n_dev, 128), shape_of(6, 2 * n_dev, 128)], got.reshape(n_dev * 2 * ROWS, 128)
+    both = jnp.concatenate([packet, other], axis=0)
+    (mine,) = run(merge_kernel, [(2 * DOUBLE, 128)], both, shifted(both, "row", -1), shifted(both, "row", 1))
+    got = lax.all_to_all(jnp.broadcast_to(mine[None], (n_dev, 2 * DOUBLE, 128)), GROUP, 0, 0, tiled=False)
+    wide = (6, 2 * n_dev, 128)
+    blocks, v0, e0, v1, e1, v2 = run(
+        window_kernel, [(93, 2 * n_dev, 128)] + [wide] * 5, got.reshape(n_dev * 2 * DOUBLE, 128)
     )
-    vs = [v0]
-    nexts = []
-    for step in range(ITERS - 1):
-        v = vs[-1]
-        nexts.append(shifted(v, "row", -1))
-        lows = shifted(v, "row", 1)
-        vs.append(run(apply_kernel, shape_of(*v.shape), blocks, v, nexts[-1], lows))
-    nexts.append(shifted(vs[-1], "row", -1))
-    part = run(moments_kernel, shape_of(1, 128), blocks, *vs, nexts[-1])
+    e2, v3, e3, part = run(
+        moments_kernel,
+        [wide, wide, wide, (1, 128)],
+        blocks,
+        v0,
+        v1,
+        v2,
+        shifted(v2, "row", -1),
+        shifted(v2, "row", 1),
+    )
     n_other = lax.axis_size(OTHERS)
     sums = lax.all_to_all(jnp.broadcast_to(part[None], (n_other, 1, 128)), OTHERS, 0, 0, tiled=False)
-    place = (member + n_dev // 2).astype(jnp.int32).reshape(1)
     affines, residual = run(
         finish_kernel,
-        [shape_of(6, 128), shape_of(1024, 128)],
-        place,
+        [(6,) + counts.shape[1:], (1024, 128)],
+        flags,
         sums.reshape(n_other, 128),
-        *vs,
-        *nexts,
+        v0,
+        v1,
+        v2,
+        v3,
+        e0,
+        e1,
+        e2,
+        e3,
         kept,
         scalars=1,
+        results="hbm",
     )
-    return affines.reshape((6,) + counts.shape[1:]), residual.reshape(first_pts.shape)
+    return affines, residual.reshape(first_pts.shape)
 
 
 def split_mesh(mesh):

time: 189 us -> 151 us (0.80)
  blocking collectives: 15.6 us -> 63.7 us
  starting transfers between devices: 91.4 us -> 43.8 us
  waiting for transfers between devices: 49.9 us -> 30.9 us
  local copies, waits for them, and re-layouts: 11.2 us -> 1.47 us
  Pallas kernels: 15.2 us -> 7.68 us
    all_to_all x1 -> x2, blocking collectives: 15.6 us -> 63.7 us  [the longest x1 42.3 us: per_device(): lax.all_to_all(jnp.broadcast_to(part[None], (n_other, 1, 128)), OTHERS, 0...]
    all_to_all x1 -> x0, starting transfers between devices: 28.4 us -> none  [per_device(): lax.all_to_all(jnp.broadcast_to(part[None], (n_other, 1, 128)), OTHERS, 0...]
    all_to_all x1 -> x0, waiting for transfers between devices: 23.3 us -> none  [per_device(): lax.all_to_all(jnp.broadcast_to(part[None], (n_other, 1, 128)), OTHERS, 0...]
    ppermute x10 -> x7, starting transfers between devices: 54.6 us -> 36.6 us  [shifted(): return lax.ppermute(value, axes, pairs)]
    pallas_call x7, Pallas kernels: 15.2 us -> 7.68 us  [call(): pl.pallas_call(kernel, out_shape=shapes, in_specs=spaces, out_specs=[pl.B...]
    ppermute x10 -> x7, waiting for transfers between devices: 20.2 us -> 23.6 us  [shifted(): return lax.ppermute(value, axes, pairs)]
    slice x4 -> x0, local copies, waits for them, and re-layouts: 3.33 us -> none  [the longest x1 0.91 us: per_device(): g[768:1024]]
    unnamed x24 -> x9, local copies, waits for them, and re-layouts: 4.39 us -> 1.34 us
  transfers between devices with their start and end apart: 12 -> 8, of which waited for: 10 -> 6; matrix products, arithmetic and copies ran while one was open for 2% -> 0% of each run, Pallas kernels for 0% -> 1%
where the time goes in v2:
time: 151 us; the launch traced here: 149 us
  blocking collectives  63.7 us (42%)
  starting transfers between devices  43.8 us (29%)
  waiting for transfers between devices  30.9 us (20%)
  Pallas kernels  7.68 us (5%)
    all_to_all x1, blocking collectives, per_device(): lax.all_to_all(jnp.broadcast_to(part[None], (n_other, 1, 128)), OTHERS, 0...  42.3 us
    ppermute x7, starting transfers between devices, shifted(): return lax.ppermute(value, axes, pairs)  36.6 us
    ppermute x7, waiting for transfers between devices, shifted(): return lax.ppermute(value, axes, pairs)  23.6 us
    all_to_all x1, blocking collectives, per_device(): lax.all_to_all(jnp.broadcast_to(mine[None], (n_dev, 2 * DOUBLE, 128)), GR...  21.4 us
    pallas_call x7, Pallas kernels, call(): pl.pallas_call(kernel, out_shape=shapes, in_specs=spaces, out_specs=[pl.B...  7.68 us
    ppermute x1, waiting for transfers between devices, per_device(): other = lax.ppermute(packet, SEC_AXES, pairs)  7.36 us
    ppermute x1, starting transfers between devices, per_device(): other = lax.ppermute(packet, SEC_AXES, pairs)  7.18 us
  transfers between devices with their start and end apart: 8, of which 6 were waited for; matrix products, arithmetic and copies ran while one was open for 0% of the time, Pallas kernels for 1%

profile of v2, /device:TPU:24, one launch (start us, length us, event | category | flops | bytes accessed | tf_op | source)
XLA Modules:
  0.0 149.0 jit_solution(13415797166255906952)
XLA Ops:
  0.7 1.0 shard_map.50
  1.7 24.8 %collective-permute-start = (f32[384,128]{1,0:T(8,128)S(1)}, f32[384,128]{1,0:T(8,128)S(1)}, u32[]{:S(2)}, u32[]{:S(2)}) collective-permute-start(f32[384,128]{1,0:T(8,128)S(1)} %shard_map.50), channel_id=1, source_target_pairs={{8,0},{16,8},{24,16},{32,24},{40,32},{48,40},{56,48},{64,56},{72,6... | collective-permute-start | bytes 589832 | tf_op jit(solution)/shard_map/ppermute | solution.py:473
  26.5 1.5 %shard_map.51 = (f32[128,128]{1,0:T(8,128)S(1)}, f32[136,128]{1,0:T(8,128)S(1)}) custom-call(f32[1024,128]{1,0:T(8,128)} %bitcast.13, f32[1024,128]{1,0:T(8,128)} %bitcast.11, s32[4,2,2,32]{3,2,1,0:T(2,128)} %counts_ref.3), custom_call_target="tpu_custom_call" | custom-call | tf_op jit(solution)/shard_map/pallas_call | solution.py:460
  28.1 1.3 collective-permute-start.1
  29.4 4.5 %collective-permute-start.2 = (f32[136,128]{1,0:T(8,128)S(1)}, f32[136,128]{1,0:T(8,128)S(1)}, u32[]{:S(2)}, u32[]{:S(2)}) collective-permute-start(f32[136,128]{1,0:T(8,128)S(1)} %get-tuple-element.19), channel_id=1, source_target_pairs={{0,1},{1,2},{2,3},{3,4},{4,5},{5,6},{6,7},{8,9},{9,10},{10,11},{11... | collective-permute-start | bytes 208904 | tf_op jit(solution)/shard_map/ppermute | solution.py:473
  33.9 0.7 pad_add_fusion.flags.place
  34.6 13.9 %collective-permute-done.1.next_ref = f32[128,128]{1,0:T(8,128)S(1)} collective-permute-done((f32[128,128]{1,0:T(8,128)S(1)}, f32[128,128]{1,0:T(8,128)S(1)}, u32[]{:S(2)}, u32[]{:S(2)}) %collective-permute-start.1) | collective-permute-done | bytes 65568 | tf_op jit(solution)/shard_map/ppermute | solution.py:473
  48.6 1.5 %shard_map.52 = (f32[72,128]{1,0:T(8,128)S(1)}, f32[20,128,128]{2,1,0:T(8,128)S(1)}) custom-call(s32[3]{0:T(128)} %pad_add_fusion.flags.place, f32[1024,128]{1,0:T(8,128)S(1)} %bitcast.14, f32[1024,128]{1,0:T(8,128)S(1)} %bitcast.12, s32[4,2,2,32]{3,2,1,0:T(2,128)} %counts_ref.3, f32[384,128]{1,0:T(8,128)S(1)} %collective-permute-done.up_ref, ...), custom_call_target="tpu_custom_call" | custom-call | tf_op jit(solution)/shard_map/pallas_call | solution.py:460
  50.1 7.2 %collective-permute-start.3 = (f32[72,128]{1,0:T(8,128)S(1)}, f32[72,128]{1,0:T(8,128)S(1)}, u32[]{:S(2)}, u32[]{:S(2)}) collective-permute-start(f32[72,128]{1,0:T(8,128)S(1)} %get-tuple-element.20), channel_id=1, source_target_pairs={{64,0},{72,8},{80,16},{88,24},{128,64},{136,72},{144,80},{152,88},... | collective-permute-start | bytes 110600 | tf_op jit(solution)/shard_map/ppermute | solution.py:513
  57.3 7.4 %collective-permute-done.3 = f32[72,128]{1,0:T(8,128)S(1)} collective-permute-done((f32[72,128]{1,0:T(8,128)S(1)}, f32[72,128]{1,0:T(8,128)S(1)}, u32[]{:S(2)}, u32[]{:S(2)}) %collective-permute-start.3) | collective-permute-done | bytes 36896 | tf_op jit(solution)/shard_map/ppermute | solution.py:513
  64.7 1.4 collective-permute-start.5
  66.1 1.3 collective-permute-start.4
  67.4 0.7 collective-permute-done.5.below
  68.1 4.3 %collective-permute-done.4.above = f32[144,128]{1,0:T(8,128)S(1)} collective-permute-done((f32[144,128]{1,0:T(8,128)S(1)}, f32[144,128]{1,0:T(8,128)S(1)}, u32[]{:S(2)}, u32[]{:S(2)}) %collective-permute-start.4) | collective-permute-done | bytes 73760 | tf_op jit(solution)/shard_map/ppermute | solution.py:473
  72.5 21.4 %all_to_all.10 = f32[8,320,128]{2,1,0:T(8,128)S(1)} all-to-all(f32[8,320,128]{2,1,0:T(8,128)S(1)} %broadcast_in_dim.6), channel_id=1, replica_groups=mesh['y'=4,'zhi'=4,'x'=4,'core'=2,'row'=8] {'x','core'}, dimensions={0} | all-to-all | bytes 2621440 | tf_op jit(solution)/shard_map/all_to_all | solution.py:516
  93.9 1.1 shard_map.54
  95.0 1.9 %collective-permute-start.7 = (f32[6,16,128]{2,1,0:T(8,128)S(1)}, f32[6,16,128]{2,1,0:T(8,128)S(1)}, u32[]{:S(2)}, u32[]{:S(2)}) collective-permute-start(f32[6,16,128]{2,1,0:T(8,128)S(1)} %get-tuple-element.24.v2), channel_id=1, source_target_pairs={{0,1},{1,2},{2,3},{3,4},{4,5},{5,6},{6,7},{8,9},{9,10},{10,11},{11... | collective-permute-start | bytes 147464 | tf_op jit(solution)/shard_map/ppermute | solution.py:473
  96.9 1.3 collective-permute-start.6
  98.2 0.4 collective-permute-done.7.below
  98.6 4.3 %collective-permute-done.6.above = f32[6,16,128]{2,1,0:T(8,128)S(1)} collective-permute-done((f32[6,16,128]{2,1,0:T(8,128)S(1)}, f32[6,16,128]{2,1,0:T(8,128)S(1)}, u32[]{:S(2)}, u32[]{:S(2)}) %collective-permute-start.6) | collective-permute-done | bytes 49184 | tf_op jit(solution)/shard_map/ppermute | solution.py:473
  102.9 0.4 shard_map.55
  103.4 42.3 %all_to_all.11 = f32[128,1,128]{2,1,0:T(1,128)S(1)} all-to-all(f32[128,1,128]{2,1,0:T(1,128)S(1)} %broadcast_in_dim.16), channel_id=1, replica_groups=mesh['y'=4,'zhi'=4,'x'=4,'core'=2,'row'=8] {'y','zhi','row'}, dimensions={0} | all-to-all | bytes 131072 | tf_op jit(solution)/shard_map/all_to_all | solution.py:532
  145.7 1.3 copy-done.3
  147.0 2.0 %shard_map.56 = (f32[6,2,2,32]{3,2,1,0:T(2,128)}, f32[1024,128]{1,0:T(8,128)}) custom-call(s32[3]{0:T(128)} %pad_add_fusion.flags.place, f32[128,128]{1,0:T(8,128)S(1)} %bitcast.15, f32[6,16,128]{2,1,0:T(8,128)S(1)} %get-tuple-element.22.v0, f32[6,16,128]{2,1,0:T(8,128)S(1)} %get-tuple-element.23.v1, f32[6,16,128]{2,1,0:T(8,128)S(1)} %get-tuple-element.24.v2, ...), custom_call_target="tpu_custom_call" | custom-call | tf_op jit(solution)/shard_map/pallas_call | solution.py:460
  (14 shorter events, 0.2 us)
Async XLA Ops:
  0.6 47.9 %copy-start = (f32[4,2,2,32,2,128]{5,4,3,2,1,0:T(2,128)S(1)}, f32[4,2,2,32,2,128]{5,4,3,2,1,0:T(2,128)}, u32[]{:S(2)}) copy-start(f32[4,2,2,32,2,128]{5,4,3,2,1,0:T(2,128)} %param.4) | copy-start | bytes 1572868
  0.6 47.9 %copy-start.1 = (f32[4,2,2,32,2,128]{5,4,3,2,1,0:T(2,128)S(1)}, f32[4,2,2,32,2,128]{5,4,3,2,1,0:T(2,128)}, u32[]{:S(2)}) copy-start(f32[4,2,2,32,2,128]{5,4,3,2,1,0:T(2,128)} %param.3) | copy-start | bytes 1572868
  1.7 46.8 %collective-permute-start = (f32[384,128]{1,0:T(8,128)S(1)}, f32[384,128]{1,0:T(8,128)S(1)}, u32[]{:S(2)}, u32[]{:S(2)}) collective-permute-start(f32[384,128]{1,0:T(8,128)S(1)} %shard_map.50), channel_id=1, source_target_pairs={{8,0},{16,8},{24,16},{32,24},{40,32},{48,40},{56,48},{64,56},{72,6... | collective-permute-start | bytes 589832 | tf_op jit(solution)/shard_map/ppermute | solution.py:473
  28.1 20.5 %collective-permute-start.1 = (f32[128,128]{1,0:T(8,128)S(1)}, f32[128,128]{1,0:T(8,128)S(1)}, u32[]{:S(2)}, u32[]{:S(2)}) collective-permute-start(f32[128,128]{1,0:T(8,128)S(1)} %get-tuple-element.18), channel_id=1, source_target_pairs={{1,0},{2,1},{3,2},{4,3},{5,4},{6,5},{7,6},{9,8},{10,9},{11,10},{12... | collective-permute-start | bytes 196616 | tf_op jit(solution)/shard_map/ppermute | solution.py:473
  29.4 19.2 %collective-permute-start.2 = (f32[136,128]{1,0:T(8,128)S(1)}, f32[136,128]{1,0:T(8,128)S(1)}, u32[]{:S(2)}, u32[]{:S(2)}) collective-permute-start(f32[136,128]{1,0:T(8,128)S(1)} %get-tuple-element.19), channel_id=1, source_target_pairs={{0,1},{1,2},{2,3},{3,4},{4,5},{5,6},{6,7},{8,9},{9,10},{10,11},{11... | collective-permute-start | bytes 208904 | tf_op jit(solution)/shard_map/ppermute | solution.py:473
  50.1 43.8 %copy-start.2 = (f32[20,128,128]{2,1,0:T(8,128)}, f32[20,128,128]{2,1,0:T(8,128)S(1)}, u32[]{:S(2)}) copy-start(f32[20,128,128]{2,1,0:T(8,128)S(1)} %get-tuple-element.31.kept) | copy-start | bytes 3932164
  50.1 14.6 %collective-permute-start.3 = (f32[72,128]{1,0:T(8,128)S(1)}, f32[72,128]{1,0:T(8,128)S(1)}, u32[]{:S(2)}, u32[]{:S(2)}) collective-permute-start(f32[72,128]{1,0:T(8,128)S(1)} %get-tuple-element.20), channel_id=1, source_target_pairs={{64,0},{72,8},{80,16},{88,24},{128,64},{136,72},{144,80},{152,88},... | collective-permute-start | bytes 110600 | tf_op jit(solution)/shard_map/ppermute | solution.py:513
  64.7 3.4 %collective-permute-start.5 = (f32[144,128]{1,0:T(8,128)S(1)}, f32[144,128]{1,0:T(8,128)S(1)}, u32[]{:S(2)}, u32[]{:S(2)}) collective-permute-start(f32[144,128]{1,0:T(8,128)S(1)} %constant_dynamic-update-slice_fusion.both), channel_id=1, source_target_pairs={{0,1},{1,2},{2,3},{3,4},{4,5},{5,6},{6,7},{8,9},{9,10},{10,11},{11... | collective-permute-start | bytes 221192 | tf_op jit(solution)/shard_map/ppermute | solution.py:473
  66.1 6.2 %collective-permute-start.4 = (f32[144,128]{1,0:T(8,128)S(1)}, f32[144,128]{1,0:T(8,128)S(1)}, u32[]{:S(2)}, u32[]{:S(2)}) collective-permute-start(f32[144,128]{1,0:T(8,128)S(1)} %constant_dynamic-update-slice_fusion.both), channel_id=1, source_target_pairs={{1,0},{2,1},{3,2},{4,3},{5,4},{6,5},{7,6},{9,8},{10,9},{11,10},{12... | collective-permute-start | bytes 221192 | tf_op jit(solution)/shard_map/ppermute | solution.py:473
  95.0 3.7 %collective-permute-start.7 = (f32[6,16,128]{2,1,0:T(8,128)S(1)}, f32[6,16,128]{2,1,0:T(8,128)S(1)}, u32[]{:S(2)}, u32[]{:S(2)}) collective-permute-start(f32[6,16,128]{2,1,0:T(8,128)S(1)} %get-tuple-element.24.v2), channel_id=1, source_target_pairs={{0,1},{1,2},{2,3},{3,4},{4,5},{5,6},{6,7},{8,9},{9,10},{10,11},{11... | collective-permute-start | bytes 147464 | tf_op jit(solution)/shard_map/ppermute | solution.py:473
  96.9 6.0 %collective-permute-start.6 = (f32[6,16,128]{2,1,0:T(8,128)S(1)}, f32[6,16,128]{2,1,0:T(8,128)S(1)}, u32[]{:S(2)}, u32[]{:S(2)}) collective-permute-start(f32[6,16,128]{2,1,0:T(8,128)S(1)} %get-tuple-element.24.v2), channel_id=1, source_target_pairs={{1,0},{2,1},{3,2},{4,3},{5,4},{6,5},{7,6},{9,8},{10,9},{11,10},{12... | collective-permute-start | bytes 147464 | tf_op jit(solution)/shard_map/ppermute | solution.py:473
  145.7 1.3 copy-start.3

commit v3 on v2

--- a/solution.py
+++ b/solution.py
@@ -67,7 +67,7 @@
     return F, G, C, s1, s2
 
 
-def gram_kernel(flags, f_ref, g_ref, counts_ref, up_ref, next_ref, low_ref, packet, kept):
+def gram_kernel(flags, f_ref, g_ref, counts_ref, up_ref, rest_ref, outside_ref, next_ref, low_ref, packet, kept):
     row_zero, sec_zero = lane_bits((1, 128))
     lane = lax.broadcasted_iota(jnp.int32, (1, 128), 1)
     last_row = flags[0] == 1
@@ -108,7 +108,8 @@
             elif kind == 2:
                 parts = [pair_rows(g_ref, 256 + 64, 64, comp), pair_rows(up_ref, 0, 64, comp)]
             else:
-                parts = [pair_rows(up_ref, 64, 128, comp)]
+                rest = pair_rows(rest_ref, 0, 96, comp) + pair_rows(outside_ref, 0, 96, comp)
+                parts = [pair_rows(up_ref, 64, 32, comp), rest]
             out.append(jnp.concatenate(parts, axis=0).T)
         return out
 
@@ -179,10 +180,11 @@
     return roll(value, 1, 0)
 
 
-def pack_up_kernel(g_ref, up, sems):
+def pack_up_kernel(g_ref, up, rest, sems):
     copies = [
         pltpu.make_async_copy(g_ref.at[pl.ds(512, 128)], up.at[pl.ds(0, 128)], sems.at[0]),
-        pltpu.make_async_copy(g_ref.at[pl.ds(768, 256)], up.at[pl.ds(128, 256)], sems.at[1]),
+        pltpu.make_async_copy(g_ref.at[pl.ds(768, 64)], up.at[pl.ds(128, 64)], sems.at[1]),
+        pltpu.make_async_copy(g_ref.at[pl.ds(832, 192)], rest, sems.at[2]),
     ]
     for copy in copies:
         copy.start()
@@ -404,7 +406,14 @@
     return [value * (1.0 / SPAN) for value in x]
 
 
-def finish_kernel(place, sums, v0, v1, v2, v3, n0, n1, n2, n3, kept, affines, residual):
+def finish_kernel(place, sums, v0, v1, v2, v3, n0, n1, n2, n3, kept_hbm, affines, residual_hbm, kept, residual, sems):
+    fetches = [
+        pltpu.make_async_copy(kept_hbm.at[pl.ds(5 * kind, 5)], kept.at[pl.ds(5 * kind, 5)], sems.at[kind])
+        for kind in range(4)
+    ]
+    for fetch in fetches:
+        fetch.start()
+    stores = []
     total = jnp.sum(sums[...], axis=0, keepdims=True)
     lane = lax.broadcasted_iota(jnp.int32, (1, 128), 1)
     moments = [jnp.sum(jnp.where(lane == n, total, 0.0), axis=1, keepdims=True) for n in range(8)]
@@ -433,36 +442,47 @@
             b = [jnp.where(sec_zero, roll(z, 64, 1), roll(w, 64, 1)) for z, w in zip(x, above)]
         else:
             b = above
+        fetches[kind].wait()
         u, v, p, q, live = (kept[5 * kind + i] for i in range(5))
         for comp in range(2):
             o = 3 * comp
             r = (p - u) if comp == 0 else (q - v)
             r = r - (x[o] * u + x[o + 1] * v) + (b[o] * p + b[o + 1] * q) - live * (x[o + 2] - b[o + 2])
             residual[pl.ds(kind * 256 + comp, 128, stride=2), :] = r.T
+        part = pl.ds(kind * 256, 256)
+        stores.append(pltpu.make_async_copy(residual.at[part], residual_hbm.at[part], sems.at[4 + kind]))
+        stores[-1].start()
+    for store in stores:
+        store.wait()
 
 
 def shape_of(*shape):
     return jax.ShapeDtypeStruct(shape, jnp.float32)
 
 
-def call(interpret, kernel, outs, *args, scalars=0, anywhere=0, copies=0, results="vmem"):
-    spaces = [pl.BlockSpec(memory_space=pltpu.SMEM)] * scalars
-    spaces += [pl.BlockSpec(memory_space=pl.ANY)] * anywhere
-    spaces += [pl.BlockSpec(memory_space=pltpu.VMEM)] * (len(args) - scalars - anywhere)
+def call(interpret, kernel, outs, *args, scalars=0, anywhere=(), copies=0, buffers=(), results=None):
+    spaces = []
     args = list(args)
     shapes = [shape_of(*out) for out in outs]
-    if not interpret:
-        for n in range(scalars + anywhere, len(args)):
-            if args[n].dtype == jnp.float32:
-                args[n] = pltpu.with_memory_space_constraint(args[n], pltpu.VMEM)
-        if results == "vmem":
-            shapes = [pltpu.VMEM(out, jnp.float32) for out in outs]
+    for n, arg in enumerate(args):
+        if n < scalars:
+            spaces.append(pl.BlockSpec(memory_space=pltpu.SMEM))
+        elif n in anywhere:
+            spaces.append(pl.BlockSpec(memory_space=pl.ANY))
+        else:
+            spaces.append(pl.BlockSpec(memory_space=pltpu.VMEM))
+            if arg.dtype == jnp.float32 and not interpret:
+                args[n] = pltpu.with_memory_space_constraint(arg, pltpu.VMEM)
+    if not results and not interpret:
+        shapes = [pltpu.VMEM(out, jnp.float32) for out in outs]
+    results = results or [pltpu.VMEM] * len(outs)
     return pl.pallas_call(
         kernel,
         out_shape=shapes,
         in_specs=spaces,
-        out_specs=[pl.BlockSpec(memory_space=pltpu.VMEM) for _ in outs],
-        scratch_shapes=[pltpu.SemaphoreType.DMA((copies,))] if copies else [],
+        out_specs=[pl.BlockSpec(memory_space=space) for space in results],
+        scratch_shapes=[pltpu.VMEM(b, jnp.float32) for b in buffers]
+        + ([pltpu.SemaphoreType.DMA((copies,))] if copies else []),
         interpret=interpret,
     )(*args)
 
@@ -474,11 +494,11 @@
 
 
 def pack_up(run, g):
-    return run(pack_up_kernel, [(384, 128)], g, anywhere=1, copies=2)[0]
+    return run(pack_up_kernel, [(192, 128), (192, 128)], g, anywhere=(0,), copies=3)
 
 
 def pack_rows(run, f, g, counts):
-    return run(pack_rows_kernel, [(128, 128), (136, 128)], f, g, counts, anywhere=2, copies=4)
+    return run(pack_rows_kernel, [(128, 128), (136, 128)], f, g, counts, anywhere=(0, 1), copies=4)
 
 
 def per_device(interpret, first_pts, second_pts, counts):
@@ -497,11 +517,20 @@
         ]
     )
 
-    up = shifted(pack_up(run, g), SEC_AXES, -1)
-    beside, odd = pack_rows(run, f, g, counts)
+    up, rest = pack_up(run, g)
+    up = shifted(up, SEC_AXES, -1)
+    relay = n_dev - 2
+    inside = [(i + 1, i) for i in range(n_sec - 1) if (i + 1) % n_dev]
+    to_relay = [(group * n_dev, group * n_dev + relay) for group in range(1, n_group)]
+    from_relay = [(group * n_dev + relay, group * n_dev - 1) for group in range(1, n_group)]
+    relayed = lax.ppermute(rest, SEC_AXES, to_relay)
+    relayed, f_later, g_later = lax.optimization_barrier((relayed, f, g))
+    outside = lax.ppermute(relayed, SEC_AXES, from_relay)
+    beside, odd, rest = lax.optimization_barrier((*pack_rows(run, f_later, g_later, counts), rest))
+    rest = lax.ppermute(rest, SEC_AXES, inside)
     beside = shifted(beside, "row", -1)
     low = shifted(odd, "row", 1)
-    packet, kept = run(gram_kernel, [(ROWS, 128), (20, 128, 128)], flags, f, g, counts, up, beside, low, scalars=1)
+    packet, kept = run(gram_kernel, [(ROWS, 128), (20, 128, 128)], flags, f, g, counts, up, rest, outside, beside, low, scalars=1)
 
     half = n_dev // 2
     pairs = []
@@ -545,7 +574,10 @@
         e3,
         kept,
         scalars=1,
-        results="hbm",
+        anywhere=(10,),
+        copies=8,
+        buffers=[(20, 128, 128), (1024, 128)],
+        results=[pltpu.VMEM, pl.ANY],
     )
     return affines, residual.reshape(first_pts.shape)
 

time: 151 us -> 148 us (0.980)
  waiting for transfers between devices: 30.9 us -> 22.2 us
  starting transfers between devices: 43.8 us -> 50.3 us
  Pallas kernels: 7.68 us -> 9.27 us
    ppermute x7, waiting for transfers between devices: 23.6 us -> 10.4 us  [shifted(): return lax.ppermute(value, axes, pairs)]
    ppermute x0 -> x3, starting transfers between devices: none -> 6.63 us  [the longest x1 4.67 us: per_device(): relayed = lax.ppermute(rest, SEC_AXES, to_relay)]
    ppermute x1, waiting for transfers between devices: 7.36 us -> 11.2 us  [per_device(): other = lax.ppermute(packet, SEC_AXES, pairs)]
    all_to_all x1, blocking collectives: 42.3 us -> 39.9 us  [per_device(): lax.all_to_all(jnp.broadcast_to(part[None], (n_other, 1, 128)), OTHERS, 0...]
    all_to_all x1, blocking collectives: 21.4 us -> 23.1 us  [per_device(): lax.all_to_all(jnp.broadcast_to(mine[None], (n_dev, 2 * DOUBLE, 128)), GR...]
    ppermute x7, starting transfers between devices: 36.6 us -> 35 us  [shifted(): return lax.ppermute(value, axes, pairs)]
    pallas_call x7, Pallas kernels: 7.68 us -> 9.27 us  [call(): pl.pallas_call(kernel, out_shape=shapes, in_specs=spaces, out_specs=[pl.B...]
    ppermute x1, starting transfers between devices: 7.18 us -> 8.72 us  [per_device(): other = lax.ppermute(packet, SEC_AXES, pairs)]
  transfers between devices with their start and end apart: 8 -> 11, of which waited for: 6 -> 7; matrix products, arithmetic and copies ran while one was open for 0% -> 0% of each run, Pallas kernels for 1% -> 1%
where the time goes in v3:
time: 148 us; the launch traced here: 146 us
  blocking collectives  63 us (43%)
  starting transfers between devices  50.3 us (34%)
  waiting for transfers between devices  22.2 us (15%)
  Pallas kernels  9.27 us (6%)
    all_to_all x1, blocking collectives, per_device(): lax.all_to_all(jnp.broadcast_to(part[None], (n_other, 1, 128)), OTHERS, 0...  39.9 us
    ppermute x7, starting transfers between devices, shifted(): return lax.ppermute(value, axes, pairs)  35 us
    all_to_all x1, blocking collectives, per_device(): lax.all_to_all(jnp.broadcast_to(mine[None], (n_dev, 2 * DOUBLE, 128)), GR...  23.1 us
    ppermute x1, waiting for transfers between devices, per_device(): other = lax.ppermute(packet, SEC_AXES, pairs)  11.2 us
    ppermute x7, waiting for transfers between devices, shifted(): return lax.ppermute(value, axes, pairs)  10.4 us
    pallas_call x7, Pallas kernels, call(): pl.pallas_call(kernel, out_shape=shapes, in_specs=spaces, out_specs=[pl.B...  9.27 us
    ppermute x1, starting transfers between devices, per_device(): other = lax.ppermute(packet, SEC_AXES, pairs)  8.72 us
    ppermute x1, starting transfers between devices, per_device(): relayed = lax.ppermute(rest, SEC_AXES, to_relay)  4.67 us
  transfers between devices with their start and end apart: 11, of which 7 were waited for; matrix products, arithmetic and copies ran while one was open for 0% of the time, Pallas kernels for 1%

profile of v3, /device:TPU:24, one launch (start us, length us, event | category | flops | bytes accessed | tf_op | source)
XLA Modules:
  0.0 146.3 jit_solution(7801986360067130852)
XLA Ops:
  0.7 1.1 shard_map.50
  1.7 4.7 %collective-permute-start.1 = (f32[192,128]{1,0:T(8,128)S(1)}, f32[192,128]{1,0:T(8,128)S(1)}, u32[]{:S(2)}, u32[]{:S(2)}) collective-permute-start(f32[192,128]{1,0:T(8,128)S(1)} %get-tuple-element.32), channel_id=1, source_target_pairs={{64,112},{128,176},{192,240},{256,304},{320,368},{384,432},{448,49... | collective-permute-start | bytes 294920 | tf_op jit(solution)/shard_map/ppermute | solution.py:526
  6.4 20.8 %collective-permute-start = (f32[192,128]{1,0:T(8,128)S(1)}, f32[192,128]{1,0:T(8,128)S(1)}, u32[]{:S(2)}, u32[]{:S(2)}) collective-permute-start(f32[192,128]{1,0:T(8,128)S(1)} %get-tuple-element.26), channel_id=1, source_target_pairs={{8,0},{16,8},{24,16},{32,24},{40,32},{48,40},{56,48},{64,56},{72,6... | collective-permute-start | bytes 294920 | tf_op jit(solution)/shard_map/ppermute | solution.py:493
  27.2 0.7 collective-permute-start.3
  27.9 1.5 %shard_map.51 = (f32[128,128]{1,0:T(8,128)S(1)}, f32[136,128]{1,0:T(8,128)S(1)}) custom-call(f32[1024,128]{1,0:T(8,128)} %bitcast.13, f32[1024,128]{1,0:T(8,128)} %bitcast.11, s32[4,2,2,32]{3,2,1,0:T(2,128)} %counts_ref.3), custom_call_target="tpu_custom_call" | custom-call | tf_op jit(solution)/shard_map/pallas_call | solution.py:479
  29.5 1.3 collective-permute-start.4
  30.8 4.5 %collective-permute-start.5 = (f32[136,128]{1,0:T(8,128)S(1)}, f32[136,128]{1,0:T(8,128)S(1)}, u32[]{:S(2)}, u32[]{:S(2)}) collective-permute-start(f32[136,128]{1,0:T(8,128)S(1)} %get-tuple-element.35), channel_id=1, source_target_pairs={{0,1},{1,2},{2,3},{3,4},{4,5},{5,6},{6,7},{8,9},{9,10},{10,11},{11... | collective-permute-start | bytes 208904 | tf_op jit(solution)/shard_map/ppermute | solution.py:493
  35.3 1.3 collective-permute-start.2
  37.2 0.7 collective-permute-done.4.next_ref
  37.9 0.6 collective-permute-done.2.rest_ref
  38.5 1.6 %shard_map.52 = (f32[72,128]{1,0:T(8,128)S(1)}, f32[20,128,128]{2,1,0:T(8,128)S(1)}) custom-call(s32[3]{0:T(128)} %pad_add_fusion.flags.place, f32[1024,128]{1,0:T(8,128)S(1)} %bitcast.14, f32[1024,128]{1,0:T(8,128)S(1)} %bitcast.12, s32[4,2,2,32]{3,2,1,0:T(2,128)} %counts_ref.3, f32[192,128]{1,0:T(8,128)S(1)} %collective-permute-done.up_ref, ...), custom_call_target="tpu_custom_call" | custom-call | tf_op jit(solution)/shard_map/pallas_call | solution.py:479
  40.1 8.7 %collective-permute-start.6 = (f32[72,128]{1,0:T(8,128)S(1)}, f32[72,128]{1,0:T(8,128)S(1)}, u32[]{:S(2)}, u32[]{:S(2)}) collective-permute-start(f32[72,128]{1,0:T(8,128)S(1)} %get-tuple-element.36), channel_id=1, source_target_pairs={{64,0},{72,8},{80,16},{88,24},{128,64},{136,72},{144,80},{152,88},... | collective-permute-start | bytes 110600 | tf_op jit(solution)/shard_map/ppermute | solution.py:542
  48.8 11.2 %collective-permute-done.6 = f32[72,128]{1,0:T(8,128)S(1)} collective-permute-done((f32[72,128]{1,0:T(8,128)S(1)}, f32[72,128]{1,0:T(8,128)S(1)}, u32[]{:S(2)}, u32[]{:S(2)}) %collective-permute-start.6) | collective-permute-done | bytes 36896 | tf_op jit(solution)/shard_map/ppermute | solution.py:542
  60.0 2.2 %collective-permute-start.8 = (f32[144,128]{1,0:T(8,128)S(1)}, f32[144,128]{1,0:T(8,128)S(1)}, u32[]{:S(2)}, u32[]{:S(2)}) collective-permute-start(f32[144,128]{1,0:T(8,128)S(1)} %constant_dynamic-update-slice_fusion.both), channel_id=1, source_target_pairs={{0,1},{1,2},{2,3},{3,4},{4,5},{5,6},{6,7},{8,9},{9,10},{10,11},{11... | collective-permute-start | bytes 221192 | tf_op jit(solution)/shard_map/ppermute | solution.py:493
  62.2 1.3 collective-permute-start.7
  63.5 0.7 collective-permute-done.8.below
  64.2 4.3 %collective-permute-done.7.above = f32[144,128]{1,0:T(8,128)S(1)} collective-permute-done((f32[144,128]{1,0:T(8,128)S(1)}, f32[144,128]{1,0:T(8,128)S(1)}, u32[]{:S(2)}, u32[]{:S(2)}) %collective-permute-start.7) | collective-permute-done | bytes 73760 | tf_op jit(solution)/shard_map/ppermute | solution.py:493
  68.6 23.1 %all_to_all.10 = f32[8,320,128]{2,1,0:T(8,128)S(1)} all-to-all(f32[8,320,128]{2,1,0:T(8,128)S(1)} %broadcast_in_dim.6), channel_id=1, replica_groups=mesh['y'=4,'zhi'=4,'x'=4,'core'=2,'row'=8] {'x','core'}, dimensions={0} | all-to-all | bytes 2621440 | tf_op jit(solution)/shard_map/all_to_all | solution.py:545
  91.7 1.1 shard_map.54
  92.7 3.6 %collective-permute-start.10 = (f32[6,16,128]{2,1,0:T(8,128)S(1)}, f32[6,16,128]{2,1,0:T(8,128)S(1)}, u32[]{:S(2)}, u32[]{:S(2)}) collective-permute-start(f32[6,16,128]{2,1,0:T(8,128)S(1)} %get-tuple-element.40.v2), channel_id=1, source_target_pairs={{0,1},{1,2},{2,3},{3,4},{4,5},{5,6},{6,7},{8,9},{9,10},{10,11},{11... | collective-permute-start | bytes 147464 | tf_op jit(solution)/shard_map/ppermute | solution.py:493
  96.3 1.3 collective-permute-start.9
  98.0 4.3 %collective-permute-done.9.above = f32[6,16,128]{2,1,0:T(8,128)S(1)} collective-permute-done((f32[6,16,128]{2,1,0:T(8,128)S(1)}, f32[6,16,128]{2,1,0:T(8,128)S(1)}, u32[]{:S(2)}, u32[]{:S(2)}) %collective-permute-start.9) | collective-permute-done | bytes 49184 | tf_op jit(solution)/shard_map/ppermute | solution.py:493
  102.8 39.9 %all_to_all.11 = f32[128,1,128]{2,1,0:T(1,128)S(1)} all-to-all(f32[128,1,128]{2,1,0:T(1,128)S(1)} %broadcast_in_dim.16), channel_id=1, replica_groups=mesh['y'=4,'zhi'=4,'x'=4,'core'=2,'row'=8] {'y','zhi','row'}, dimensions={0} | all-to-all | bytes 131072 | tf_op jit(solution)/shard_map/all_to_all | solution.py:561
  142.7 3.6 %shard_map.56 = (f32[6,2,2,32]{3,2,1,0:T(2,128)}, f32[1024,128]{1,0:T(8,128)}) custom-call(s32[3]{0:T(128)} %pad_add_fusion.flags.place, f32[128,128]{1,0:T(8,128)S(1)} %bitcast.15, f32[6,16,128]{2,1,0:T(8,128)S(1)} %get-tuple-element.38.v0, f32[6,16,128]{2,1,0:T(8,128)S(1)} %get-tuple-element.39.v1, f32[6,16,128]{2,1,0:T(8,128)S(1)} %get-tuple-element.40.v2, ...), custom_call_target="tpu_custom_call" | custom-call | tf_op jit(solution)/shard_map/pallas_call | solution.py:479
  (18 shorter events, 1.6 us)
Async XLA Ops:
  0.6 37.9 %copy-start = (f32[4,2,2,32,2,128]{5,4,3,2,1,0:T(2,128)S(1)}, f32[4,2,2,32,2,128]{5,4,3,2,1,0:T(2,128)}, u32[]{:S(2)}) copy-start(f32[4,2,2,32,2,128]{5,4,3,2,1,0:T(2,128)} %param.4) | copy-start | bytes 1572868
  0.6 37.9 %copy-start.1 = (f32[4,2,2,32,2,128]{5,4,3,2,1,0:T(2,128)S(1)}, f32[4,2,2,32,2,128]{5,4,3,2,1,0:T(2,128)}, u32[]{:S(2)}) copy-start(f32[4,2,2,32,2,128]{5,4,3,2,1,0:T(2,128)} %param.3) | copy-start | bytes 1572868
  1.7 25.5 %collective-permute-start.1 = (f32[192,128]{1,0:T(8,128)S(1)}, f32[192,128]{1,0:T(8,128)S(1)}, u32[]{:S(2)}, u32[]{:S(2)}) collective-permute-start(f32[192,128]{1,0:T(8,128)S(1)} %get-tuple-element.32), channel_id=1, source_target_pairs={{64,112},{128,176},{192,240},{256,304},{320,368},{384,432},{448,49... | collective-permute-start | bytes 294920 | tf_op jit(solution)/shard_map/ppermute | solution.py:526
  6.4 30.8 %collective-permute-start = (f32[192,128]{1,0:T(8,128)S(1)}, f32[192,128]{1,0:T(8,128)S(1)}, u32[]{:S(2)}, u32[]{:S(2)}) collective-permute-start(f32[192,128]{1,0:T(8,128)S(1)} %get-tuple-element.26), channel_id=1, source_target_pairs={{8,0},{16,8},{24,16},{32,24},{40,32},{48,40},{56,48},{64,56},{72,6... | collective-permute-start | bytes 294920 | tf_op jit(solution)/shard_map/ppermute | solution.py:493
  27.2 10.7 %collective-permute-start.3 = (f32[192,128]{1,0:T(8,128)S(1)}, f32[192,128]{1,0:T(8,128)S(1)}, u32[]{:S(2)}, u32[]{:S(2)}) collective-permute-start(f32[192,128]{1,0:T(8,128)S(1)} %collective-permute-done.1), channel_id=1, source_target_pairs={{112,56},{176,120},{240,184},{304,248},{368,312},{432,376},{496,44... | collective-permute-start | bytes 294920 | tf_op jit(solution)/shard_map/ppermute | solution.py:528
  29.5 8.4 %collective-permute-start.4 = (f32[128,128]{1,0:T(8,128)S(1)}, f32[128,128]{1,0:T(8,128)S(1)}, u32[]{:S(2)}, u32[]{:S(2)}) collective-permute-start(f32[128,128]{1,0:T(8,128)S(1)} %get-tuple-element.34), channel_id=1, source_target_pairs={{1,0},{2,1},{3,2},{4,3},{5,4},{6,5},{7,6},{9,8},{10,9},{11,10},{12... | collective-permute-start | bytes 196616 | tf_op jit(solution)/shard_map/ppermute | solution.py:493
  30.8 7.1 %collective-permute-start.5 = (f32[136,128]{1,0:T(8,128)S(1)}, f32[136,128]{1,0:T(8,128)S(1)}, u32[]{:S(2)}, u32[]{:S(2)}) collective-permute-start(f32[136,128]{1,0:T(8,128)S(1)} %get-tuple-element.35), channel_id=1, source_target_pairs={{0,1},{1,2},{2,3},{3,4},{4,5},{5,6},{6,7},{8,9},{9,10},{10,11},{11... | collective-permute-start | bytes 208904 | tf_op jit(solution)/shard_map/ppermute | solution.py:493
  35.3 3.2 %collective-permute-start.2 = (f32[192,128]{1,0:T(8,128)S(1)}, f32[192,128]{1,0:T(8,128)S(1)}, u32[]{:S(2)}, u32[]{:S(2)}) collective-permute-start(f32[192,128]{1,0:T(8,128)S(1)} %get-tuple-element.32), channel_id=1, source_target_pairs={{8,0},{16,8},{24,16},{32,24},{40,32},{48,40},{56,48},{72,64},{80,7... | collective-permute-start | bytes 294920 | tf_op jit(solution)/shard_map/ppermute | solution.py:530
  40.1 51.6 %copy-start.2 = (f32[20,128,128]{2,1,0:T(8,128)}, f32[20,128,128]{2,1,0:T(8,128)S(1)}, u32[]{:S(2)}) copy-start(f32[20,128,128]{2,1,0:T(8,128)S(1)} %get-tuple-element.47.kept_hbm) | copy-start | bytes 3932164
  40.1 19.9 %collective-permute-start.6 = (f32[72,128]{1,0:T(8,128)S(1)}, f32[72,128]{1,0:T(8,128)S(1)}, u32[]{:S(2)}, u32[]{:S(2)}) collective-permute-start(f32[72,128]{1,0:T(8,128)S(1)} %get-tuple-element.36), channel_id=1, source_target_pairs={{64,0},{72,8},{80,16},{88,24},{128,64},{136,72},{144,80},{152,88},... | collective-permute-start | bytes 110600 | tf_op jit(solution)/shard_map/ppermute | solution.py:542
  60.0 4.1 %collective-permute-start.8 = (f32[144,128]{1,0:T(8,128)S(1)}, f32[144,128]{1,0:T(8,128)S(1)}, u32[]{:S(2)}, u32[]{:S(2)}) collective-permute-start(f32[144,128]{1,0:T(8,128)S(1)} %constant_dynamic-update-slice_fusion.both), channel_id=1, source_target_pairs={{0,1},{1,2},{2,3},{3,4},{4,5},{5,6},{6,7},{8,9},{9,10},{10,11},{11... | collective-permute-start | bytes 221192 | tf_op jit(solution)/shard_map/ppermute | solution.py:493
  62.2 6.2 %collective-permute-start.7 = (f32[144,128]{1,0:T(8,128)S(1)}, f32[144,128]{1,0:T(8,128)S(1)}, u32[]{:S(2)}, u32[]{:S(2)}) collective-permute-start(f32[144,128]{1,0:T(8,128)S(1)} %constant_dynamic-update-slice_fusion.both), channel_id=1, source_target_pairs={{1,0},{2,1},{3,2},{4,3},{5,4},{6,5},{7,6},{9,8},{10,9},{11,10},{12... | collective-permute-start | bytes 221192 | tf_op jit(solution)/shard_map/ppermute | solution.py:493
  92.7 5.3 %collective-permute-start.10 = (f32[6,16,128]{2,1,0:T(8,128)S(1)}, f32[6,16,128]{2,1,0:T(8,128)S(1)}, u32[]{:S(2)}, u32[]{:S(2)}) collective-permute-start(f32[6,16,128]{2,1,0:T(8,128)S(1)} %get-tuple-element.40.v2), channel_id=1, source_target_pairs={{0,1},{1,2},{2,3},{3,4},{4,5},{5,6},{6,7},{8,9},{9,10},{10,11},{11... | collective-permute-start | bytes 147464 | tf_op jit(solution)/shard_map/ppermute | solution.py:493
  96.3 6.0 %collective-permute-start.9 = (f32[6,16,128]{2,1,0:T(8,128)S(1)}, f32[6,16,128]{2,1,0:T(8,128)S(1)}, u32[]{:S(2)}, u32[]{:S(2)}) collective-permute-start(f32[6,16,128]{2,1,0:T(8,128)S(1)} %get-tuple-element.40.v2), channel_id=1, source_target_pairs={{1,0},{2,1},{3,2},{4,3},{5,4},{6,5},{7,6},{9,8},{10,9},{11,10},{12... | collective-permute-start | bytes 147464 | tf_op jit(solution)/shard_map/ppermute | solution.py:493

commit v4 on v3

--- a/solution.py
+++ b/solution.py
@@ -18,15 +18,15 @@
 GROUP = ("x", "core")
 OTHERS = ("y", "zhi", "row")
 
-ROWS = 72
+ROWS = 64
 AT_C = 12
-AT_SEND = 48
-USED = 66
-AT_E = 66
-AT_E2 = 132
-DOUBLE = 160
-BEYOND = [AT_C + 9 + i for i in range(9)] + [6 + i for i in range(6)]
-BEYOND += [AT_SEND + 3 + i for i in range(6)] + [AT_SEND + 12 + i for i in range(6)]
+AT_THREE = 48
+AT_TWO = 57
+USED = 62
+AT_E = 62
+AT_E2 = 124
+DOUBLE = 144
+BEYOND = [6 + i for i in range(6)] + [AT_THREE + 3 + i for i in range(6)] + [AT_TWO + i for i in range(3)]
 
 
 def sym_at(a, b):
@@ -46,6 +46,26 @@
 def counts_row(ref, kind):
     cells = [ref[kind, sec, row : row + 1, :] for sec in range(2) for row in range(2)]
     return jnp.concatenate(cells, axis=1).astype(jnp.float32)
+
+
+def live_counts(flags, counts_ref):
+    row_zero, sec_zero = lane_bits((1, 128))
+    lane = lax.broadcasted_iota(jnp.int32, (1, 128), 1)
+    last_row = flags[0] == 1
+    last_sec = flags[1] == 1
+    zero = jnp.zeros((1, 128), jnp.float32)
+    counts = [counts_row(counts_ref, kind) for kind in range(4)]
+    return [
+        jnp.where(lane % 32 == 31, zero, counts[0]),
+        jnp.where(jnp.logical_and(jnp.logical_not(row_zero), last_row), zero, counts[1]),
+        jnp.where(jnp.logical_and(jnp.logical_not(sec_zero), last_sec), zero, counts[2]),
+        jnp.where(last_sec, zero, counts[3]),
+    ]
+
+
+def live_points(count):
+    point = lax.broadcasted_iota(jnp.int32, (128, 128), 0).astype(jnp.float32)
+    return jnp.where(point < count, 1.0, 0.0)
 
 
 def block_sums(first, second, live):
@@ -69,9 +89,6 @@
 
 def gram_kernel(flags, f_ref, g_ref, counts_ref, up_ref, rest_ref, outside_ref, next_ref, low_ref, packet, kept):
     row_zero, sec_zero = lane_bits((1, 128))
-    lane = lax.broadcasted_iota(jnp.int32, (1, 128), 1)
-    last_row = flags[0] == 1
-    last_sec = flags[1] == 1
 
     def pair_rows(ref, start, count, comp):
         return ref[pl.ds(2 * start + comp, count, stride=2), :]
@@ -80,17 +97,10 @@
         return [pair_rows(ref, kind * 128, 128, comp).T for comp in range(2)]
 
     zero = jnp.zeros((1, 128), jnp.float32)
-    counts = [counts_row(counts_ref, kind) for kind in range(4)]
-    alive = [
-        jnp.where(lane % 32 == 31, zero, counts[0]),
-        jnp.where(jnp.logical_and(jnp.logical_not(row_zero), last_row), zero, counts[1]),
-        jnp.where(jnp.logical_and(jnp.logical_not(sec_zero), last_sec), zero, counts[2]),
-        jnp.where(last_sec, zero, counts[3]),
-    ]
-    point = lax.broadcasted_iota(jnp.int32, (128, 128), 0).astype(jnp.float32)
+    alive = live_counts(flags, counts_ref)
 
     def masked(points, count):
-        live = jnp.where(point < count, 1.0, 0.0)
+        live = live_points(count)
         return [z * live for z in points], live
 
     def second_of(kind):
@@ -123,11 +133,8 @@
     for kind in range(4):
         first, live = masked(own(f_ref, kind), alive[kind])
         second, _ = masked(second_of(kind), alive[kind])
-        kept[5 * kind] = first[0]
-        kept[5 * kind + 1] = first[1]
-        kept[5 * kind + 2] = second[0]
-        kept[5 * kind + 3] = second[1]
-        kept[5 * kind + 4] = live
+        for i, points in enumerate(first + second):
+            kept[4 * kind + i] = points
         F, G, C, s1, s2 = block_sums(first, second, live)
         D = [a + b for a, b in zip(D, F)]
         S = [a + b for a, b in zip(S, s1)]
@@ -142,13 +149,16 @@
         elif kind == 2:
             D = [a + jnp.where(sec_zero, zero, roll(b, 64, 1)) for a, b in zip(D, G)]
             S = [a - jnp.where(sec_zero, zero, roll(b, 64, 1)) for a, b in zip(S, s2)]
-        if kind >= 2:
-            base = AT_SEND + 9 * (kind - 2)
-            put(base, G[0] * unit)
-            put(base + 1, G[1] * unit)
-            put(base + 2, G[3] * unit)
+            for i in range(3):
+                put(AT_TWO + i, jnp.where(sec_zero, roll(s2[3 + i], 64, 1), s2[i]))
+            put(AT_TWO + 3, jnp.where(sec_zero, roll(G[1], 64, 1), G[0]) * unit)
+            put(AT_TWO + 4, G[3] * unit)
+        else:
+            put(AT_THREE, G[0] * unit)
+            put(AT_THREE + 1, G[1] * unit)
+            put(AT_THREE + 2, G[3] * unit)
             for i in range(6):
-                put(base + 3 + i, s2[i])
+                put(AT_THREE + 3 + i, s2[i])
 
     low_count = jnp.where(row_zero, zero, low_ref[128:129, :])
     first = []
@@ -168,7 +178,7 @@
         a, b = SYM[i]
         put(i, D[i] * unit + ((SQUARES[a] - SHIFT) * unit if a == b else 0.0))
         put(6 + i, S[i])
-    for row in range(AT_SEND + 18, ROWS):
+    for row in range(USED, ROWS):
         put(row, zero)
 
 
@@ -215,11 +225,14 @@
         a = above[at : at + USED, :]
         b = below[at : at + USED, :]
         out[to + AT_E : to + AT_E + USED, :] = jnp.where(row_zero, a, b)
+        first = AT_C + 9
+        for i in range(5):
+            one, two = b[first + i : first + i + 1], b[first + min(5 + i, 8) : first + min(5 + i, 8) + 1]
+            out[to + AT_E2 + i : to + AT_E2 + i + 1, :] = jnp.where(row_zero, one, roll(two, 32, 1))
         for i, source in enumerate(BEYOND):
-            out[to + AT_E2 + i : to + AT_E2 + i + 1, :] = jnp.where(
+            out[to + AT_E2 + 5 + i : to + AT_E2 + 6 + i, :] = jnp.where(
                 row_zero, b[source : source + 1], a[source : source + 1]
             )
-        out[to + AT_E2 + len(BEYOND) : to + DOUBLE, :] = jnp.zeros((DOUBLE - AT_E2 - len(BEYOND), 128), jnp.float32)
 
 
 class Window:
@@ -300,31 +313,38 @@
             [got[pl.ds(slot * DOUBLE + i, n_dev, stride=2 * DOUBLE), :] for slot in range(2)], axis=0
         )
 
-    def pushed(kind, value):
-        if kind == 2:
-            return from_below(jnp.where(sec_zero, roll(value, 64, 1), zero))
-        return from_below(value)
+    def from_two(value, packed_second=False):
+        if not packed_second:
+            value = roll(value, 64, 1)
+        return from_below(jnp.where(sec_zero, value, zero))
+
+    def s_terms(three, two):
+        return [
+            from_below(row(three + i)) + from_two(row(two + i % 3), packed_second=i >= 3) for i in range(6)
+        ]
 
     starts = []
     for side, at in enumerate((0, AT_E)):
+        base = side * 42
         for i in range(36):
-            blocks[side * 42 + 6 + i] = row(at + AT_C + i)
-        D = [row(at + i) for i in range(6)]
-        S = [row(at + 6 + i) for i in range(6)]
-        for kind in (2, 3):
-            base = at + AT_SEND + 9 * (kind - 2)
-            last = [blocks[side * 42 + 6 + 9 * kind + i] for i in (6, 7, 8)]
-            G = [row(base), row(base + 1), last[0], row(base + 2), last[1], last[2]]
-            D = [a + pushed(kind, b) for a, b in zip(D, G)]
-            S = [a - pushed(kind, row(base + 3 + i)) for i, a in enumerate(S)]
+            blocks[base + 6 + i] = row(at + AT_C + i)
+        two = [blocks[base + 24 + i] for i in (6, 7, 8)]
+        three = [blocks[base + 33 + i] for i in (6, 7, 8)]
+        pair, last = row(at + AT_TWO + 3), row(at + AT_TWO + 4)
+        G_two = [from_two(z) for z in (pair, pair, two[0], last, two[1], two[2])]
+        G_two[1] = from_two(pair, packed_second=True)
+        G_three = [row(at + AT_THREE), row(at + AT_THREE + 1), three[0], row(at + AT_THREE + 2), three[1], three[2]]
         for i in range(6):
-            blocks[side * 42 + i] = D[i]
-        starts.append(S)
-    for i in range(9):
-        blocks[84 + i] = row(AT_E2 + i)
-    outer = [
-        row(AT_E2 + 9 + i) - pushed(2, row(AT_E2 + 15 + i)) - pushed(3, row(AT_E2 + 21 + i)) for i in range(6)
-    ]
+            blocks[base + i] = row(at + i) + G_two[i] + from_below(G_three[i])
+        terms = s_terms(at + AT_THREE + 3, at + AT_TWO)
+        starts.append([row(at + 6 + i) - terms[i] for i in range(6)])
+    for i in range(5):
+        packed = row(AT_E2 + i)
+        blocks[84 + i] = packed
+        if i < 4:
+            blocks[89 + i] = roll(packed, -32, 1)
+    terms = s_terms(AT_E2 + 11, AT_E2 + 17)
+    outer = [row(AT_E2 + 5 + i) - terms[i] for i in range(6)]
     window = Window(lambda i: blocks[i], n_dev)
     v, e = starts
     w, f = window.apply(v, e, outer, (0, 1))
@@ -337,7 +357,9 @@
         v2[i] = last[i]
 
 
-def moments_kernel(blocks, v0, v1, v2, above, below, e2, v3, e3, out):
+def moments_kernel(blocks, v0, v1, v2, above, below, kept_hbm, e2, v3, e3, out, kept, sems):
+    fetch = pltpu.make_async_copy(kept_hbm, kept, sems.at[0])
+    fetch.start()
     shape = v2.shape[1:]
     n_dev = shape[0] // 2
     bits = lane_bits(shape)
@@ -374,6 +396,7 @@
         value = jnp.sum(jnp.sum(value, axis=0, keepdims=True), axis=1, keepdims=True)
         packed = jnp.where(lane == n, value, packed)
     out[...] = packed
+    fetch.wait()
 
 
 def coefficients(moments):
@@ -406,19 +429,14 @@
     return [value * (1.0 / SPAN) for value in x]
 
 
-def finish_kernel(place, sums, v0, v1, v2, v3, n0, n1, n2, n3, kept_hbm, affines, residual_hbm, kept, residual, sems):
-    fetches = [
-        pltpu.make_async_copy(kept_hbm.at[pl.ds(5 * kind, 5)], kept.at[pl.ds(5 * kind, 5)], sems.at[kind])
-        for kind in range(4)
-    ]
-    for fetch in fetches:
-        fetch.start()
+def finish_kernel(flags, counts_ref, sums, v0, v1, v2, v3, n0, n1, n2, n3, kept, affines, residual_hbm, residual, sems):
     stores = []
     total = jnp.sum(sums[...], axis=0, keepdims=True)
     lane = lax.broadcasted_iota(jnp.int32, (1, 128), 1)
     moments = [jnp.sum(jnp.where(lane == n, total, 0.0), axis=1, keepdims=True) for n in range(8)]
     weights = coefficients(moments)
-    at = place[2]
+    at = flags[2]
+    alive = live_counts(flags, counts_ref)
     row_zero, sec_zero = lane_bits((1, 128))
 
     def mix(refs, i, dev):
@@ -442,15 +460,15 @@
             b = [jnp.where(sec_zero, roll(z, 64, 1), roll(w, 64, 1)) for z, w in zip(x, above)]
         else:
             b = above
-        fetches[kind].wait()
-        u, v, p, q, live = (kept[5 * kind + i] for i in range(5))
+        u, v, p, q = (kept[4 * kind + i] for i in range(4))
+        live = live_points(alive[kind])
         for comp in range(2):
             o = 3 * comp
             r = (p - u) if comp == 0 else (q - v)
             r = r - (x[o] * u + x[o + 1] * v) + (b[o] * p + b[o + 1] * q) - live * (x[o + 2] - b[o + 2])
             residual[pl.ds(kind * 256 + comp, 128, stride=2), :] = r.T
         part = pl.ds(kind * 256, 256)
-        stores.append(pltpu.make_async_copy(residual.at[part], residual_hbm.at[part], sems.at[4 + kind]))
+        stores.append(pltpu.make_async_copy(residual.at[part], residual_hbm.at[part], sems.at[kind]))
         stores[-1].start()
     for store in stores:
         store.wait()
@@ -530,7 +548,7 @@
     rest = lax.ppermute(rest, SEC_AXES, inside)
     beside = shifted(beside, "row", -1)
     low = shifted(odd, "row", 1)
-    packet, kept = run(gram_kernel, [(ROWS, 128), (20, 128, 128)], flags, f, g, counts, up, rest, outside, beside, low, scalars=1)
+    packet, kept = run(gram_kernel, [(ROWS, 128), (16, 128, 128)], flags, f, g, counts, up, rest, outside, beside, low, scalars=1)
 
     half = n_dev // 2
     pairs = []
@@ -547,15 +565,18 @@
     blocks, v0, e0, v1, e1, v2 = run(
         window_kernel, [(93, 2 * n_dev, 128)] + [wide] * 5, got.reshape(n_dev * 2 * DOUBLE, 128)
     )
-    e2, v3, e3, part = run(
+    e2, v3, e3, part, kept = run(
         moments_kernel,
-        [wide, wide, wide, (1, 128)],
+        [wide, wide, wide, (1, 128), (16, 128, 128)],
         blocks,
         v0,
         v1,
         v2,
         shifted(v2, "row", -1),
         shifted(v2, "row", 1),
+        kept,
+        anywhere=(6,),
+        copies=1,
     )
     n_other = lax.axis_size(OTHERS)
     sums = lax.all_to_all(jnp.broadcast_to(part[None], (n_other, 1, 128)), OTHERS, 0, 0, tiled=False)
@@ -563,6 +584,7 @@
         finish_kernel,
         [(6,) + counts.shape[1:], (1024, 128)],
         flags,
+        counts,
         sums.reshape(n_other, 128),
         v0,
         v1,
@@ -574,9 +596,8 @@
         e3,
         kept,
         scalars=1,
-        anywhere=(10,),
-        copies=8,
-        buffers=[(20, 128, 128), (1024, 128)],
+        copies=4,
+        buffers=[(1024, 128)],
         results=[pltpu.VMEM, pl.ANY],
     )
     return affines, residual.reshape(first_pts.shape)

time: 148 us -> 147 us (level)
  no operation moved by 1% of the time
where the time goes in v4:
time: 147 us; the launch traced here: 144 us
  blocking collectives  63.2 us (43%)
  starting transfers between devices  49.2 us (33%)
  waiting for transfers between devices  21.3 us (14%)
  Pallas kernels  9.02 us (6%)
    all_to_all x1, blocking collectives, per_device(): lax.all_to_all(jnp.broadcast_to(part[None], (n_other, 1, 128)), OTHERS, 0...  40.4 us
    ppermute x7, starting transfers between devices, shifted(): return lax.ppermute(value, axes, pairs)  33.9 us
    all_to_all x1, blocking collectives, per_device(): lax.all_to_all(jnp.broadcast_to(mine[None], (n_dev, 2 * DOUBLE, 128)), GR...  22.8 us
    ppermute x1, waiting for transfers between devices, per_device(): other = lax.ppermute(packet, SEC_AXES, pairs)  10.5 us
    ppermute x7, waiting for transfers between devices, shifted(): return lax.ppermute(value, axes, pairs)  10.2 us
    pallas_call x7, Pallas kernels, call(): pl.pallas_call(kernel, out_shape=shapes, in_specs=spaces, out_specs=[pl.B...  9.02 us
    ppermute x1, starting transfers between devices, per_device(): other = lax.ppermute(packet, SEC_AXES, pairs)  8.72 us
    ppermute x1, starting transfers between devices, per_device(): relayed = lax.ppermute(rest, SEC_AXES, to_relay)  4.67 us
  transfers between devices with their start and end apart: 11, of which 7 were waited for; matrix products, arithmetic and copies ran while one was open for 0% of the time, Pallas kernels for 1%

profile of v4, /device:TPU:24, one launch (start us, length us, event | category | flops | bytes accessed | tf_op | source)
XLA Modules:
  0.0 144.4 jit_solution(5585923027139162848)
XLA Ops:
  0.7 1.1 shard_map.50
  1.7 4.7 %collective-permute-start.1 = (f32[192,128]{1,0:T(8,128)S(1)}, f32[192,128]{1,0:T(8,128)S(1)}, u32[]{:S(2)}, u32[]{:S(2)}) collective-permute-start(f32[192,128]{1,0:T(8,128)S(1)} %get-tuple-element.33), channel_id=1, source_target_pairs={{64,112},{128,176},{192,240},{256,304},{320,368},{384,432},{448,49... | collective-permute-start | bytes 294920 | tf_op jit(solution)/shard_map/ppermute | solution.py:544
  6.4 20.8 %collective-permute-start = (f32[192,128]{1,0:T(8,128)S(1)}, f32[192,128]{1,0:T(8,128)S(1)}, u32[]{:S(2)}, u32[]{:S(2)}) collective-permute-start(f32[192,128]{1,0:T(8,128)S(1)} %get-tuple-element.27), channel_id=1, source_target_pairs={{8,0},{16,8},{24,16},{32,24},{40,32},{48,40},{56,48},{64,56},{72,6... | collective-permute-start | bytes 294920 | tf_op jit(solution)/shard_map/ppermute | solution.py:511
  27.2 0.7 collective-permute-start.3
  27.9 1.5 %shard_map.51 = (f32[128,128]{1,0:T(8,128)S(1)}, f32[136,128]{1,0:T(8,128)S(1)}) custom-call(f32[1024,128]{1,0:T(8,128)} %bitcast.13, f32[1024,128]{1,0:T(8,128)} %bitcast.11, s32[4,2,2,32]{3,2,1,0:T(2,128)} %counts_ref.5), custom_call_target="tpu_custom_call" | custom-call | tf_op jit(solution)/shard_map/pallas_call | solution.py:497
  29.5 1.3 collective-permute-start.4
  30.8 4.5 %collective-permute-start.5 = (f32[136,128]{1,0:T(8,128)S(1)}, f32[136,128]{1,0:T(8,128)S(1)}, u32[]{:S(2)}, u32[]{:S(2)}) collective-permute-start(f32[136,128]{1,0:T(8,128)S(1)} %get-tuple-element.36), channel_id=1, source_target_pairs={{0,1},{1,2},{2,3},{3,4},{4,5},{5,6},{6,7},{8,9},{9,10},{10,11},{11... | collective-permute-start | bytes 208904 | tf_op jit(solution)/shard_map/ppermute | solution.py:511
  35.3 1.3 collective-permute-start.2
  36.6 0.6 pad_add_fusion.flags
  37.2 0.7 collective-permute-done.4.next_ref
  38.5 1.5 %shard_map.52 = (f32[64,128]{1,0:T(8,128)S(1)}, f32[16,128,128]{2,1,0:T(8,128)S(1)}) custom-call(s32[3]{0:T(128)} %pad_add_fusion.flags, f32[1024,128]{1,0:T(8,128)S(1)} %bitcast.14, f32[1024,128]{1,0:T(8,128)S(1)} %bitcast.12, s32[4,2,2,32]{3,2,1,0:T(2,128)} %counts_ref.5, f32[192,128]{1,0:T(8,128)S(1)} %collective-permute-done.up_ref, ...), custom_call_target="tpu_custom_call" | custom-call | tf_op jit(solution)/shard_map/pallas_call | solution.py:497
  40.1 8.7 %collective-permute-start.6 = (f32[64,128]{1,0:T(8,128)S(1)}, f32[64,128]{1,0:T(8,128)S(1)}, u32[]{:S(2)}, u32[]{:S(2)}) collective-permute-start(f32[64,128]{1,0:T(8,128)S(1)} %get-tuple-element.37), channel_id=1, source_target_pairs={{64,0},{72,8},{80,16},{88,24},{128,64},{136,72},{144,80},{152,88},... | collective-permute-start | bytes 98312 | tf_op jit(solution)/shard_map/ppermute | solution.py:560
  48.8 10.5 %collective-permute-done.6 = f32[64,128]{1,0:T(8,128)S(1)} collective-permute-done((f32[64,128]{1,0:T(8,128)S(1)}, f32[64,128]{1,0:T(8,128)S(1)}, u32[]{:S(2)}, u32[]{:S(2)}) %collective-permute-start.6) | collective-permute-done | bytes 32800 | tf_op jit(solution)/shard_map/ppermute | solution.py:560
  59.3 1.3 collective-permute-start.8
  60.6 1.3 collective-permute-start.7
  62.5 4.3 %collective-permute-done.7.above = f32[128,128]{1,0:T(8,128)S(1)} collective-permute-done((f32[128,128]{1,0:T(8,128)S(1)}, f32[128,128]{1,0:T(8,128)S(1)}, u32[]{:S(2)}, u32[]{:S(2)}) %collective-permute-start.7) | collective-permute-done | bytes 65568 | tf_op jit(solution)/shard_map/ppermute | solution.py:511
  66.9 22.8 %all_to_all.10 = f32[8,288,128]{2,1,0:T(8,128)S(1)} all-to-all(f32[8,288,128]{2,1,0:T(8,128)S(1)} %broadcast_in_dim.6), channel_id=1, replica_groups=mesh['y'=4,'zhi'=4,'x'=4,'core'=2,'row'=8] {'x','core'}, dimensions={0} | all-to-all | bytes 2359296 | tf_op jit(solution)/shard_map/all_to_all | solution.py:563
  89.7 1.0 shard_map.54
  90.7 3.4 %collective-permute-start.10 = (f32[6,16,128]{2,1,0:T(8,128)S(1)}, f32[6,16,128]{2,1,0:T(8,128)S(1)}, u32[]{:S(2)}, u32[]{:S(2)}) collective-permute-start(f32[6,16,128]{2,1,0:T(8,128)S(1)} %get-tuple-element.41.v2), channel_id=1, source_target_pairs={{0,1},{1,2},{2,3},{3,4},{4,5},{5,6},{6,7},{8,9},{9,10},{10,11},{11... | collective-permute-start | bytes 147464 | tf_op jit(solution)/shard_map/ppermute | solution.py:511
  94.1 1.3 collective-permute-start.9
  95.8 4.3 %collective-permute-done.9.above = f32[6,16,128]{2,1,0:T(8,128)S(1)} collective-permute-done((f32[6,16,128]{2,1,0:T(8,128)S(1)}, f32[6,16,128]{2,1,0:T(8,128)S(1)}, u32[]{:S(2)}, u32[]{:S(2)}) %collective-permute-start.9) | collective-permute-done | bytes 49184 | tf_op jit(solution)/shard_map/ppermute | solution.py:511
  100.1 1.2 shard_map.55
  101.4 40.4 %all_to_all.11 = f32[128,1,128]{2,1,0:T(1,128)S(1)} all-to-all(f32[128,1,128]{2,1,0:T(1,128)S(1)} %broadcast_in_dim.16), channel_id=1, replica_groups=mesh['y'=4,'zhi'=4,'x'=4,'core'=2,'row'=8] {'y','zhi','row'}, dimensions={0} | all-to-all | bytes 131072 | tf_op jit(solution)/shard_map/all_to_all | solution.py:582
  141.8 2.6 %shard_map.56 = (f32[6,2,2,32]{3,2,1,0:T(2,128)}, f32[1024,128]{1,0:T(8,128)}) custom-call(s32[3]{0:T(128)} %pad_add_fusion.flags, s32[4,2,2,32]{3,2,1,0:T(2,128)} %counts_ref.5, f32[128,128]{1,0:T(8,128)S(1)} %bitcast.15, f32[6,16,128]{2,1,0:T(8,128)S(1)} %get-tuple-element.39.v0, f32[6,16,128]{2,1,0:T(8,128)S(1)} %get-tuple-element.40.v1, ...), custom_call_target="tpu_custom_call" | custom-call | tf_op jit(solution)/shard_map/pallas_call | solution.py:497
  (18 shorter events, 1.8 us)
Async XLA Ops:
  0.6 37.9 %copy-start = (f32[4,2,2,32,2,128]{5,4,3,2,1,0:T(2,128)S(1)}, f32[4,2,2,32,2,128]{5,4,3,2,1,0:T(2,128)}, u32[]{:S(2)}) copy-start(f32[4,2,2,32,2,128]{5,4,3,2,1,0:T(2,128)} %param.4) | copy-start | bytes 1572868
  0.6 37.9 %copy-start.1 = (f32[4,2,2,32,2,128]{5,4,3,2,1,0:T(2,128)S(1)}, f32[4,2,2,32,2,128]{5,4,3,2,1,0:T(2,128)}, u32[]{:S(2)}) copy-start(f32[4,2,2,32,2,128]{5,4,3,2,1,0:T(2,128)} %param.3) | copy-start | bytes 1572868
  1.7 25.5 %collective-permute-start.1 = (f32[192,128]{1,0:T(8,128)S(1)}, f32[192,128]{1,0:T(8,128)S(1)}, u32[]{:S(2)}, u32[]{:S(2)}) collective-permute-start(f32[192,128]{1,0:T(8,128)S(1)} %get-tuple-element.33), channel_id=1, source_target_pairs={{64,112},{128,176},{192,240},{256,304},{320,368},{384,432},{448,49... | collective-permute-start | bytes 294920 | tf_op jit(solution)/shard_map/ppermute | solution.py:544
  6.4 30.8 %collective-permute-start = (f32[192,128]{1,0:T(8,128)S(1)}, f32[192,128]{1,0:T(8,128)S(1)}, u32[]{:S(2)}, u32[]{:S(2)}) collective-permute-start(f32[192,128]{1,0:T(8,128)S(1)} %get-tuple-element.27), channel_id=1, source_target_pairs={{8,0},{16,8},{24,16},{32,24},{40,32},{48,40},{56,48},{64,56},{72,6... | collective-permute-start | bytes 294920 | tf_op jit(solution)/shard_map/ppermute | solution.py:511
  27.2 10.7 %collective-permute-start.3 = (f32[192,128]{1,0:T(8,128)S(1)}, f32[192,128]{1,0:T(8,128)S(1)}, u32[]{:S(2)}, u32[]{:S(2)}) collective-permute-start(f32[192,128]{1,0:T(8,128)S(1)} %collective-permute-done.1), channel_id=1, source_target_pairs={{112,56},{176,120},{240,184},{304,248},{368,312},{432,376},{496,44... | collective-permute-start | bytes 294920 | tf_op jit(solution)/shard_map/ppermute | solution.py:546
  29.5 8.4 %collective-permute-start.4 = (f32[128,128]{1,0:T(8,128)S(1)}, f32[128,128]{1,0:T(8,128)S(1)}, u32[]{:S(2)}, u32[]{:S(2)}) collective-permute-start(f32[128,128]{1,0:T(8,128)S(1)} %get-tuple-element.35), channel_id=1, source_target_pairs={{1,0},{2,1},{3,2},{4,3},{5,4},{6,5},{7,6},{9,8},{10,9},{11,10},{12... | collective-permute-start | bytes 196616 | tf_op jit(solution)/shard_map/ppermute | solution.py:511
  30.8 7.1 %collective-permute-start.5 = (f32[136,128]{1,0:T(8,128)S(1)}, f32[136,128]{1,0:T(8,128)S(1)}, u32[]{:S(2)}, u32[]{:S(2)}) collective-permute-start(f32[136,128]{1,0:T(8,128)S(1)} %get-tuple-element.36), channel_id=1, source_target_pairs={{0,1},{1,2},{2,3},{3,4},{4,5},{5,6},{6,7},{8,9},{9,10},{10,11},{11... | collective-permute-start | bytes 208904 | tf_op jit(solution)/shard_map/ppermute | solution.py:511
  35.3 3.2 %collective-permute-start.2 = (f32[192,128]{1,0:T(8,128)S(1)}, f32[192,128]{1,0:T(8,128)S(1)}, u32[]{:S(2)}, u32[]{:S(2)}) collective-permute-start(f32[192,128]{1,0:T(8,128)S(1)} %get-tuple-element.33), channel_id=1, source_target_pairs={{8,0},{16,8},{24,16},{32,24},{40,32},{48,40},{56,48},{72,64},{80,7... | collective-permute-start | bytes 294920 | tf_op jit(solution)/shard_map/ppermute | solution.py:548
  40.1 49.7 %copy-start.2 = (f32[16,128,128]{2,1,0:T(8,128)}, f32[16,128,128]{2,1,0:T(8,128)S(1)}, u32[]{:S(2)}) copy-start(f32[16,128,128]{2,1,0:T(8,128)S(1)} %get-tuple-element.42.kept_hbm) | copy-start | bytes 3145732
  40.1 19.2 %collective-permute-start.6 = (f32[64,128]{1,0:T(8,128)S(1)}, f32[64,128]{1,0:T(8,128)S(1)}, u32[]{:S(2)}, u32[]{:S(2)}) collective-permute-start(f32[64,128]{1,0:T(8,128)S(1)} %get-tuple-element.37), channel_id=1, source_target_pairs={{64,0},{72,8},{80,16},{88,24},{128,64},{136,72},{144,80},{152,88},... | collective-permute-start | bytes 98312 | tf_op jit(solution)/shard_map/ppermute | solution.py:560
  59.3 3.2 %collective-permute-start.8 = (f32[128,128]{1,0:T(8,128)S(1)}, f32[128,128]{1,0:T(8,128)S(1)}, u32[]{:S(2)}, u32[]{:S(2)}) collective-permute-start(f32[128,128]{1,0:T(8,128)S(1)} %constant_dynamic-update-slice_fusion.both), channel_id=1, source_target_pairs={{0,1},{1,2},{2,3},{3,4},{4,5},{5,6},{6,7},{8,9},{9,10},{10,11},{11... | collective-permute-start | bytes 196616 | tf_op jit(solution)/shard_map/ppermute | solution.py:511
  60.6 6.2 %collective-permute-start.7 = (f32[128,128]{1,0:T(8,128)S(1)}, f32[128,128]{1,0:T(8,128)S(1)}, u32[]{:S(2)}, u32[]{:S(2)}) collective-permute-start(f32[128,128]{1,0:T(8,128)S(1)} %constant_dynamic-update-slice_fusion.both), channel_id=1, source_target_pairs={{1,0},{2,1},{3,2},{4,3},{5,4},{6,5},{7,6},{9,8},{10,9},{11,10},{12... | collective-permute-start | bytes 196616 | tf_op jit(solution)/shard_map/ppermute | solution.py:511
  90.7 5.1 %collective-permute-start.10 = (f32[6,16,128]{2,1,0:T(8,128)S(1)}, f32[6,16,128]{2,1,0:T(8,128)S(1)}, u32[]{:S(2)}, u32[]{:S(2)}) collective-permute-start(f32[6,16,128]{2,1,0:T(8,128)S(1)} %get-tuple-element.41.v2), channel_id=1, source_target_pairs={{0,1},{1,2},{2,3},{3,4},{4,5},{5,6},{6,7},{8,9},{9,10},{10,11},{11... | collective-permute-start | bytes 147464 | tf_op jit(solution)/shard_map/ppermute | solution.py:511
  94.1 6.0 %collective-permute-start.9 = (f32[6,16,128]{2,1,0:T(8,128)S(1)}, f32[6,16,128]{2,1,0:T(8,128)S(1)}, u32[]{:S(2)}, u32[]{:S(2)}) collective-permute-start(f32[6,16,128]{2,1,0:T(8,128)S(1)} %get-tuple-element.41.v2), channel_id=1, source_target_pairs={{1,0},{2,1},{3,2},{4,3},{5,4},{6,5},{7,6},{9,8},{10,9},{11,10},{12... | collective-permute-start | bytes 147464 | tf_op jit(solution)/shard_map/ppermute | solution.py:511

commit v5 on v4

--- a/solution.py
+++ b/solution.py
@@ -17,6 +17,7 @@
 SEC_AXES = ("y", "zhi", "x", "core")
 GROUP = ("x", "core")
 OTHERS = ("y", "zhi", "row")
+EVERY = SEC_AXES + ("row",)
 
 ROWS = 64
 AT_C = 12
@@ -579,7 +580,10 @@
         copies=1,
     )
     n_other = lax.axis_size(OTHERS)
-    sums = lax.all_to_all(jnp.broadcast_to(part[None], (n_other, 1, 128)), OTHERS, 0, 0, tiled=False)
+    groups = sum_groups([lax.axis_size(axis) for axis in EVERY])
+    sums = lax.all_to_all(
+        jnp.broadcast_to(part[None], (n_other, 1, 128)), EVERY, 0, 0, axis_index_groups=groups, tiled=False
+    )
     affines, residual = run(
         finish_kernel,
         [(6,) + counts.shape[1:], (1024, 128)],
@@ -603,6 +607,15 @@
     return affines, residual.reshape(first_pts.shape)
 
 
+def sum_groups(sizes):
+    n_y, n_zhi, n_x, n_core, n_row = sizes
+    groups = []
+    for place in range(n_x * n_core):
+        order = [((n_zhi - 1 + step) % n_zhi, y, row) for step in range(n_zhi) for y in range(n_y) for row in range(n_row)]
+        groups.append([((y * n_zhi + zhi) * n_x * n_core + place) * n_row + row for zhi, y, row in order])
+    return groups
+
+
 def split_mesh(mesh):
     n_row = mesh.shape["row"]
     return Mesh(mesh.devices.reshape(4, 4, 4, 2, n_row), SEC_AXES + ("row",))

time: 147 us -> 140 us (0.952)
  blocking collectives: 63.2 us -> 56.5 us
    all_to_all x1, blocking collectives: 40.4 us -> 33.7 us  [per_device(): lax.all_to_all(jnp.broadcast_to(part[None], (n_other, 1, 128)), EVERY, 0,...]
where the time goes in v5:
time: 140 us; the launch traced here: 138 us
  blocking collectives  56.5 us (40%)
  starting transfers between devices  49.2 us (35%)
  waiting for transfers between devices  21.3 us (15%)
  Pallas kernels  9.02 us (6%)
    ppermute x7, starting transfers between devices, shifted(): return lax.ppermute(value, axes, pairs)  33.9 us
    all_to_all x1, blocking collectives, per_device(): lax.all_to_all(jnp.broadcast_to(part[None], (n_other, 1, 128)), EVERY, 0,...  33.7 us
    all_to_all x1, blocking collectives, per_device(): lax.all_to_all(jnp.broadcast_to(mine[None], (n_dev, 2 * DOUBLE, 128)), GR...  22.8 us
    ppermute x1, waiting for transfers between devices, per_device(): other = lax.ppermute(packet, SEC_AXES, pairs)  10.5 us
    ppermute x7, waiting for transfers between devices, shifted(): return lax.ppermute(value, axes, pairs)  10.2 us
    pallas_call x7, Pallas kernels, call(): pl.pallas_call(kernel, out_shape=shapes, in_specs=spaces, out_specs=[pl.B...  9.02 us
    ppermute x1, starting transfers between devices, per_device(): other = lax.ppermute(packet, SEC_AXES, pairs)  8.72 us
    ppermute x1, starting transfers between devices, per_device(): relayed = lax.ppermute(rest, SEC_AXES, to_relay)  4.67 us
  transfers between devices with their start and end apart: 11, of which 7 were waited for; matrix products, arithmetic and copies ran while one was open for 0% of the time, Pallas kernels for 1%

profile of v5, /device:TPU:24, one launch (start us, length us, event | category | flops | bytes accessed | tf_op | source)
XLA Modules:
  0.0 137.7 jit_solution(16662785426238414707)
XLA Ops:
  0.7 1.1 shard_map.50
  1.7 4.7 %collective-permute-start.1 = (f32[192,128]{1,0:T(8,128)S(1)}, f32[192,128]{1,0:T(8,128)S(1)}, u32[]{:S(2)}, u32[]{:S(2)}) collective-permute-start(f32[192,128]{1,0:T(8,128)S(1)} %get-tuple-element.33), channel_id=1, source_target_pairs={{64,112},{128,176},{192,240},{256,304},{320,368},{384,432},{448,49... | collective-permute-start | bytes 294920 | tf_op jit(solution)/shard_map/ppermute | solution.py:545
  6.4 20.8 %collective-permute-start = (f32[192,128]{1,0:T(8,128)S(1)}, f32[192,128]{1,0:T(8,128)S(1)}, u32[]{:S(2)}, u32[]{:S(2)}) collective-permute-start(f32[192,128]{1,0:T(8,128)S(1)} %get-tuple-element.27), channel_id=1, source_target_pairs={{8,0},{16,8},{24,16},{32,24},{40,32},{48,40},{56,48},{64,56},{72,6... | collective-permute-start | bytes 294920 | tf_op jit(solution)/shard_map/ppermute | solution.py:512
  27.2 0.7 collective-permute-start.3
  27.9 1.5 %shard_map.51 = (f32[128,128]{1,0:T(8,128)S(1)}, f32[136,128]{1,0:T(8,128)S(1)}) custom-call(f32[1024,128]{1,0:T(8,128)} %bitcast.13, f32[1024,128]{1,0:T(8,128)} %bitcast.11, s32[4,2,2,32]{3,2,1,0:T(2,128)} %counts_ref.5), custom_call_target="tpu_custom_call" | custom-call | tf_op jit(solution)/shard_map/pallas_call | solution.py:498
  29.5 1.3 collective-permute-start.4
  30.8 4.5 %collective-permute-start.5 = (f32[136,128]{1,0:T(8,128)S(1)}, f32[136,128]{1,0:T(8,128)S(1)}, u32[]{:S(2)}, u32[]{:S(2)}) collective-permute-start(f32[136,128]{1,0:T(8,128)S(1)} %get-tuple-element.36), channel_id=1, source_target_pairs={{0,1},{1,2},{2,3},{3,4},{4,5},{5,6},{6,7},{8,9},{9,10},{10,11},{11... | collective-permute-start | bytes 208904 | tf_op jit(solution)/shard_map/ppermute | solution.py:512
  35.3 1.3 collective-permute-start.2
  36.6 0.6 pad_add_fusion.flags
  37.2 0.7 collective-permute-done.4.next_ref
  38.5 1.5 %shard_map.52 = (f32[64,128]{1,0:T(8,128)S(1)}, f32[16,128,128]{2,1,0:T(8,128)S(1)}) custom-call(s32[3]{0:T(128)} %pad_add_fusion.flags, f32[1024,128]{1,0:T(8,128)S(1)} %bitcast.14, f32[1024,128]{1,0:T(8,128)S(1)} %bitcast.12, s32[4,2,2,32]{3,2,1,0:T(2,128)} %counts_ref.5, f32[192,128]{1,0:T(8,128)S(1)} %collective-permute-done.up_ref, ...), custom_call_target="tpu_custom_call" | custom-call | tf_op jit(solution)/shard_map/pallas_call | solution.py:498
  40.1 8.7 %collective-permute-start.6 = (f32[64,128]{1,0:T(8,128)S(1)}, f32[64,128]{1,0:T(8,128)S(1)}, u32[]{:S(2)}, u32[]{:S(2)}) collective-permute-start(f32[64,128]{1,0:T(8,128)S(1)} %get-tuple-element.37), channel_id=1, source_target_pairs={{64,0},{72,8},{80,16},{88,24},{128,64},{136,72},{144,80},{152,88},... | collective-permute-start | bytes 98312 | tf_op jit(solution)/shard_map/ppermute | solution.py:561
  48.8 10.5 %collective-permute-done.6 = f32[64,128]{1,0:T(8,128)S(1)} collective-permute-done((f32[64,128]{1,0:T(8,128)S(1)}, f32[64,128]{1,0:T(8,128)S(1)}, u32[]{:S(2)}, u32[]{:S(2)}) %collective-permute-start.6) | collective-permute-done | bytes 32800 | tf_op jit(solution)/shard_map/ppermute | solution.py:561
  59.3 1.3 collective-permute-start.8
  60.6 1.3 collective-permute-start.7
  62.5 4.3 %collective-permute-done.7.above = f32[128,128]{1,0:T(8,128)S(1)} collective-permute-done((f32[128,128]{1,0:T(8,128)S(1)}, f32[128,128]{1,0:T(8,128)S(1)}, u32[]{:S(2)}, u32[]{:S(2)}) %collective-permute-start.7) | collective-permute-done | bytes 65568 | tf_op jit(solution)/shard_map/ppermute | solution.py:512
  66.9 22.8 %all_to_all.10 = f32[8,288,128]{2,1,0:T(8,128)S(1)} all-to-all(f32[8,288,128]{2,1,0:T(8,128)S(1)} %broadcast_in_dim.6), channel_id=1, replica_groups=mesh['y'=4,'zhi'=4,'x'=4,'core'=2,'row'=8] {'x','core'}, dimensions={0} | all-to-all | bytes 2359296 | tf_op jit(solution)/shard_map/all_to_all | solution.py:564
  89.7 1.0 shard_map.54
  90.7 3.4 %collective-permute-start.10 = (f32[6,16,128]{2,1,0:T(8,128)S(1)}, f32[6,16,128]{2,1,0:T(8,128)S(1)}, u32[]{:S(2)}, u32[]{:S(2)}) collective-permute-start(f32[6,16,128]{2,1,0:T(8,128)S(1)} %get-tuple-element.41.v2), channel_id=1, source_target_pairs={{0,1},{1,2},{2,3},{3,4},{4,5},{5,6},{6,7},{8,9},{9,10},{10,11},{11... | collective-permute-start | bytes 147464 | tf_op jit(solution)/shard_map/ppermute | solution.py:512
  94.1 1.3 collective-permute-start.9
  95.8 4.3 %collective-permute-done.9.above = f32[6,16,128]{2,1,0:T(8,128)S(1)} collective-permute-done((f32[6,16,128]{2,1,0:T(8,128)S(1)}, f32[6,16,128]{2,1,0:T(8,128)S(1)}, u32[]{:S(2)}, u32[]{:S(2)}) %collective-permute-start.9) | collective-permute-done | bytes 49184 | tf_op jit(solution)/shard_map/ppermute | solution.py:512
  100.1 1.2 shard_map.55
  101.4 33.7 %all_to_all.11 = f32[128,1,128]{2,1,0:T(1,128)S(1)} all-to-all(f32[128,1,128]{2,1,0:T(1,128)S(1)} %broadcast_in_dim.16), channel_id=1, replica_groups={{192,193,194,195,196,197,198,199,448,449,450,451,452,453,454,455,704,70..., dimensions={0} | all-to-all | bytes 131072 | tf_op jit(solution)/shard_map/all_to_all | solution.py:584
  135.1 2.6 %shard_map.56 = (f32[6,2,2,32]{3,2,1,0:T(2,128)}, f32[1024,128]{1,0:T(8,128)}) custom-call(s32[3]{0:T(128)} %pad_add_fusion.flags, s32[4,2,2,32]{3,2,1,0:T(2,128)} %counts_ref.5, f32[128,128]{1,0:T(8,128)S(1)} %bitcast.15, f32[6,16,128]{2,1,0:T(8,128)S(1)} %get-tuple-element.39.v0, f32[6,16,128]{2,1,0:T(8,128)S(1)} %get-tuple-element.40.v1, ...), custom_call_target="tpu_custom_call" | custom-call | tf_op jit(solution)/shard_map/pallas_call | solution.py:498
  (18 shorter events, 1.8 us)
Async XLA Ops:
  0.6 37.9 %copy-start = (f32[4,2,2,32,2,128]{5,4,3,2,1,0:T(2,128)S(1)}, f32[4,2,2,32,2,128]{5,4,3,2,1,0:T(2,128)}, u32[]{:S(2)}) copy-start(f32[4,2,2,32,2,128]{5,4,3,2,1,0:T(2,128)} %param.4) | copy-start | bytes 1572868
  0.6 37.9 %copy-start.1 = (f32[4,2,2,32,2,128]{5,4,3,2,1,0:T(2,128)S(1)}, f32[4,2,2,32,2,128]{5,4,3,2,1,0:T(2,128)}, u32[]{:S(2)}) copy-start(f32[4,2,2,32,2,128]{5,4,3,2,1,0:T(2,128)} %param.3) | copy-start | bytes 1572868
  1.7 25.5 %collective-permute-start.1 = (f32[192,128]{1,0:T(8,128)S(1)}, f32[192,128]{1,0:T(8,128)S(1)}, u32[]{:S(2)}, u32[]{:S(2)}) collective-permute-start(f32[192,128]{1,0:T(8,128)S(1)} %get-tuple-element.33), channel_id=1, source_target_pairs={{64,112},{128,176},{192,240},{256,304},{320,368},{384,432},{448,49... | collective-permute-start | bytes 294920 | tf_op jit(solution)/shard_map/ppermute | solution.py:545
  6.4 30.8 %collective-permute-start = (f32[192,128]{1,0:T(8,128)S(1)}, f32[192,128]{1,0:T(8,128)S(1)}, u32[]{:S(2)}, u32[]{:S(2)}) collective-permute-start(f32[192,128]{1,0:T(8,128)S(1)} %get-tuple-element.27), channel_id=1, source_target_pairs={{8,0},{16,8},{24,16},{32,24},{40,32},{48,40},{56,48},{64,56},{72,6... | collective-permute-start | bytes 294920 | tf_op jit(solution)/shard_map/ppermute | solution.py:512
  27.2 10.7 %collective-permute-start.3 = (f32[192,128]{1,0:T(8,128)S(1)}, f32[192,128]{1,0:T(8,128)S(1)}, u32[]{:S(2)}, u32[]{:S(2)}) collective-permute-start(f32[192,128]{1,0:T(8,128)S(1)} %collective-permute-done.1), channel_id=1, source_target_pairs={{112,56},{176,120},{240,184},{304,248},{368,312},{432,376},{496,44... | collective-permute-start | bytes 294920 | tf_op jit(solution)/shard_map/ppermute | solution.py:547
  29.5 8.4 %collective-permute-start.4 = (f32[128,128]{1,0:T(8,128)S(1)}, f32[128,128]{1,0:T(8,128)S(1)}, u32[]{:S(2)}, u32[]{:S(2)}) collective-permute-start(f32[128,128]{1,0:T(8,128)S(1)} %get-tuple-element.35), channel_id=1, source_target_pairs={{1,0},{2,1},{3,2},{4,3},{5,4},{6,5},{7,6},{9,8},{10,9},{11,10},{12... | collective-permute-start | bytes 196616 | tf_op jit(solution)/shard_map/ppermute | solution.py:512
  30.8 7.1 %collective-permute-start.5 = (f32[136,128]{1,0:T(8,128)S(1)}, f32[136,128]{1,0:T(8,128)S(1)}, u32[]{:S(2)}, u32[]{:S(2)}) collective-permute-start(f32[136,128]{1,0:T(8,128)S(1)} %get-tuple-element.36), channel_id=1, source_target_pairs={{0,1},{1,2},{2,3},{3,4},{4,5},{5,6},{6,7},{8,9},{9,10},{10,11},{11... | collective-permute-start | bytes 208904 | tf_op jit(solution)/shard_map/ppermute | solution.py:512
  35.3 3.2 %collective-permute-start.2 = (f32[192,128]{1,0:T(8,128)S(1)}, f32[192,128]{1,0:T(8,128)S(1)}, u32[]{:S(2)}, u32[]{:S(2)}) collective-permute-start(f32[192,128]{1,0:T(8,128)S(1)} %get-tuple-element.33), channel_id=1, source_target_pairs={{8,0},{16,8},{24,16},{32,24},{40,32},{48,40},{56,48},{72,64},{80,7... | collective-permute-start | bytes 294920 | tf_op jit(solution)/shard_map/ppermute | solution.py:549
  40.1 49.7 %copy-start.2 = (f32[16,128,128]{2,1,0:T(8,128)}, f32[16,128,128]{2,1,0:T(8,128)S(1)}, u32[]{:S(2)}) copy-start(f32[16,128,128]{2,1,0:T(8,128)S(1)} %get-tuple-element.42.kept_hbm) | copy-start | bytes 3145732
  40.1 19.2 %collective-permute-start.6 = (f32[64,128]{1,0:T(8,128)S(1)}, f32[64,128]{1,0:T(8,128)S(1)}, u32[]{:S(2)}, u32[]{:S(2)}) collective-permute-start(f32[64,128]{1,0:T(8,128)S(1)} %get-tuple-element.37), channel_id=1, source_target_pairs={{64,0},{72,8},{80,16},{88,24},{128,64},{136,72},{144,80},{152,88},... | collective-permute-start | bytes 98312 | tf_op jit(solution)/shard_map/ppermute | solution.py:561
  59.3 3.2 %collective-permute-start.8 = (f32[128,128]{1,0:T(8,128)S(1)}, f32[128,128]{1,0:T(8,128)S(1)}, u32[]{:S(2)}, u32[]{:S(2)}) collective-permute-start(f32[128,128]{1,0:T(8,128)S(1)} %constant_dynamic-update-slice_fusion.both), channel_id=1, source_target_pairs={{0,1},{1,2},{2,3},{3,4},{4,5},{5,6},{6,7},{8,9},{9,10},{10,11},{11... | collective-permute-start | bytes 196616 | tf_op jit(solution)/shard_map/ppermute | solution.py:512
  60.6 6.2 %collective-permute-start.7 = (f32[128,128]{1,0:T(8,128)S(1)}, f32[128,128]{1,0:T(8,128)S(1)}, u32[]{:S(2)}, u32[]{:S(2)}) collective-permute-start(f32[128,128]{1,0:T(8,128)S(1)} %constant_dynamic-update-slice_fusion.both), channel_id=1, source_target_pairs={{1,0},{2,1},{3,2},{4,3},{5,4},{6,5},{7,6},{9,8},{10,9},{11,10},{12... | collective-permute-start | bytes 196616 | tf_op jit(solution)/shard_map/ppermute | solution.py:512
  90.7 5.1 %collective-permute-start.10 = (f32[6,16,128]{2,1,0:T(8,128)S(1)}, f32[6,16,128]{2,1,0:T(8,128)S(1)}, u32[]{:S(2)}, u32[]{:S(2)}) collective-permute-start(f32[6,16,128]{2,1,0:T(8,128)S(1)} %get-tuple-element.41.v2), channel_id=1, source_target_pairs={{0,1},{1,2},{2,3},{3,4},{4,5},{5,6},{6,7},{8,9},{9,10},{10,11},{11... | collective-permute-start | bytes 147464 | tf_op jit(solution)/shard_map/ppermute | solution.py:512
  94.1 6.0 %collective-permute-start.9 = (f32[6,16,128]{2,1,0:T(8,128)S(1)}, f32[6,16,128]{2,1,0:T(8,128)S(1)}, u32[]{:S(2)}, u32[]{:S(2)}) collective-permute-start(f32[6,16,128]{2,1,0:T(8,128)S(1)} %get-tuple-element.41.v2), channel_id=1, source_target_pairs={{1,0},{2,1},{3,2},{4,3},{5,4},{6,5},{7,6},{9,8},{10,9},{11,10},{12... | collective-permute-start | bytes 147464 | tf_op jit(solution)/shard_map/ppermute | solution.py:512

commit v6 on v5

--- a/solution.py
+++ b/solution.py
@@ -49,11 +49,15 @@
     return jnp.concatenate(cells, axis=1).astype(jnp.float32)
 
 
-def live_counts(flags, counts_ref):
+def live_counts(counts_ref, sizes):
+    n_sec, n_row = sizes
     row_zero, sec_zero = lane_bits((1, 128))
     lane = lax.broadcasted_iota(jnp.int32, (1, 128), 1)
-    last_row = flags[0] == 1
-    last_sec = flags[1] == 1
+    section = 0
+    for axis in SEC_AXES:
+        section = section * lax.axis_size(axis) + lax.axis_index(axis)
+    last_row = lax.axis_index("row") == n_row - 1
+    last_sec = section == n_sec - 1
     zero = jnp.zeros((1, 128), jnp.float32)
     counts = [counts_row(counts_ref, kind) for kind in range(4)]
     return [
@@ -88,7 +92,7 @@
     return F, G, C, s1, s2
 
 
-def gram_kernel(flags, f_ref, g_ref, counts_ref, up_ref, rest_ref, outside_ref, next_ref, low_ref, packet, kept):
+def gram_kernel(f_ref, g_ref, alive_ref, up_ref, rest_ref, outside_ref, next_ref, low_ref, packet, kept):
     row_zero, sec_zero = lane_bits((1, 128))
 
     def pair_rows(ref, start, count, comp):
@@ -98,7 +102,7 @@
         return [pair_rows(ref, kind * 128, 128, comp).T for comp in range(2)]
 
     zero = jnp.zeros((1, 128), jnp.float32)
-    alive = live_counts(flags, counts_ref)
+    alive = [alive_ref[kind : kind + 1, :] for kind in range(4)]
 
     def masked(points, count):
         live = live_points(count)
@@ -203,7 +207,7 @@
         copy.wait()
 
 
-def pack_rows_kernel(f_ref, g_ref, counts_ref, beside, odd, sems):
+def pack_rows_kernel(sizes, f_ref, g_ref, counts_ref, beside, odd, alive, sems):
     copies = [
         pltpu.make_async_copy(g_ref.at[pl.ds(256, 64)], beside.at[pl.ds(0, 64)], sems.at[0]),
         pltpu.make_async_copy(g_ref.at[pl.ds(384, 64)], beside.at[pl.ds(64, 64)], sems.at[1]),
@@ -213,6 +217,9 @@
     for copy in copies:
         copy.start()
     odd[128:136, :] = jnp.broadcast_to(counts_row(counts_ref, 1), (8, 128))
+    for kind, row in enumerate(live_counts(counts_ref, sizes)):
+        alive[kind : kind + 1, :] = row
+    alive[4:8, :] = jnp.zeros((4, 128), jnp.float32)
     for copy in copies:
         copy.wait()
 
@@ -430,14 +437,14 @@
     return [value * (1.0 / SPAN) for value in x]
 
 
-def finish_kernel(flags, counts_ref, sums, v0, v1, v2, v3, n0, n1, n2, n3, kept, affines, residual_hbm, residual, sems):
+def finish_kernel(alive_ref, sums, v0, v1, v2, v3, n0, n1, n2, n3, kept, affines_hbm, residual_hbm, affines, residual, sems):
     stores = []
     total = jnp.sum(sums[...], axis=0, keepdims=True)
     lane = lax.broadcasted_iota(jnp.int32, (1, 128), 1)
     moments = [jnp.sum(jnp.where(lane == n, total, 0.0), axis=1, keepdims=True) for n in range(8)]
     weights = coefficients(moments)
-    at = flags[2]
-    alive = live_counts(flags, counts_ref)
+    at = lax.axis_index("x") * lax.axis_size("core") + lax.axis_index("core")
+    alive = [alive_ref[kind : kind + 1, :] for kind in range(4)]
     row_zero, sec_zero = lane_bits((1, 128))
 
     def mix(refs, i, dev):
@@ -452,6 +459,8 @@
             for row in range(2):
                 start = 64 * sec + 32 * row
                 affines[i, sec, row : row + 1, :] = x[i][:, start : start + 32]
+    stores.append(pltpu.make_async_copy(affines, affines_hbm, sems.at[4]))
+    stores[-1].start()
     for kind in range(4):
         if kind == 0:
             b = [roll(z, -1, 1) for z in x]
@@ -516,8 +525,9 @@
     return run(pack_up_kernel, [(192, 128), (192, 128)], g, anywhere=(0,), copies=3)
 
 
-def pack_rows(run, f, g, counts):
-    return run(pack_rows_kernel, [(128, 128), (136, 128)], f, g, counts, anywhere=(0, 1), copies=4)
+def pack_rows(run, f, g, counts, sizes):
+    kernel = functools.partial(pack_rows_kernel, sizes)
+    return run(kernel, [(128, 128), (136, 128), (8, 128)], f, g, counts, anywhere=(0, 1), copies=4)
 
 
 def per_device(interpret, first_pts, second_pts, counts):
@@ -525,17 +535,8 @@
     n_sec = lax.axis_size(SEC_AXES)
     n_dev = lax.axis_size(GROUP)
     n_group = n_sec // n_dev
-    sec = lax.axis_index(SEC_AXES)
     f = first_pts.reshape(1024, 128)
     g = second_pts.reshape(1024, 128)
-    flags = jnp.stack(
-        [
-            (lax.axis_index("row") == lax.axis_size("row") - 1).astype(jnp.int32),
-            (sec == n_sec - 1).astype(jnp.int32),
-            lax.axis_index(GROUP).astype(jnp.int32),
-        ]
-    )
-
     up, rest = pack_up(run, g)
     up = shifted(up, SEC_AXES, -1)
     relay = n_dev - 2
@@ -545,11 +546,12 @@
     relayed = lax.ppermute(rest, SEC_AXES, to_relay)
     relayed, f_later, g_later = lax.optimization_barrier((relayed, f, g))
     outside = lax.ppermute(relayed, SEC_AXES, from_relay)
-    beside, odd, rest = lax.optimization_barrier((*pack_rows(run, f_later, g_later, counts), rest))
-    rest = lax.ppermute(rest, SEC_AXES, inside)
+    sizes = (n_sec, lax.axis_size("row"))
+    beside, odd, alive, rest = lax.optimization_barrier((*pack_rows(run, f_later, g_later, counts, sizes), rest))
     beside = shifted(beside, "row", -1)
     low = shifted(odd, "row", 1)
-    packet, kept = run(gram_kernel, [(ROWS, 128), (16, 128, 128)], flags, f, g, counts, up, rest, outside, beside, low, scalars=1)
+    rest = lax.ppermute(rest, SEC_AXES, inside)
+    packet, kept = run(gram_kernel, [(ROWS, 128), (16, 128, 128)], f, g, alive, up, rest, outside, beside, low)
 
     half = n_dev // 2
     pairs = []
@@ -587,8 +589,7 @@
     affines, residual = run(
         finish_kernel,
         [(6,) + counts.shape[1:], (1024, 128)],
-        flags,
-        counts,
+        alive,
         sums.reshape(n_other, 128),
         v0,
         v1,
@@ -599,20 +600,21 @@
         e2,
         e3,
         kept,
-        scalars=1,
-        copies=4,
-        buffers=[(1024, 128)],
-        results=[pltpu.VMEM, pl.ANY],
+        copies=5,
+        buffers=[(6,) + counts.shape[1:], (1024, 128)],
+        results=[pl.ANY, pl.ANY],
     )
     return affines, residual.reshape(first_pts.shape)
 
 
 def sum_groups(sizes):
     n_y, n_zhi, n_x, n_core, n_row = sizes
+    n_z = n_zhi * n_row
+    first = 5 * n_z // 8
     groups = []
     for place in range(n_x * n_core):
-        order = [((n_zhi - 1 + step) % n_zhi, y, row) for step in range(n_zhi) for y in range(n_y) for row in range(n_row)]
-        groups.append([((y * n_zhi + zhi) * n_x * n_core + place) * n_row + row for zhi, y, row in order])
+        order = [((first + step) % n_z, y) for step in range(n_z) for y in reversed(range(n_y))]
+        groups.append([((y * n_zhi + z // n_row) * n_x * n_core + place) * n_row + z % n_row for z, y in order])
     return groups
 
 

time: 140 us -> 137 us (0.979); the launches traced: 138 us -> 136 us
  waiting for transfers between devices: 21.3 us -> 25.5 us
  starting transfers between devices: 49.2 us -> 47.1 us
  Pallas kernels: 9.02 us -> 7.12 us
    ppermute x7, waiting for transfers between devices: 10.2 us -> 15 us  [shifted(): return lax.ppermute(value, axes, pairs)]
    all_to_all x1, blocking collectives: 22.8 us -> 20.8 us  [per_device(): lax.all_to_all(jnp.broadcast_to(mine[None], (n_dev, 2 * DOUBLE, 128)), GR...]
    pallas_call x7, Pallas kernels: 9.02 us -> 7.12 us  [call(): pl.pallas_call(kernel, out_shape=shapes, in_specs=spaces, out_specs=[pl.B...]
    ppermute x7, starting transfers between devices: 33.9 us -> 32.1 us  [shifted(): return lax.ppermute(value, axes, pairs)]
where the time goes in v6:
time: 137 us; the launch traced here: 136 us
  blocking collectives  55.6 us (41%)
  starting transfers between devices  47.1 us (34%)
  waiting for transfers between devices  25.5 us (19%)
  Pallas kernels  7.12 us (5%)
    all_to_all x1, blocking collectives, per_device(): lax.all_to_all(jnp.broadcast_to(part[None], (n_other, 1, 128)), EVERY, 0,...  34.7 us
    ppermute x7, starting transfers between devices, shifted(): return lax.ppermute(value, axes, pairs)  32.1 us
    all_to_all x1, blocking collectives, per_device(): lax.all_to_all(jnp.broadcast_to(mine[None], (n_dev, 2 * DOUBLE, 128)), GR...  20.8 us
    ppermute x7, waiting for transfers between devices, shifted(): return lax.ppermute(value, axes, pairs)  15 us
    ppermute x1, waiting for transfers between devices, per_device(): other = lax.ppermute(packet, SEC_AXES, pairs)  10.5 us
    ppermute x1, starting transfers between devices, per_device(): other = lax.ppermute(packet, SEC_AXES, pairs)  8.45 us
    pallas_call x7, Pallas kernels, call(): pl.pallas_call(kernel, out_shape=shapes, in_specs=spaces, out_specs=[pl.B...  7.12 us
    ppermute x1, starting transfers between devices, per_device(): relayed = lax.ppermute(rest, SEC_AXES, to_relay)  4.67 us
  transfers between devices with their start and end apart: 11, of which 7 were waited for; matrix products, arithmetic and copies ran while one was open for 0% of the time, Pallas kernels for 1%

profile of v6, /device:TPU:24, one launch (start us, length us, event | category | flops | bytes accessed | tf_op | source)
XLA Modules:
  0.0 136.3 jit_solution(6566740765578188204)
XLA Ops:
  0.7 1.1 shard_map.50
  1.7 4.7 %collective-permute-start = (f32[192,128]{1,0:T(8,128)S(1)}, f32[192,128]{1,0:T(8,128)S(1)}, u32[]{:S(2)}, u32[]{:S(2)}) collective-permute-start(f32[192,128]{1,0:T(8,128)S(1)} %get-tuple-element.37), channel_id=1, source_target_pairs={{64,112},{128,176},{192,240},{256,304},{320,368},{384,432},{448,49... | collective-permute-start | bytes 294920 | tf_op jit(solution)/shard_map/ppermute | solution.py:546
  6.4 20.8 %collective-permute-start.1 = (f32[192,128]{1,0:T(8,128)S(1)}, f32[192,128]{1,0:T(8,128)S(1)}, u32[]{:S(2)}, u32[]{:S(2)}) collective-permute-start(f32[192,128]{1,0:T(8,128)S(1)} %get-tuple-element.36), channel_id=1, source_target_pairs={{8,0},{16,8},{24,16},{32,24},{40,32},{48,40},{56,48},{64,56},{72,6... | collective-permute-start | bytes 294920 | tf_op jit(solution)/shard_map/ppermute | solution.py:521
  27.2 0.7 collective-permute-start.3
  27.9 1.5 %shard_map.51 = (f32[128,128]{1,0:T(8,128)S(1)}, f32[136,128]{1,0:T(8,128)S(1)}, f32[8,128]{1,0:T(8,128)S(1)}) custom-call(f32[1024,128]{1,0:T(8,128)} %bitcast.10, f32[1024,128]{1,0:T(8,128)} %bitcast.7, s32[4,2,2,32]{3,2,1,0:T(2,128)} %counts_ref.1), custom_call_target="tpu_custom_call" | custom-call | tf_op jit(solution)/shard_map/pallas_call | solution.py:507
  29.4 1.3 collective-permute-start.2
  30.7 2.9 %collective-permute-start.5 = (f32[136,128]{1,0:T(8,128)S(1)}, f32[136,128]{1,0:T(8,128)S(1)}, u32[]{:S(2)}, u32[]{:S(2)}) collective-permute-start(f32[136,128]{1,0:T(8,128)S(1)} %get-tuple-element.40), channel_id=1, source_target_pairs={{0,1},{1,2},{2,3},{3,4},{4,5},{5,6},{6,7},{8,9},{9,10},{10,11},{11... | collective-permute-start | bytes 208904 | tf_op jit(solution)/shard_map/ppermute | solution.py:521
  33.7 1.3 collective-permute-start.4
  35.0 1.9 %collective-permute-done.1.up_ref = f32[192,128]{1,0:T(8,128)S(1)} collective-permute-done((f32[192,128]{1,0:T(8,128)S(1)}, f32[192,128]{1,0:T(8,128)S(1)}, u32[]{:S(2)}, u32[]{:S(2)}) %collective-permute-start.1) | collective-permute-done | bytes 98336 | tf_op jit(solution)/shard_map/ppermute | solution.py:521
  36.9 3.5 %collective-permute-done.4.next_ref = f32[128,128]{1,0:T(8,128)S(1)} collective-permute-done((f32[128,128]{1,0:T(8,128)S(1)}, f32[128,128]{1,0:T(8,128)S(1)}, u32[]{:S(2)}, u32[]{:S(2)}) %collective-permute-start.4) | collective-permute-done | bytes 65568 | tf_op jit(solution)/shard_map/ppermute | solution.py:521
  40.4 0.8 shard_map.52
  41.3 8.4 %collective-permute-start.6 = (f32[64,128]{1,0:T(8,128)S(1)}, f32[64,128]{1,0:T(8,128)S(1)}, u32[]{:S(2)}, u32[]{:S(2)}) collective-permute-start(f32[64,128]{1,0:T(8,128)S(1)} %get-tuple-element.41), channel_id=1, source_target_pairs={{64,0},{72,8},{80,16},{88,24},{128,64},{136,72},{144,80},{152,88},... | collective-permute-start | bytes 98312 | tf_op jit(solution)/shard_map/ppermute | solution.py:563
  49.8 10.5 %collective-permute-done.6 = f32[64,128]{1,0:T(8,128)S(1)} collective-permute-done((f32[64,128]{1,0:T(8,128)S(1)}, f32[64,128]{1,0:T(8,128)S(1)}, u32[]{:S(2)}, u32[]{:S(2)}) %collective-permute-start.6) | collective-permute-done | bytes 32800 | tf_op jit(solution)/shard_map/ppermute | solution.py:563
  60.3 1.3 collective-permute-start.8
  61.6 1.3 collective-permute-start.7
  63.5 4.3 %collective-permute-done.7.above = f32[128,128]{1,0:T(8,128)S(1)} collective-permute-done((f32[128,128]{1,0:T(8,128)S(1)}, f32[128,128]{1,0:T(8,128)S(1)}, u32[]{:S(2)}, u32[]{:S(2)}) %collective-permute-start.7) | collective-permute-done | bytes 65568 | tf_op jit(solution)/shard_map/ppermute | solution.py:521
  67.9 20.8 %all_to_all.10 = f32[8,288,128]{2,1,0:T(8,128)S(1)} all-to-all(f32[8,288,128]{2,1,0:T(8,128)S(1)} %broadcast_in_dim.6), channel_id=1, replica_groups=mesh['y'=4,'zhi'=4,'x'=4,'core'=2,'row'=8] {'x','core'}, dimensions={0} | all-to-all | bytes 2359296 | tf_op jit(solution)/shard_map/all_to_all | solution.py:566
  88.8 1.0 shard_map.54
  89.8 3.2 %collective-permute-start.10 = (f32[6,16,128]{2,1,0:T(8,128)S(1)}, f32[6,16,128]{2,1,0:T(8,128)S(1)}, u32[]{:S(2)}, u32[]{:S(2)}) collective-permute-start(f32[6,16,128]{2,1,0:T(8,128)S(1)} %get-tuple-element.45.v2), channel_id=1, source_target_pairs={{0,1},{1,2},{2,3},{3,4},{4,5},{5,6},{6,7},{8,9},{9,10},{10,11},{11... | collective-permute-start | bytes 147464 | tf_op jit(solution)/shard_map/ppermute | solution.py:521
  93.0 1.3 collective-permute-start.9
  94.7 4.3 %collective-permute-done.9.above = f32[6,16,128]{2,1,0:T(8,128)S(1)} collective-permute-done((f32[6,16,128]{2,1,0:T(8,128)S(1)}, f32[6,16,128]{2,1,0:T(8,128)S(1)}, u32[]{:S(2)}, u32[]{:S(2)}) %collective-permute-start.9) | collective-permute-done | bytes 49184 | tf_op jit(solution)/shard_map/ppermute | solution.py:521
  99.0 1.2 shard_map.55
  100.3 34.7 %all_to_all.11 = f32[128,1,128]{2,1,0:T(1,128)S(1)} all-to-all(f32[128,1,128]{2,1,0:T(1,128)S(1)} %broadcast_in_dim.16), channel_id=1, replica_groups={{900,644,388,132,901,645,389,133,902,646,390,134,903,647,391,135,960,70..., dimensions={0} | all-to-all | bytes 131072 | tf_op jit(solution)/shard_map/all_to_all | solution.py:586
  135.0 1.3 shard_map.56
  (17 shorter events, 1.2 us)
Async XLA Ops:
  0.6 39.8 %copy-start = (f32[4,2,2,32,2,128]{5,4,3,2,1,0:T(2,128)S(1)}, f32[4,2,2,32,2,128]{5,4,3,2,1,0:T(2,128)}, u32[]{:S(2)}) copy-start(f32[4,2,2,32,2,128]{5,4,3,2,1,0:T(2,128)} %param.4) | copy-start | bytes 1572868
  0.6 39.8 %copy-start.1 = (f32[4,2,2,32,2,128]{5,4,3,2,1,0:T(2,128)S(1)}, f32[4,2,2,32,2,128]{5,4,3,2,1,0:T(2,128)}, u32[]{:S(2)}) copy-start(f32[4,2,2,32,2,128]{5,4,3,2,1,0:T(2,128)} %param.3) | copy-start | bytes 1572868
  1.7 25.5 %collective-permute-start = (f32[192,128]{1,0:T(8,128)S(1)}, f32[192,128]{1,0:T(8,128)S(1)}, u32[]{:S(2)}, u32[]{:S(2)}) collective-permute-start(f32[192,128]{1,0:T(8,128)S(1)} %get-tuple-element.37), channel_id=1, source_target_pairs={{64,112},{128,176},{192,240},{256,304},{320,368},{384,432},{448,49... | collective-permute-start | bytes 294920 | tf_op jit(solution)/shard_map/ppermute | solution.py:546
  6.4 30.5 %collective-permute-start.1 = (f32[192,128]{1,0:T(8,128)S(1)}, f32[192,128]{1,0:T(8,128)S(1)}, u32[]{:S(2)}, u32[]{:S(2)}) collective-permute-start(f32[192,128]{1,0:T(8,128)S(1)} %get-tuple-element.36), channel_id=1, source_target_pairs={{8,0},{16,8},{24,16},{32,24},{40,32},{48,40},{56,48},{64,56},{72,6... | collective-permute-start | bytes 294920 | tf_op jit(solution)/shard_map/ppermute | solution.py:521
  27.2 13.2 %collective-permute-start.3 = (f32[192,128]{1,0:T(8,128)S(1)}, f32[192,128]{1,0:T(8,128)S(1)}, u32[]{:S(2)}, u32[]{:S(2)}) collective-permute-start(f32[192,128]{1,0:T(8,128)S(1)} %collective-permute-done), channel_id=1, source_target_pairs={{112,56},{176,120},{240,184},{304,248},{368,312},{432,376},{496,44... | collective-permute-start | bytes 294920 | tf_op jit(solution)/shard_map/ppermute | solution.py:548
  29.4 11.0 %collective-permute-start.2 = (f32[192,128]{1,0:T(8,128)S(1)}, f32[192,128]{1,0:T(8,128)S(1)}, u32[]{:S(2)}, u32[]{:S(2)}) collective-permute-start(f32[192,128]{1,0:T(8,128)S(1)} %get-tuple-element.37), channel_id=1, source_target_pairs={{8,0},{16,8},{24,16},{32,24},{40,32},{48,40},{56,48},{72,64},{80,7... | collective-permute-start | bytes 294920 | tf_op jit(solution)/shard_map/ppermute | solution.py:553
  30.7 9.7 %collective-permute-start.5 = (f32[136,128]{1,0:T(8,128)S(1)}, f32[136,128]{1,0:T(8,128)S(1)}, u32[]{:S(2)}, u32[]{:S(2)}) collective-permute-start(f32[136,128]{1,0:T(8,128)S(1)} %get-tuple-element.40), channel_id=1, source_target_pairs={{0,1},{1,2},{2,3},{3,4},{4,5},{5,6},{6,7},{8,9},{9,10},{10,11},{11... | collective-permute-start | bytes 208904 | tf_op jit(solution)/shard_map/ppermute | solution.py:521
  33.7 6.7 %collective-permute-start.4 = (f32[128,128]{1,0:T(8,128)S(1)}, f32[128,128]{1,0:T(8,128)S(1)}, u32[]{:S(2)}, u32[]{:S(2)}) collective-permute-start(f32[128,128]{1,0:T(8,128)S(1)} %get-tuple-element.39), channel_id=1, source_target_pairs={{1,0},{2,1},{3,2},{4,3},{5,4},{6,5},{7,6},{9,8},{10,9},{11,10},{12... | collective-permute-start | bytes 196616 | tf_op jit(solution)/shard_map/ppermute | solution.py:521
  41.3 47.5 %copy-start.2 = (f32[16,128,128]{2,1,0:T(8,128)}, f32[16,128,128]{2,1,0:T(8,128)S(1)}, u32[]{:S(2)}) copy-start(f32[16,128,128]{2,1,0:T(8,128)S(1)} %get-tuple-element.46.kept_hbm) | copy-start | bytes 3145732
  41.3 19.0 %collective-permute-start.6 = (f32[64,128]{1,0:T(8,128)S(1)}, f32[64,128]{1,0:T(8,128)S(1)}, u32[]{:S(2)}, u32[]{:S(2)}) collective-permute-start(f32[64,128]{1,0:T(8,128)S(1)} %get-tuple-element.41), channel_id=1, source_target_pairs={{64,0},{72,8},{80,16},{88,24},{128,64},{136,72},{144,80},{152,88},... | collective-permute-start | bytes 98312 | tf_op jit(solution)/shard_map/ppermute | solution.py:563
  60.3 3.2 %collective-permute-start.8 = (f32[128,128]{1,0:T(8,128)S(1)}, f32[128,128]{1,0:T(8,128)S(1)}, u32[]{:S(2)}, u32[]{:S(2)}) collective-permute-start(f32[128,128]{1,0:T(8,128)S(1)} %constant_dynamic-update-slice_fusion.both), channel_id=1, source_target_pairs={{0,1},{1,2},{2,3},{3,4},{4,5},{5,6},{6,7},{8,9},{9,10},{10,11},{11... | collective-permute-start | bytes 196616 | tf_op jit(solution)/shard_map/ppermute | solution.py:521
  61.6 6.2 %collective-permute-start.7 = (f32[128,128]{1,0:T(8,128)S(1)}, f32[128,128]{1,0:T(8,128)S(1)}, u32[]{:S(2)}, u32[]{:S(2)}) collective-permute-start(f32[128,128]{1,0:T(8,128)S(1)} %constant_dynamic-update-slice_fusion.both), channel_id=1, source_target_pairs={{1,0},{2,1},{3,2},{4,3},{5,4},{6,5},{7,6},{9,8},{10,9},{11,10},{12... | collective-permute-start | bytes 196616 | tf_op jit(solution)/shard_map/ppermute | solution.py:521
  89.8 4.9 %collective-permute-start.10 = (f32[6,16,128]{2,1,0:T(8,128)S(1)}, f32[6,16,128]{2,1,0:T(8,128)S(1)}, u32[]{:S(2)}, u32[]{:S(2)}) collective-permute-start(f32[6,16,128]{2,1,0:T(8,128)S(1)} %get-tuple-element.45.v2), channel_id=1, source_target_pairs={{0,1},{1,2},{2,3},{3,4},{4,5},{5,6},{6,7},{8,9},{9,10},{10,11},{11... | collective-permute-start | bytes 147464 | tf_op jit(solution)/shard_map/ppermute | solution.py:521
  93.0 6.0 %collective-permute-start.9 = (f32[6,16,128]{2,1,0:T(8,128)S(1)}, f32[6,16,128]{2,1,0:T(8,128)S(1)}, u32[]{:S(2)}, u32[]{:S(2)}) collective-permute-start(f32[6,16,128]{2,1,0:T(8,128)S(1)} %get-tuple-element.45.v2), channel_id=1, source_target_pairs={{1,0},{2,1},{3,2},{4,3},{5,4},{6,5},{7,6},{9,8},{10,9},{11,10},{12... | collective-permute-start | bytes 147464 | tf_op jit(solution)/shard_map/ppermute | solution.py:521

commit v7 on v6

--- a/solution.py
+++ b/solution.py
@@ -207,19 +207,22 @@
         copy.wait()
 
 
-def pack_rows_kernel(sizes, f_ref, g_ref, counts_ref, beside, odd, alive, sems):
+def pack_rows_kernel(sizes, f_ref, g_ref, counts_hbm, beside, odd, alive, counts_ref, sems):
     copies = [
         pltpu.make_async_copy(g_ref.at[pl.ds(256, 64)], beside.at[pl.ds(0, 64)], sems.at[0]),
         pltpu.make_async_copy(g_ref.at[pl.ds(384, 64)], beside.at[pl.ds(64, 64)], sems.at[1]),
         pltpu.make_async_copy(f_ref.at[pl.ds(320, 64)], odd.at[pl.ds(0, 64)], sems.at[2]),
         pltpu.make_async_copy(f_ref.at[pl.ds(448, 64)], odd.at[pl.ds(64, 64)], sems.at[3]),
     ]
+    fetch = pltpu.make_async_copy(counts_hbm, counts_ref, sems.at[4])
+    fetch.start()
     for copy in copies:
         copy.start()
-    odd[128:136, :] = jnp.broadcast_to(counts_row(counts_ref, 1), (8, 128))
+    fetch.wait()
     for kind, row in enumerate(live_counts(counts_ref, sizes)):
         alive[kind : kind + 1, :] = row
     alive[4:8, :] = jnp.zeros((4, 128), jnp.float32)
+    odd[128:136, :] = jnp.broadcast_to(counts_row(counts_ref, 1), (8, 128))
     for copy in copies:
         copy.wait()
 
@@ -311,7 +314,9 @@
         return outs
 
 
-def window_kernel(got, blocks, v0, e0, v1, e1, v2):
+def window_kernel(got, kept_hbm, blocks, v0, e0, v1, e1, v2, kept, sems):
+    fetch = pltpu.make_async_copy(kept_hbm, kept, sems.at[0])
+    fetch.start()
     n_dev = got.shape[0] // (2 * DOUBLE)
     row_zero, sec_zero = lane_bits((2 * n_dev, 128))
     zero = jnp.zeros((2 * n_dev, 128), jnp.float32)
@@ -363,11 +368,10 @@
         v1[i] = w[i]
         e1[i] = f[i]
         v2[i] = last[i]
-
-
-def moments_kernel(blocks, v0, v1, v2, above, below, kept_hbm, e2, v3, e3, out, kept, sems):
-    fetch = pltpu.make_async_copy(kept_hbm, kept, sems.at[0])
-    fetch.start()
+    fetch.wait()
+
+
+def moments_kernel(blocks, v0, v1, v2, above, below, e2, v3, e3, out):
     shape = v2.shape[1:]
     n_dev = shape[0] // 2
     bits = lane_bits(shape)
@@ -404,7 +408,6 @@
         value = jnp.sum(jnp.sum(value, axis=0, keepdims=True), axis=1, keepdims=True)
         packed = jnp.where(lane == n, value, packed)
     out[...] = packed
-    fetch.wait()
 
 
 def coefficients(moments):
@@ -509,7 +512,7 @@
         out_shape=shapes,
         in_specs=spaces,
         out_specs=[pl.BlockSpec(memory_space=space) for space in results],
-        scratch_shapes=[pltpu.VMEM(b, jnp.float32) for b in buffers]
+        scratch_shapes=list(buffers)
         + ([pltpu.SemaphoreType.DMA((copies,))] if copies else []),
         interpret=interpret,
     )(*args)
@@ -526,8 +529,16 @@
 
 
 def pack_rows(run, f, g, counts, sizes):
-    kernel = functools.partial(pack_rows_kernel, sizes)
-    return run(kernel, [(128, 128), (136, 128), (8, 128)], f, g, counts, anywhere=(0, 1), copies=4)
+    return run(
+        functools.partial(pack_rows_kernel, sizes),
+        [(128, 128), (136, 128), (8, 128)],
+        f,
+        g,
+        counts,
+        anywhere=(0, 1, 2),
+        copies=5,
+        buffers=[pltpu.VMEM(counts.shape, jnp.int32)],
+    )
 
 
 def per_device(interpret, first_pts, second_pts, counts):
@@ -565,21 +576,23 @@
     (mine,) = run(merge_kernel, [(2 * DOUBLE, 128)], both, shifted(both, "row", -1), shifted(both, "row", 1))
     got = lax.all_to_all(jnp.broadcast_to(mine[None], (n_dev, 2 * DOUBLE, 128)), GROUP, 0, 0, tiled=False)
     wide = (6, 2 * n_dev, 128)
-    blocks, v0, e0, v1, e1, v2 = run(
-        window_kernel, [(93, 2 * n_dev, 128)] + [wide] * 5, got.reshape(n_dev * 2 * DOUBLE, 128)
+    blocks, v0, e0, v1, e1, v2, kept = run(
+        window_kernel,
+        [(93, 2 * n_dev, 128)] + [wide] * 5 + [(16, 128, 128)],
+        got.reshape(n_dev * 2 * DOUBLE, 128),
+        kept,
+        anywhere=(1,),
+        copies=1,
     )
-    e2, v3, e3, part, kept = run(
+    e2, v3, e3, part = run(
         moments_kernel,
-        [wide, wide, wide, (1, 128), (16, 128, 128)],
+        [wide, wide, wide, (1, 128)],
         blocks,
         v0,
         v1,
         v2,
         shifted(v2, "row", -1),
         shifted(v2, "row", 1),
-        kept,
-        anywhere=(6,),
-        copies=1,
     )
     n_other = lax.axis_size(OTHERS)
     groups = sum_groups([lax.axis_size(axis) for axis in EVERY])
@@ -601,7 +614,7 @@
         e3,
         kept,
         copies=5,
-        buffers=[(6,) + counts.shape[1:], (1024, 128)],
+        buffers=[pltpu.VMEM((6,) + counts.shape[1:], jnp.float32), pltpu.VMEM((1024, 128), jnp.float32)],
         results=[pl.ANY, pl.ANY],
     )
     return affines, residual.reshape(first_pts.shape)

time: 137 us -> 137 us (level)
  no operation moved by 1% of the time
where the time goes in v7:
time: 137 us; the launch traced here: 136 us
  blocking collectives  55.4 us (40%)
  starting transfers between devices  47.8 us (35%)
  waiting for transfers between devices  25.1 us (18%)
  Pallas kernels  6.74 us (5%)
    all_to_all x1, blocking collectives, per_device(): lax.all_to_all(jnp.broadcast_to(part[None], (n_other, 1, 128)), EVERY, 0,...  34.6 us
    ppermute x7, starting transfers between devices, shifted(): return lax.ppermute(value, axes, pairs)  32.3 us
    all_to_all x1, blocking collectives, per_device(): lax.all_to_all(jnp.broadcast_to(mine[None], (n_dev, 2 * DOUBLE, 128)), GR...  20.7 us
    ppermute x7, waiting for transfers between devices, shifted(): return lax.ppermute(value, axes, pairs)  15 us
    ppermute x1, waiting for transfers between devices, per_device(): other = lax.ppermute(packet, SEC_AXES, pairs)  10.1 us
    ppermute x1, starting transfers between devices, per_device(): other = lax.ppermute(packet, SEC_AXES, pairs)  8.89 us
    pallas_call x7, Pallas kernels, call(): pl.pallas_call(kernel, out_shape=shapes, in_specs=spaces, out_specs=[pl.B...  6.74 us
    ppermute x1, starting transfers between devices, per_device(): relayed = lax.ppermute(rest, SEC_AXES, to_relay)  4.67 us
  transfers between devices with their start and end apart: 11, of which 7 were waited for; matrix products, arithmetic and copies ran while one was open for 0% of the time, Pallas kernels for 1%

profile of v7, /device:TPU:24, one launch (start us, length us, event | category | flops | bytes accessed | tf_op | source)
XLA Modules:
  0.0 135.9 jit_solution(17023141608535957320)
XLA Ops:
  0.7 1.1 shard_map.50
  1.7 4.7 %collective-permute-start = (f32[192,128]{1,0:T(8,128)S(1)}, f32[192,128]{1,0:T(8,128)S(1)}, u32[]{:S(2)}, u32[]{:S(2)}) collective-permute-start(f32[192,128]{1,0:T(8,128)S(1)} %get-tuple-element.37), channel_id=1, source_target_pairs={{64,112},{128,176},{192,240},{256,304},{320,368},{384,432},{448,49... | collective-permute-start | bytes 294920 | tf_op jit(solution)/shard_map/ppermute | solution.py:557
  6.4 20.8 %collective-permute-start.1 = (f32[192,128]{1,0:T(8,128)S(1)}, f32[192,128]{1,0:T(8,128)S(1)}, u32[]{:S(2)}, u32[]{:S(2)}) collective-permute-start(f32[192,128]{1,0:T(8,128)S(1)} %get-tuple-element.36), channel_id=1, source_target_pairs={{8,0},{16,8},{24,16},{32,24},{40,32},{48,40},{56,48},{64,56},{72,6... | collective-permute-start | bytes 294920 | tf_op jit(solution)/shard_map/ppermute | solution.py:524
  27.2 0.7 collective-permute-start.3
  27.9 0.9 shard_map.51
  28.8 1.3 collective-permute-start.2
  30.1 2.9 %collective-permute-start.5 = (f32[136,128]{1,0:T(8,128)S(1)}, f32[136,128]{1,0:T(8,128)S(1)}, u32[]{:S(2)}, u32[]{:S(2)}) collective-permute-start(f32[136,128]{1,0:T(8,128)S(1)} %get-tuple-element.40), channel_id=1, source_target_pairs={{0,1},{1,2},{2,3},{3,4},{4,5},{5,6},{6,7},{8,9},{9,10},{10,11},{11... | collective-permute-start | bytes 208904 | tf_op jit(solution)/shard_map/ppermute | solution.py:524
  33.0 1.3 collective-permute-start.4
  34.3 2.6 %collective-permute-done.1.up_ref = f32[192,128]{1,0:T(8,128)S(1)} collective-permute-done((f32[192,128]{1,0:T(8,128)S(1)}, f32[192,128]{1,0:T(8,128)S(1)}, u32[]{:S(2)}, u32[]{:S(2)}) %collective-permute-start.1) | collective-permute-done | bytes 98336 | tf_op jit(solution)/shard_map/ppermute | solution.py:524
  36.9 2.8 %collective-permute-done.4.next_ref = f32[128,128]{1,0:T(8,128)S(1)} collective-permute-done((f32[128,128]{1,0:T(8,128)S(1)}, f32[128,128]{1,0:T(8,128)S(1)}, u32[]{:S(2)}, u32[]{:S(2)}) %collective-permute-start.4) | collective-permute-done | bytes 65568 | tf_op jit(solution)/shard_map/ppermute | solution.py:524
  39.8 0.8 shard_map.52
  40.6 8.9 %collective-permute-start.6 = (f32[64,128]{1,0:T(8,128)S(1)}, f32[64,128]{1,0:T(8,128)S(1)}, u32[]{:S(2)}, u32[]{:S(2)}) collective-permute-start(f32[64,128]{1,0:T(8,128)S(1)} %get-tuple-element.41), channel_id=1, source_target_pairs={{64,0},{72,8},{80,16},{88,24},{128,64},{136,72},{144,80},{152,88},... | collective-permute-start | bytes 98312 | tf_op jit(solution)/shard_map/ppermute | solution.py:574
  49.5 10.1 %collective-permute-done.6 = f32[64,128]{1,0:T(8,128)S(1)} collective-permute-done((f32[64,128]{1,0:T(8,128)S(1)}, f32[64,128]{1,0:T(8,128)S(1)}, u32[]{:S(2)}, u32[]{:S(2)}) %collective-permute-start.6) | collective-permute-done | bytes 32800 | tf_op jit(solution)/shard_map/ppermute | solution.py:574
  59.7 1.3 collective-permute-start.8
  60.9 1.3 collective-permute-start.7
  62.2 0.6 collective-permute-done.8.below
  62.8 4.3 %collective-permute-done.7.above = f32[128,128]{1,0:T(8,128)S(1)} collective-permute-done((f32[128,128]{1,0:T(8,128)S(1)}, f32[128,128]{1,0:T(8,128)S(1)}, u32[]{:S(2)}, u32[]{:S(2)}) %collective-permute-start.7) | collective-permute-done | bytes 65568 | tf_op jit(solution)/shard_map/ppermute | solution.py:524
  67.3 20.7 %all_to_all.10 = f32[8,288,128]{2,1,0:T(8,128)S(1)} all-to-all(f32[8,288,128]{2,1,0:T(8,128)S(1)} %broadcast_in_dim.6), channel_id=1, replica_groups=mesh['y'=4,'zhi'=4,'x'=4,'core'=2,'row'=8] {'x','core'}, dimensions={0} | all-to-all | bytes 2359296 | tf_op jit(solution)/shard_map/all_to_all | solution.py:577
  88.0 2.1 %shard_map.54 = (f32[93,16,128]{2,1,0:T(8,128)S(1)}, f32[6,16,128]{2,1,0:T(8,128)S(1)}, f32[6,16,128]{2,1,0:T(8,128)S(1)}, f32[6,16,128]{2,1,0:T(8,128)S(1)}, f3...) custom-call(f32[2304,128]{1,0:T(8,128)S(1)} %bitcast.9, f32[16,128,128]{2,1,0:T(8,128)} %copy-done.2), custom_call_target="tpu_custom_call" | custom-call | tf_op jit(solution)/shard_map/pallas_call | solution.py:510
  90.2 3.4 %collective-permute-start.10 = (f32[6,16,128]{2,1,0:T(8,128)S(1)}, f32[6,16,128]{2,1,0:T(8,128)S(1)}, u32[]{:S(2)}, u32[]{:S(2)}) collective-permute-start(f32[6,16,128]{2,1,0:T(8,128)S(1)} %get-tuple-element.46.v2), channel_id=1, source_target_pairs={{0,1},{1,2},{2,3},{3,4},{4,5},{5,6},{6,7},{8,9},{9,10},{10,11},{11... | collective-permute-start | bytes 147464 | tf_op jit(solution)/shard_map/ppermute | solution.py:524
  93.5 1.3 collective-permute-start.9
  95.3 4.3 %collective-permute-done.9.above = f32[6,16,128]{2,1,0:T(8,128)S(1)} collective-permute-done((f32[6,16,128]{2,1,0:T(8,128)S(1)}, f32[6,16,128]{2,1,0:T(8,128)S(1)}, u32[]{:S(2)}, u32[]{:S(2)}) %collective-permute-start.9) | collective-permute-done | bytes 49184 | tf_op jit(solution)/shard_map/ppermute | solution.py:524
  100.0 34.6 %all_to_all.11 = f32[128,1,128]{2,1,0:T(1,128)S(1)} all-to-all(f32[128,1,128]{2,1,0:T(1,128)S(1)} %broadcast_in_dim.16), channel_id=1, replica_groups={{900,644,388,132,901,645,389,133,902,646,390,134,903,647,391,135,960,70..., dimensions={0} | all-to-all | bytes 131072 | tf_op jit(solution)/shard_map/all_to_all | solution.py:599
  134.6 1.3 shard_map.56
  (17 shorter events, 1.1 us)
Async XLA Ops:
  0.6 39.1 %copy-start = (f32[4,2,2,32,2,128]{5,4,3,2,1,0:T(2,128)S(1)}, f32[4,2,2,32,2,128]{5,4,3,2,1,0:T(2,128)}, u32[]{:S(2)}) copy-start(f32[4,2,2,32,2,128]{5,4,3,2,1,0:T(2,128)} %param.4) | copy-start | bytes 1572868
  0.6 39.1 %copy-start.1 = (f32[4,2,2,32,2,128]{5,4,3,2,1,0:T(2,128)S(1)}, f32[4,2,2,32,2,128]{5,4,3,2,1,0:T(2,128)}, u32[]{:S(2)}) copy-start(f32[4,2,2,32,2,128]{5,4,3,2,1,0:T(2,128)} %param.3) | copy-start | bytes 1572868
  1.7 25.5 %collective-permute-start = (f32[192,128]{1,0:T(8,128)S(1)}, f32[192,128]{1,0:T(8,128)S(1)}, u32[]{:S(2)}, u32[]{:S(2)}) collective-permute-start(f32[192,128]{1,0:T(8,128)S(1)} %get-tuple-element.37), channel_id=1, source_target_pairs={{64,112},{128,176},{192,240},{256,304},{320,368},{384,432},{448,49... | collective-permute-start | bytes 294920 | tf_op jit(solution)/shard_map/ppermute | solution.py:557
  6.4 30.5 %collective-permute-start.1 = (f32[192,128]{1,0:T(8,128)S(1)}, f32[192,128]{1,0:T(8,128)S(1)}, u32[]{:S(2)}, u32[]{:S(2)}) collective-permute-start(f32[192,128]{1,0:T(8,128)S(1)} %get-tuple-element.36), channel_id=1, source_target_pairs={{8,0},{16,8},{24,16},{32,24},{40,32},{48,40},{56,48},{64,56},{72,6... | collective-permute-start | bytes 294920 | tf_op jit(solution)/shard_map/ppermute | solution.py:524
  27.2 12.5 %collective-permute-start.3 = (f32[192,128]{1,0:T(8,128)S(1)}, f32[192,128]{1,0:T(8,128)S(1)}, u32[]{:S(2)}, u32[]{:S(2)}) collective-permute-start(f32[192,128]{1,0:T(8,128)S(1)} %collective-permute-done), channel_id=1, source_target_pairs={{112,56},{176,120},{240,184},{304,248},{368,312},{432,376},{496,44... | collective-permute-start | bytes 294920 | tf_op jit(solution)/shard_map/ppermute | solution.py:559
  28.8 11.0 %collective-permute-start.2 = (f32[192,128]{1,0:T(8,128)S(1)}, f32[192,128]{1,0:T(8,128)S(1)}, u32[]{:S(2)}, u32[]{:S(2)}) collective-permute-start(f32[192,128]{1,0:T(8,128)S(1)} %get-tuple-element.37), channel_id=1, source_target_pairs={{8,0},{16,8},{24,16},{32,24},{40,32},{48,40},{56,48},{72,64},{80,7... | collective-permute-start | bytes 294920 | tf_op jit(solution)/shard_map/ppermute | solution.py:564
  30.1 9.7 %collective-permute-start.5 = (f32[136,128]{1,0:T(8,128)S(1)}, f32[136,128]{1,0:T(8,128)S(1)}, u32[]{:S(2)}, u32[]{:S(2)}) collective-permute-start(f32[136,128]{1,0:T(8,128)S(1)} %get-tuple-element.40), channel_id=1, source_target_pairs={{0,1},{1,2},{2,3},{3,4},{4,5},{5,6},{6,7},{8,9},{9,10},{10,11},{11... | collective-permute-start | bytes 208904 | tf_op jit(solution)/shard_map/ppermute | solution.py:524
  33.0 6.7 %collective-permute-start.4 = (f32[128,128]{1,0:T(8,128)S(1)}, f32[128,128]{1,0:T(8,128)S(1)}, u32[]{:S(2)}, u32[]{:S(2)}) collective-permute-start(f32[128,128]{1,0:T(8,128)S(1)} %get-tuple-element.39), channel_id=1, source_target_pairs={{1,0},{2,1},{3,2},{4,3},{5,4},{6,5},{7,6},{9,8},{10,9},{11,10},{12... | collective-permute-start | bytes 196616 | tf_op jit(solution)/shard_map/ppermute | solution.py:524
  40.6 47.4 %copy-start.2 = (f32[16,128,128]{2,1,0:T(8,128)}, f32[16,128,128]{2,1,0:T(8,128)S(1)}, u32[]{:S(2)}) copy-start(f32[16,128,128]{2,1,0:T(8,128)S(1)} %get-tuple-element.42.kept_hbm) | copy-start | bytes 3145732
  40.6 19.0 %collective-permute-start.6 = (f32[64,128]{1,0:T(8,128)S(1)}, f32[64,128]{1,0:T(8,128)S(1)}, u32[]{:S(2)}, u32[]{:S(2)}) collective-permute-start(f32[64,128]{1,0:T(8,128)S(1)} %get-tuple-element.41), channel_id=1, source_target_pairs={{64,0},{72,8},{80,16},{88,24},{128,64},{136,72},{144,80},{152,88},... | collective-permute-start | bytes 98312 | tf_op jit(solution)/shard_map/ppermute | solution.py:574
  59.7 3.2 %collective-permute-start.8 = (f32[128,128]{1,0:T(8,128)S(1)}, f32[128,128]{1,0:T(8,128)S(1)}, u32[]{:S(2)}, u32[]{:S(2)}) collective-permute-start(f32[128,128]{1,0:T(8,128)S(1)} %constant_dynamic-update-slice_fusion.both), channel_id=1, source_target_pairs={{0,1},{1,2},{2,3},{3,4},{4,5},{5,6},{6,7},{8,9},{9,10},{10,11},{11... | collective-permute-start | bytes 196616 | tf_op jit(solution)/shard_map/ppermute | solution.py:524
  60.9 6.2 %collective-permute-start.7 = (f32[128,128]{1,0:T(8,128)S(1)}, f32[128,128]{1,0:T(8,128)S(1)}, u32[]{:S(2)}, u32[]{:S(2)}) collective-permute-start(f32[128,128]{1,0:T(8,128)S(1)} %constant_dynamic-update-slice_fusion.both), channel_id=1, source_target_pairs={{1,0},{2,1},{3,2},{4,3},{5,4},{6,5},{7,6},{9,8},{10,9},{11,10},{12... | collective-permute-start | bytes 196616 | tf_op jit(solution)/shard_map/ppermute | solution.py:524
  90.2 5.1 %collective-permute-start.10 = (f32[6,16,128]{2,1,0:T(8,128)S(1)}, f32[6,16,128]{2,1,0:T(8,128)S(1)}, u32[]{:S(2)}, u32[]{:S(2)}) collective-permute-start(f32[6,16,128]{2,1,0:T(8,128)S(1)} %get-tuple-element.46.v2), channel_id=1, source_target_pairs={{0,1},{1,2},{2,3},{3,4},{4,5},{5,6},{6,7},{8,9},{9,10},{10,11},{11... | collective-permute-start | bytes 147464 | tf_op jit(solution)/shard_map/ppermute | solution.py:524
  93.5 6.0 %collective-permute-start.9 = (f32[6,16,128]{2,1,0:T(8,128)S(1)}, f32[6,16,128]{2,1,0:T(8,128)S(1)}, u32[]{:S(2)}, u32[]{:S(2)}) collective-permute-start(f32[6,16,128]{2,1,0:T(8,128)S(1)} %get-tuple-element.46.v2), channel_id=1, source_target_pairs={{1,0},{2,1},{3,2},{4,3},{5,4},{6,5},{7,6},{9,8},{10,9},{11,10},{12... | collective-permute-start | bytes 147464 | tf_op jit(solution)/shard_map/ppermute | solution.py:524

commit v8 on v7

--- a/solution.py
+++ b/solution.py
@@ -314,9 +314,7 @@
         return outs
 
 
-def window_kernel(got, kept_hbm, blocks, v0, e0, v1, e1, v2, kept, sems):
-    fetch = pltpu.make_async_copy(kept_hbm, kept, sems.at[0])
-    fetch.start()
+def window_kernel(got, blocks, v0, e0, v1, e1, v2):
     n_dev = got.shape[0] // (2 * DOUBLE)
     row_zero, sec_zero = lane_bits((2 * n_dev, 128))
     zero = jnp.zeros((2 * n_dev, 128), jnp.float32)
@@ -368,10 +366,14 @@
         v1[i] = w[i]
         e1[i] = f[i]
         v2[i] = last[i]
-    fetch.wait()
-
-
-def moments_kernel(blocks, v0, v1, v2, above, below, e2, v3, e3, out):
+
+
+def moments_kernel(blocks, v0, v1, v2, above, below, kept_hbm, e2, v3, e3, out, kept, sems):
+    fetches = [
+        pltpu.make_async_copy(kept_hbm.at[pl.ds(2 * i, 2)], kept.at[pl.ds(2 * i, 2)], sems.at[i]) for i in range(8)
+    ]
+    for fetch in fetches:
+        fetch.start()
     shape = v2.shape[1:]
     n_dev = shape[0] // 2
     bits = lane_bits(shape)
@@ -408,6 +410,8 @@
         value = jnp.sum(jnp.sum(value, axis=0, keepdims=True), axis=1, keepdims=True)
         packed = jnp.where(lane == n, value, packed)
     out[...] = packed
+    for fetch in fetches:
+        fetch.wait()
 
 
 def coefficients(moments):
@@ -576,23 +580,21 @@
     (mine,) = run(merge_kernel, [(2 * DOUBLE, 128)], both, shifted(both, "row", -1), shifted(both, "row", 1))
     got = lax.all_to_all(jnp.broadcast_to(mine[None], (n_dev, 2 * DOUBLE, 128)), GROUP, 0, 0, tiled=False)
     wide = (6, 2 * n_dev, 128)
-    blocks, v0, e0, v1, e1, v2, kept = run(
-        window_kernel,
-        [(93, 2 * n_dev, 128)] + [wide] * 5 + [(16, 128, 128)],
-        got.reshape(n_dev * 2 * DOUBLE, 128),
-        kept,
-        anywhere=(1,),
-        copies=1,
+    blocks, v0, e0, v1, e1, v2 = run(
+        window_kernel, [(93, 2 * n_dev, 128)] + [wide] * 5, got.reshape(n_dev * 2 * DOUBLE, 128)
     )
-    e2, v3, e3, part = run(
+    e2, v3, e3, part, kept = run(
         moments_kernel,
-        [wide, wide, wide, (1, 128)],
+        [wide, wide, wide, (1, 128), (16, 128, 128)],
         blocks,
         v0,
         v1,
         v2,
         shifted(v2, "row", -1),
         shifted(v2, "row", 1),
+        kept,
+        anywhere=(6,),
+        copies=8,
     )
     n_other = lax.axis_size(OTHERS)
     groups = sum_groups([lax.axis_size(axis) for axis in EVERY])

time: 137 us -> 137 us (level)
  no operation moved by 1% of the time
where the time goes in v8:
time: 137 us; the launch traced here: 136 us
  blocking collectives  55.4 us (40%)
  starting transfers between devices  47.8 us (35%)
  waiting for transfers between devices  25.1 us (18%)
  Pallas kernels  6.92 us (5%)
    all_to_all x1, blocking collectives, per_device(): lax.all_to_all(jnp.broadcast_to(part[None], (n_other, 1, 128)), EVERY, 0,...  34.6 us
    ppermute x7, starting transfers between devices, shifted(): return lax.ppermute(value, axes, pairs)  32.3 us
    all_to_all x1, blocking collectives, per_device(): lax.all_to_all(jnp.broadcast_to(mine[None], (n_dev, 2 * DOUBLE, 128)), GR...  20.7 us
    ppermute x7, waiting for transfers between devices, shifted(): return lax.ppermute(value, axes, pairs)  15 us
    ppermute x1, waiting for transfers between devices, per_device(): other = lax.ppermute(packet, SEC_AXES, pairs)  10.1 us
    ppermute x1, starting transfers between devices, per_device(): other = lax.ppermute(packet, SEC_AXES, pairs)  8.89 us
    pallas_call x7, Pallas kernels, call(): pl.pallas_call(kernel, out_shape=shapes, in_specs=spaces, out_specs=[pl.B...  6.92 us
    ppermute x1, starting transfers between devices, per_device(): relayed = lax.ppermute(rest, SEC_AXES, to_relay)  4.67 us
  transfers between devices with their start and end apart: 11, of which 7 were waited for; matrix products, arithmetic and copies ran while one was open for 0% of the time, Pallas kernels for 1%

profile of v8, /device:TPU:24, one launch (start us, length us, event | category | flops | bytes accessed | tf_op | source)
XLA Modules:
  0.0 136.1 jit_solution(9921593228374270699)
XLA Ops:
  0.7 1.1 shard_map.50
  1.7 4.7 %collective-permute-start = (f32[192,128]{1,0:T(8,128)S(1)}, f32[192,128]{1,0:T(8,128)S(1)}, u32[]{:S(2)}, u32[]{:S(2)}) collective-permute-start(f32[192,128]{1,0:T(8,128)S(1)} %get-tuple-element.37), channel_id=1, source_target_pairs={{64,112},{128,176},{192,240},{256,304},{320,368},{384,432},{448,49... | collective-permute-start | bytes 294920 | tf_op jit(solution)/shard_map/ppermute | solution.py:561
  6.4 20.8 %collective-permute-start.1 = (f32[192,128]{1,0:T(8,128)S(1)}, f32[192,128]{1,0:T(8,128)S(1)}, u32[]{:S(2)}, u32[]{:S(2)}) collective-permute-start(f32[192,128]{1,0:T(8,128)S(1)} %get-tuple-element.36), channel_id=1, source_target_pairs={{8,0},{16,8},{24,16},{32,24},{40,32},{48,40},{56,48},{64,56},{72,6... | collective-permute-start | bytes 294920 | tf_op jit(solution)/shard_map/ppermute | solution.py:528
  27.2 0.7 collective-permute-start.3
  27.9 0.9 shard_map.51
  28.8 1.3 collective-permute-start.2
  30.1 2.9 %collective-permute-start.5 = (f32[136,128]{1,0:T(8,128)S(1)}, f32[136,128]{1,0:T(8,128)S(1)}, u32[]{:S(2)}, u32[]{:S(2)}) collective-permute-start(f32[136,128]{1,0:T(8,128)S(1)} %get-tuple-element.40), channel_id=1, source_target_pairs={{0,1},{1,2},{2,3},{3,4},{4,5},{5,6},{6,7},{8,9},{9,10},{10,11},{11... | collective-permute-start | bytes 208904 | tf_op jit(solution)/shard_map/ppermute | solution.py:528
  33.0 1.3 collective-permute-start.4
  34.3 2.6 %collective-permute-done.1.up_ref = f32[192,128]{1,0:T(8,128)S(1)} collective-permute-done((f32[192,128]{1,0:T(8,128)S(1)}, f32[192,128]{1,0:T(8,128)S(1)}, u32[]{:S(2)}, u32[]{:S(2)}) %collective-permute-start.1) | collective-permute-done | bytes 98336 | tf_op jit(solution)/shard_map/ppermute | solution.py:528
  36.9 2.8 %collective-permute-done.4.next_ref = f32[128,128]{1,0:T(8,128)S(1)} collective-permute-done((f32[128,128]{1,0:T(8,128)S(1)}, f32[128,128]{1,0:T(8,128)S(1)}, u32[]{:S(2)}, u32[]{:S(2)}) %collective-permute-start.4) | collective-permute-done | bytes 65568 | tf_op jit(solution)/shard_map/ppermute | solution.py:528
  39.8 0.8 shard_map.52
  40.6 8.9 %collective-permute-start.6 = (f32[64,128]{1,0:T(8,128)S(1)}, f32[64,128]{1,0:T(8,128)S(1)}, u32[]{:S(2)}, u32[]{:S(2)}) collective-permute-start(f32[64,128]{1,0:T(8,128)S(1)} %get-tuple-element.41), channel_id=1, source_target_pairs={{64,0},{72,8},{80,16},{88,24},{128,64},{136,72},{144,80},{152,88},... | collective-permute-start | bytes 98312 | tf_op jit(solution)/shard_map/ppermute | solution.py:578
  49.5 10.1 %collective-permute-done.6 = f32[64,128]{1,0:T(8,128)S(1)} collective-permute-done((f32[64,128]{1,0:T(8,128)S(1)}, f32[64,128]{1,0:T(8,128)S(1)}, u32[]{:S(2)}, u32[]{:S(2)}) %collective-permute-start.6) | collective-permute-done | bytes 32800 | tf_op jit(solution)/shard_map/ppermute | solution.py:578
  59.7 1.3 collective-permute-start.8
  61.0 1.3 collective-permute-start.7
  62.8 4.3 %collective-permute-done.7.above = f32[128,128]{1,0:T(8,128)S(1)} collective-permute-done((f32[128,128]{1,0:T(8,128)S(1)}, f32[128,128]{1,0:T(8,128)S(1)}, u32[]{:S(2)}, u32[]{:S(2)}) %collective-permute-start.7) | collective-permute-done | bytes 65568 | tf_op jit(solution)/shard_map/ppermute | solution.py:528
  67.3 20.7 %all_to_all.10 = f32[8,288,128]{2,1,0:T(8,128)S(1)} all-to-all(f32[8,288,128]{2,1,0:T(8,128)S(1)} %broadcast_in_dim.6), channel_id=1, replica_groups=mesh['y'=4,'zhi'=4,'x'=4,'core'=2,'row'=8] {'x','core'}, dimensions={0} | all-to-all | bytes 2359296 | tf_op jit(solution)/shard_map/all_to_all | solution.py:581
  88.0 1.0 shard_map.54
  89.0 3.4 %collective-permute-start.10 = (f32[6,16,128]{2,1,0:T(8,128)S(1)}, f32[6,16,128]{2,1,0:T(8,128)S(1)}, u32[]{:S(2)}, u32[]{:S(2)}) collective-permute-start(f32[6,16,128]{2,1,0:T(8,128)S(1)} %get-tuple-element.45.v2), channel_id=1, source_target_pairs={{0,1},{1,2},{2,3},{3,4},{4,5},{5,6},{6,7},{8,9},{9,10},{10,11},{11... | collective-permute-start | bytes 147464 | tf_op jit(solution)/shard_map/ppermute | solution.py:528
  92.4 1.3 collective-permute-start.9
  94.2 4.3 %collective-permute-done.9.above = f32[6,16,128]{2,1,0:T(8,128)S(1)} collective-permute-done((f32[6,16,128]{2,1,0:T(8,128)S(1)}, f32[6,16,128]{2,1,0:T(8,128)S(1)}, u32[]{:S(2)}, u32[]{:S(2)}) %collective-permute-start.9) | collective-permute-done | bytes 49184 | tf_op jit(solution)/shard_map/ppermute | solution.py:528
  98.4 1.7 %shard_map.55 = (f32[6,16,128]{2,1,0:T(8,128)S(1)}, f32[6,16,128]{2,1,0:T(8,128)S(1)}, f32[6,16,128]{2,1,0:T(8,128)S(1)}, f32[1,128]{1,0:T(1,128)S(1)}, f32[16,128,128]{2,1,0:T(8,128)S(1)}) custom-call(f32[93,16,128]{2,1,0:T(8,128)S(1)} %get-tuple-element.42.blocks, f32[6,16,128]{2,1,0:T(8,128)S(1)} %get-tuple-element.43.v0, ...), custom_call_target="tpu_custom_call" | custom-call | tf_op jit(solution)/shard_map/pallas_call | solution.py:514
  100.2 34.6 %all_to_all.11 = f32[128,1,128]{2,1,0:T(1,128)S(1)} all-to-all(f32[128,1,128]{2,1,0:T(1,128)S(1)} %broadcast_in_dim.16), channel_id=1, replica_groups={{900,644,388,132,901,645,389,133,902,646,390,134,903,647,391,135,960,70..., dimensions={0} | all-to-all | bytes 131072 | tf_op jit(solution)/shard_map/all_to_all | solution.py:601
  134.8 1.3 shard_map.56
  (17 shorter events, 1.2 us)
Async XLA Ops:
  0.6 39.1 %copy-start = (f32[4,2,2,32,2,128]{5,4,3,2,1,0:T(2,128)S(1)}, f32[4,2,2,32,2,128]{5,4,3,2,1,0:T(2,128)}, u32[]{:S(2)}) copy-start(f32[4,2,2,32,2,128]{5,4,3,2,1,0:T(2,128)} %param.4) | copy-start | bytes 1572868
  0.6 39.1 %copy-start.1 = (f32[4,2,2,32,2,128]{5,4,3,2,1,0:T(2,128)S(1)}, f32[4,2,2,32,2,128]{5,4,3,2,1,0:T(2,128)}, u32[]{:S(2)}) copy-start(f32[4,2,2,32,2,128]{5,4,3,2,1,0:T(2,128)} %param.3) | copy-start | bytes 1572868
  1.7 25.5 %collective-permute-start = (f32[192,128]{1,0:T(8,128)S(1)}, f32[192,128]{1,0:T(8,128)S(1)}, u32[]{:S(2)}, u32[]{:S(2)}) collective-permute-start(f32[192,128]{1,0:T(8,128)S(1)} %get-tuple-element.37), channel_id=1, source_target_pairs={{64,112},{128,176},{192,240},{256,304},{320,368},{384,432},{448,49... | collective-permute-start | bytes 294920 | tf_op jit(solution)/shard_map/ppermute | solution.py:561
  6.4 30.5 %collective-permute-start.1 = (f32[192,128]{1,0:T(8,128)S(1)}, f32[192,128]{1,0:T(8,128)S(1)}, u32[]{:S(2)}, u32[]{:S(2)}) collective-permute-start(f32[192,128]{1,0:T(8,128)S(1)} %get-tuple-element.36), channel_id=1, source_target_pairs={{8,0},{16,8},{24,16},{32,24},{40,32},{48,40},{56,48},{64,56},{72,6... | collective-permute-start | bytes 294920 | tf_op jit(solution)/shard_map/ppermute | solution.py:528
  27.2 12.5 %collective-permute-start.3 = (f32[192,128]{1,0:T(8,128)S(1)}, f32[192,128]{1,0:T(8,128)S(1)}, u32[]{:S(2)}, u32[]{:S(2)}) collective-permute-start(f32[192,128]{1,0:T(8,128)S(1)} %collective-permute-done), channel_id=1, source_target_pairs={{112,56},{176,120},{240,184},{304,248},{368,312},{432,376},{496,44... | collective-permute-start | bytes 294920 | tf_op jit(solution)/shard_map/ppermute | solution.py:563
  28.8 11.0 %collective-permute-start.2 = (f32[192,128]{1,0:T(8,128)S(1)}, f32[192,128]{1,0:T(8,128)S(1)}, u32[]{:S(2)}, u32[]{:S(2)}) collective-permute-start(f32[192,128]{1,0:T(8,128)S(1)} %get-tuple-element.37), channel_id=1, source_target_pairs={{8,0},{16,8},{24,16},{32,24},{40,32},{48,40},{56,48},{72,64},{80,7... | collective-permute-start | bytes 294920 | tf_op jit(solution)/shard_map/ppermute | solution.py:568
  30.1 9.7 %collective-permute-start.5 = (f32[136,128]{1,0:T(8,128)S(1)}, f32[136,128]{1,0:T(8,128)S(1)}, u32[]{:S(2)}, u32[]{:S(2)}) collective-permute-start(f32[136,128]{1,0:T(8,128)S(1)} %get-tuple-element.40), channel_id=1, source_target_pairs={{0,1},{1,2},{2,3},{3,4},{4,5},{5,6},{6,7},{8,9},{9,10},{10,11},{11... | collective-permute-start | bytes 208904 | tf_op jit(solution)/shard_map/ppermute | solution.py:528
  33.0 6.7 %collective-permute-start.4 = (f32[128,128]{1,0:T(8,128)S(1)}, f32[128,128]{1,0:T(8,128)S(1)}, u32[]{:S(2)}, u32[]{:S(2)}) collective-permute-start(f32[128,128]{1,0:T(8,128)S(1)} %get-tuple-element.39), channel_id=1, source_target_pairs={{1,0},{2,1},{3,2},{4,3},{5,4},{6,5},{7,6},{9,8},{10,9},{11,10},{12... | collective-permute-start | bytes 196616 | tf_op jit(solution)/shard_map/ppermute | solution.py:528
  40.6 47.4 %copy-start.2 = (f32[16,128,128]{2,1,0:T(8,128)}, f32[16,128,128]{2,1,0:T(8,128)S(1)}, u32[]{:S(2)}) copy-start(f32[16,128,128]{2,1,0:T(8,128)S(1)} %get-tuple-element.46.kept_hbm) | copy-start | bytes 3145732
  40.6 19.0 %collective-permute-start.6 = (f32[64,128]{1,0:T(8,128)S(1)}, f32[64,128]{1,0:T(8,128)S(1)}, u32[]{:S(2)}, u32[]{:S(2)}) collective-permute-start(f32[64,128]{1,0:T(8,128)S(1)} %get-tuple-element.41), channel_id=1, source_target_pairs={{64,0},{72,8},{80,16},{88,24},{128,64},{136,72},{144,80},{152,88},... | collective-permute-start | bytes 98312 | tf_op jit(solution)/shard_map/ppermute | solution.py:578
  59.7 3.2 %collective-permute-start.8 = (f32[128,128]{1,0:T(8,128)S(1)}, f32[128,128]{1,0:T(8,128)S(1)}, u32[]{:S(2)}, u32[]{:S(2)}) collective-permute-start(f32[128,128]{1,0:T(8,128)S(1)} %constant_dynamic-update-slice_fusion.both), channel_id=1, source_target_pairs={{0,1},{1,2},{2,3},{3,4},{4,5},{5,6},{6,7},{8,9},{9,10},{10,11},{11... | collective-permute-start | bytes 196616 | tf_op jit(solution)/shard_map/ppermute | solution.py:528
  61.0 6.2 %collective-permute-start.7 = (f32[128,128]{1,0:T(8,128)S(1)}, f32[128,128]{1,0:T(8,128)S(1)}, u32[]{:S(2)}, u32[]{:S(2)}) collective-permute-start(f32[128,128]{1,0:T(8,128)S(1)} %constant_dynamic-update-slice_fusion.both), channel_id=1, source_target_pairs={{1,0},{2,1},{3,2},{4,3},{5,4},{6,5},{7,6},{9,8},{10,9},{11,10},{12... | collective-permute-start | bytes 196616 | tf_op jit(solution)/shard_map/ppermute | solution.py:528
  89.0 5.1 %collective-permute-start.10 = (f32[6,16,128]{2,1,0:T(8,128)S(1)}, f32[6,16,128]{2,1,0:T(8,128)S(1)}, u32[]{:S(2)}, u32[]{:S(2)}) collective-permute-start(f32[6,16,128]{2,1,0:T(8,128)S(1)} %get-tuple-element.45.v2), channel_id=1, source_target_pairs={{0,1},{1,2},{2,3},{3,4},{4,5},{5,6},{6,7},{8,9},{9,10},{10,11},{11... | collective-permute-start | bytes 147464 | tf_op jit(solution)/shard_map/ppermute | solution.py:528
  92.4 6.0 %collective-permute-start.9 = (f32[6,16,128]{2,1,0:T(8,128)S(1)}, f32[6,16,128]{2,1,0:T(8,128)S(1)}, u32[]{:S(2)}, u32[]{:S(2)}) collective-permute-start(f32[6,16,128]{2,1,0:T(8,128)S(1)} %get-tuple-element.45.v2), channel_id=1, source_target_pairs={{1,0},{2,1},{3,2},{4,3},{5,4},{6,5},{7,6},{9,8},{10,9},{11,10},{12... | collective-permute-start | bytes 147464 | tf_op jit(solution)/shard_map/ppermute | solution.py:528

commit v9 on v8

--- a/solution.py
+++ b/solution.py
@@ -369,9 +369,7 @@
 
 
 def moments_kernel(blocks, v0, v1, v2, above, below, kept_hbm, e2, v3, e3, out, kept, sems):
-    fetches = [
-        pltpu.make_async_copy(kept_hbm.at[pl.ds(2 * i, 2)], kept.at[pl.ds(2 * i, 2)], sems.at[i]) for i in range(8)
-    ]
+    fetches = [pltpu.make_async_copy(kept_hbm, kept, sems.at[0])]
     for fetch in fetches:
         fetch.start()
     shape = v2.shape[1:]
@@ -594,7 +592,7 @@
         shifted(v2, "row", 1),
         kept,
         anywhere=(6,),
-        copies=8,
+        copies=1,
     )
     n_other = lax.axis_size(OTHERS)
     groups = sum_groups([lax.axis_size(axis) for axis in EVERY])

time: 137 us -> 136 us (level)
  no operation moved by 1% of the time
where the time goes in v9:
time: 136 us
  blocking collectives  55.4 us (41%)
  starting transfers between devices  47.8 us (35%)
  waiting for transfers between devices  25.1 us (18%)
  Pallas kernels  6.45 us (5%)
    all_to_all x1, blocking collectives, per_device(): lax.all_to_all(jnp.broadcast_to(part[None], (n_other, 1, 128)), EVERY, 0,...  34.6 us
    ppermute x7, starting transfers between devices, shifted(): return lax.ppermute(value, axes, pairs)  32.3 us
    all_to_all x1, blocking collectives, per_device(): lax.all_to_all(jnp.broadcast_to(mine[None], (n_dev, 2 * DOUBLE, 128)), GR...  20.7 us
    ppermute x7, waiting for transfers between devices, shifted(): return lax.ppermute(value, axes, pairs)  15 us
    ppermute x1, waiting for transfers between devices, per_device(): other = lax.ppermute(packet, SEC_AXES, pairs)  10.1 us
    ppermute x1, starting transfers between devices, per_device(): other = lax.ppermute(packet, SEC_AXES, pairs)  8.89 us
    pallas_call x7, Pallas kernels, call(): pl.pallas_call(kernel, out_shape=shapes, in_specs=spaces, out_specs=[pl.B...  6.45 us
    ppermute x1, starting transfers between devices, per_device(): relayed = lax.ppermute(rest, SEC_AXES, to_relay)  4.67 us
  transfers between devices with their start and end apart: 11, of which 7 were waited for; matrix products, arithmetic and copies ran while one was open for 0% of the time, Pallas kernels for 1%

profile of v9, /device:TPU:24, one launch (start us, length us, event | category | flops | bytes accessed | tf_op | source)
XLA Modules:
  0.0 135.7 jit_solution(15839807568741040086)
XLA Ops:
  0.7 1.1 shard_map.50
  1.7 4.7 %collective-permute-start = (f32[192,128]{1,0:T(8,128)S(1)}, f32[192,128]{1,0:T(8,128)S(1)}, u32[]{:S(2)}, u32[]{:S(2)}) collective-permute-start(f32[192,128]{1,0:T(8,128)S(1)} %get-tuple-element.37), channel_id=1, source_target_pairs={{64,112},{128,176},{192,240},{256,304},{320,368},{384,432},{448,49... | collective-permute-start | bytes 294920 | tf_op jit(solution)/shard_map/ppermute | solution.py:559
  6.4 20.8 %collective-permute-start.1 = (f32[192,128]{1,0:T(8,128)S(1)}, f32[192,128]{1,0:T(8,128)S(1)}, u32[]{:S(2)}, u32[]{:S(2)}) collective-permute-start(f32[192,128]{1,0:T(8,128)S(1)} %get-tuple-element.36), channel_id=1, source_target_pairs={{8,0},{16,8},{24,16},{32,24},{40,32},{48,40},{56,48},{64,56},{72,6... | collective-permute-start | bytes 294920 | tf_op jit(solution)/shard_map/ppermute | solution.py:526
  27.2 0.7 collective-permute-start.3
  27.9 0.9 shard_map.51
  28.8 1.3 collective-permute-start.2
  30.1 2.9 %collective-permute-start.5 = (f32[136,128]{1,0:T(8,128)S(1)}, f32[136,128]{1,0:T(8,128)S(1)}, u32[]{:S(2)}, u32[]{:S(2)}) collective-permute-start(f32[136,128]{1,0:T(8,128)S(1)} %get-tuple-element.40), channel_id=1, source_target_pairs={{0,1},{1,2},{2,3},{3,4},{4,5},{5,6},{6,7},{8,9},{9,10},{10,11},{11... | collective-permute-start | bytes 208904 | tf_op jit(solution)/shard_map/ppermute | solution.py:526
  33.0 1.3 collective-permute-start.4
  34.3 2.6 %collective-permute-done.1.up_ref = f32[192,128]{1,0:T(8,128)S(1)} collective-permute-done((f32[192,128]{1,0:T(8,128)S(1)}, f32[192,128]{1,0:T(8,128)S(1)}, u32[]{:S(2)}, u32[]{:S(2)}) %collective-permute-start.1) | collective-permute-done | bytes 98336 | tf_op jit(solution)/shard_map/ppermute | solution.py:526
  36.9 2.8 %collective-permute-done.4.next_ref = f32[128,128]{1,0:T(8,128)S(1)} collective-permute-done((f32[128,128]{1,0:T(8,128)S(1)}, f32[128,128]{1,0:T(8,128)S(1)}, u32[]{:S(2)}, u32[]{:S(2)}) %collective-permute-start.4) | collective-permute-done | bytes 65568 | tf_op jit(solution)/shard_map/ppermute | solution.py:526
  39.8 0.8 shard_map.52
  40.6 8.9 %collective-permute-start.6 = (f32[64,128]{1,0:T(8,128)S(1)}, f32[64,128]{1,0:T(8,128)S(1)}, u32[]{:S(2)}, u32[]{:S(2)}) collective-permute-start(f32[64,128]{1,0:T(8,128)S(1)} %get-tuple-element.41), channel_id=1, source_target_pairs={{64,0},{72,8},{80,16},{88,24},{128,64},{136,72},{144,80},{152,88},... | collective-permute-start | bytes 98312 | tf_op jit(solution)/shard_map/ppermute | solution.py:576
  49.5 10.1 %collective-permute-done.6 = f32[64,128]{1,0:T(8,128)S(1)} collective-permute-done((f32[64,128]{1,0:T(8,128)S(1)}, f32[64,128]{1,0:T(8,128)S(1)}, u32[]{:S(2)}, u32[]{:S(2)}) %collective-permute-start.6) | collective-permute-done | bytes 32800 | tf_op jit(solution)/shard_map/ppermute | solution.py:576
  59.7 1.3 collective-permute-start.8
  61.0 1.3 collective-permute-start.7
  62.8 4.3 %collective-permute-done.7.above = f32[128,128]{1,0:T(8,128)S(1)} collective-permute-done((f32[128,128]{1,0:T(8,128)S(1)}, f32[128,128]{1,0:T(8,128)S(1)}, u32[]{:S(2)}, u32[]{:S(2)}) %collective-permute-start.7) | collective-permute-done | bytes 65568 | tf_op jit(solution)/shard_map/ppermute | solution.py:526
  67.3 20.7 %all_to_all.10 = f32[8,288,128]{2,1,0:T(8,128)S(1)} all-to-all(f32[8,288,128]{2,1,0:T(8,128)S(1)} %broadcast_in_dim.6), channel_id=1, replica_groups=mesh['y'=4,'zhi'=4,'x'=4,'core'=2,'row'=8] {'x','core'}, dimensions={0} | all-to-all | bytes 2359296 | tf_op jit(solution)/shard_map/all_to_all | solution.py:579
  88.0 1.0 shard_map.54
  89.0 3.4 %collective-permute-start.10 = (f32[6,16,128]{2,1,0:T(8,128)S(1)}, f32[6,16,128]{2,1,0:T(8,128)S(1)}, u32[]{:S(2)}, u32[]{:S(2)}) collective-permute-start(f32[6,16,128]{2,1,0:T(8,128)S(1)} %get-tuple-element.45.v2), channel_id=1, source_target_pairs={{0,1},{1,2},{2,3},{3,4},{4,5},{5,6},{6,7},{8,9},{9,10},{10,11},{11... | collective-permute-start | bytes 147464 | tf_op jit(solution)/shard_map/ppermute | solution.py:526
  92.4 1.3 collective-permute-start.9
  94.2 4.3 %collective-permute-done.9.above = f32[6,16,128]{2,1,0:T(8,128)S(1)} collective-permute-done((f32[6,16,128]{2,1,0:T(8,128)S(1)}, f32[6,16,128]{2,1,0:T(8,128)S(1)}, u32[]{:S(2)}, u32[]{:S(2)}) %collective-permute-start.9) | collective-permute-done | bytes 49184 | tf_op jit(solution)/shard_map/ppermute | solution.py:526
  98.4 1.2 shard_map.55
  99.7 34.6 %all_to_all.11 = f32[128,1,128]{2,1,0:T(1,128)S(1)} all-to-all(f32[128,1,128]{2,1,0:T(1,128)S(1)} %broadcast_in_dim.16), channel_id=1, replica_groups={{900,644,388,132,901,645,389,133,902,646,390,134,903,647,391,135,960,70..., dimensions={0} | all-to-all | bytes 131072 | tf_op jit(solution)/shard_map/all_to_all | solution.py:599
  134.3 1.3 shard_map.56
  (17 shorter events, 1.2 us)
Async XLA Ops:
  0.6 39.1 %copy-start = (f32[4,2,2,32,2,128]{5,4,3,2,1,0:T(2,128)S(1)}, f32[4,2,2,32,2,128]{5,4,3,2,1,0:T(2,128)}, u32[]{:S(2)}) copy-start(f32[4,2,2,32,2,128]{5,4,3,2,1,0:T(2,128)} %param.4) | copy-start | bytes 1572868
  0.6 39.1 %copy-start.1 = (f32[4,2,2,32,2,128]{5,4,3,2,1,0:T(2,128)S(1)}, f32[4,2,2,32,2,128]{5,4,3,2,1,0:T(2,128)}, u32[]{:S(2)}) copy-start(f32[4,2,2,32,2,128]{5,4,3,2,1,0:T(2,128)} %param.3) | copy-start | bytes 1572868
  1.7 25.5 %collective-permute-start = (f32[192,128]{1,0:T(8,128)S(1)}, f32[192,128]{1,0:T(8,128)S(1)}, u32[]{:S(2)}, u32[]{:S(2)}) collective-permute-start(f32[192,128]{1,0:T(8,128)S(1)} %get-tuple-element.37), channel_id=1, source_target_pairs={{64,112},{128,176},{192,240},{256,304},{320,368},{384,432},{448,49... | collective-permute-start | bytes 294920 | tf_op jit(solution)/shard_map/ppermute | solution.py:559
  6.4 30.5 %collective-permute-start.1 = (f32[192,128]{1,0:T(8,128)S(1)}, f32[192,128]{1,0:T(8,128)S(1)}, u32[]{:S(2)}, u32[]{:S(2)}) collective-permute-start(f32[192,128]{1,0:T(8,128)S(1)} %get-tuple-element.36), channel_id=1, source_target_pairs={{8,0},{16,8},{24,16},{32,24},{40,32},{48,40},{56,48},{64,56},{72,6... | collective-permute-start | bytes 294920 | tf_op jit(solution)/shard_map/ppermute | solution.py:526
  27.2 12.5 %collective-permute-start.3 = (f32[192,128]{1,0:T(8,128)S(1)}, f32[192,128]{1,0:T(8,128)S(1)}, u32[]{:S(2)}, u32[]{:S(2)}) collective-permute-start(f32[192,128]{1,0:T(8,128)S(1)} %collective-permute-done), channel_id=1, source_target_pairs={{112,56},{176,120},{240,184},{304,248},{368,312},{432,376},{496,44... | collective-permute-start | bytes 294920 | tf_op jit(solution)/shard_map/ppermute | solution.py:561
  28.8 11.0 %collective-permute-start.2 = (f32[192,128]{1,0:T(8,128)S(1)}, f32[192,128]{1,0:T(8,128)S(1)}, u32[]{:S(2)}, u32[]{:S(2)}) collective-permute-start(f32[192,128]{1,0:T(8,128)S(1)} %get-tuple-element.37), channel_id=1, source_target_pairs={{8,0},{16,8},{24,16},{32,24},{40,32},{48,40},{56,48},{72,64},{80,7... | collective-permute-start | bytes 294920 | tf_op jit(solution)/shard_map/ppermute | solution.py:566
  30.1 9.7 %collective-permute-start.5 = (f32[136,128]{1,0:T(8,128)S(1)}, f32[136,128]{1,0:T(8,128)S(1)}, u32[]{:S(2)}, u32[]{:S(2)}) collective-permute-start(f32[136,128]{1,0:T(8,128)S(1)} %get-tuple-element.40), channel_id=1, source_target_pairs={{0,1},{1,2},{2,3},{3,4},{4,5},{5,6},{6,7},{8,9},{9,10},{10,11},{11... | collective-permute-start | bytes 208904 | tf_op jit(solution)/shard_map/ppermute | solution.py:526
  33.0 6.7 %collective-permute-start.4 = (f32[128,128]{1,0:T(8,128)S(1)}, f32[128,128]{1,0:T(8,128)S(1)}, u32[]{:S(2)}, u32[]{:S(2)}) collective-permute-start(f32[128,128]{1,0:T(8,128)S(1)} %get-tuple-element.39), channel_id=1, source_target_pairs={{1,0},{2,1},{3,2},{4,3},{5,4},{6,5},{7,6},{9,8},{10,9},{11,10},{12... | collective-permute-start | bytes 196616 | tf_op jit(solution)/shard_map/ppermute | solution.py:526
  40.6 47.4 %copy-start.2 = (f32[16,128,128]{2,1,0:T(8,128)}, f32[16,128,128]{2,1,0:T(8,128)S(1)}, u32[]{:S(2)}) copy-start(f32[16,128,128]{2,1,0:T(8,128)S(1)} %get-tuple-element.46.kept_hbm) | copy-start | bytes 3145732
  40.6 19.0 %collective-permute-start.6 = (f32[64,128]{1,0:T(8,128)S(1)}, f32[64,128]{1,0:T(8,128)S(1)}, u32[]{:S(2)}, u32[]{:S(2)}) collective-permute-start(f32[64,128]{1,0:T(8,128)S(1)} %get-tuple-element.41), channel_id=1, source_target_pairs={{64,0},{72,8},{80,16},{88,24},{128,64},{136,72},{144,80},{152,88},... | collective-permute-start | bytes 98312 | tf_op jit(solution)/shard_map/ppermute | solution.py:576
  59.7 3.2 %collective-permute-start.8 = (f32[128,128]{1,0:T(8,128)S(1)}, f32[128,128]{1,0:T(8,128)S(1)}, u32[]{:S(2)}, u32[]{:S(2)}) collective-permute-start(f32[128,128]{1,0:T(8,128)S(1)} %constant_dynamic-update-slice_fusion.both), channel_id=1, source_target_pairs={{0,1},{1,2},{2,3},{3,4},{4,5},{5,6},{6,7},{8,9},{9,10},{10,11},{11... | collective-permute-start | bytes 196616 | tf_op jit(solution)/shard_map/ppermute | solution.py:526
  61.0 6.2 %collective-permute-start.7 = (f32[128,128]{1,0:T(8,128)S(1)}, f32[128,128]{1,0:T(8,128)S(1)}, u32[]{:S(2)}, u32[]{:S(2)}) collective-permute-start(f32[128,128]{1,0:T(8,128)S(1)} %constant_dynamic-update-slice_fusion.both), channel_id=1, source_target_pairs={{1,0},{2,1},{3,2},{4,3},{5,4},{6,5},{7,6},{9,8},{10,9},{11,10},{12... | collective-permute-start | bytes 196616 | tf_op jit(solution)/shard_map/ppermute | solution.py:526
  89.0 5.1 %collective-permute-start.10 = (f32[6,16,128]{2,1,0:T(8,128)S(1)}, f32[6,16,128]{2,1,0:T(8,128)S(1)}, u32[]{:S(2)}, u32[]{:S(2)}) collective-permute-start(f32[6,16,128]{2,1,0:T(8,128)S(1)} %get-tuple-element.45.v2), channel_id=1, source_target_pairs={{0,1},{1,2},{2,3},{3,4},{4,5},{5,6},{6,7},{8,9},{9,10},{10,11},{11... | collective-permute-start | bytes 147464 | tf_op jit(solution)/shard_map/ppermute | solution.py:526
  92.4 6.0 %collective-permute-start.9 = (f32[6,16,128]{2,1,0:T(8,128)S(1)}, f32[6,16,128]{2,1,0:T(8,128)S(1)}, u32[]{:S(2)}, u32[]{:S(2)}) collective-permute-start(f32[6,16,128]{2,1,0:T(8,128)S(1)} %get-tuple-element.45.v2), channel_id=1, source_target_pairs={{1,0},{2,1},{3,2},{4,3},{5,4},{6,5},{7,6},{9,8},{10,9},{11,10},{12... | collective-permute-start | bytes 147464 | tf_op jit(solution)/shard_map/ppermute | solution.py:526
